TPU v7x, 32 devices: a whole 2x2x4 slice. The times are simulated.
32 devices in a mesh: shard: 8 (over z, y), tensor: 4 (over x, core).
Axes of the slice: x: 2, y: 2, z: 4, core: 2. Of those that a mesh axis runs over, the one named last changes fastest.
Arguments:
- grad_parts: float32 [4, 4, 768, 768], P('tensor', None, 'shard'), may hold values from -0.6 to 0.6
- adam_v: float32 [4, 768, 768], P(None, 'shard', 'tensor'), may hold values from 0.01 to 0.2
- left_stat: float32 [8, 768, 768], P('shard', 'tensor'), may hold values from -6 to 6
- right_stat: float32 [8, 768, 768], P('shard', 'tensor'), may hold values from -6 to 6
- left_root: bfloat16 [8, 768, 768], P('shard', 'tensor'), as said below
- right_root: bfloat16 [8, 768, 768], P('shard', 'tensor'), as said below
- owner: int32 [4], replicated, may hold values from 0 to 7, as said below
- vec_parts: float32 [4, 4, 768], P('tensor', None, 'shard'), may hold values from -0.6 to 0.6
- vec_m: float32 [4, 768], P(None, 'shard'), may hold values from -0.3 to 0.3
- vec_v: float32 [4, 768], P(None, 'shard'), may hold values from 0.01 to 0.2
Outputs:
- update: float32 [4, 768, 768], P(None, 'shard', 'tensor')
- new_adam_v: float32 [4, 768, 768], P(None, 'shard', 'tensor')
- new_left: float32 [8, 768, 768], P('shard', 'tensor')
- new_right: float32 [8, 768, 768], P('shard', 'tensor')
- new_vec_m: float32 [4, 768], P(None, 'shard')
- new_vec_v: float32 [4, 768], P(None, 'shard')
- vec_step: float32 [4, 768], P(None, 'shard')
Inputs may be any that keep to these rules, and one draw needn't show every extreme that they name: owner holds 4 distinct slot numbers: no slot owns two tiles. `left_root`: each slot's matrix is symmetric. `right_root`: each slot's matrix is symmetric.
All inputs are finite; a program needn't handle non-finite values.
Results may differ from a plain program's by a relative error of at most 0.0003.
Values may be sent and summed in bfloat16 or wider, within the bound.
No kernel may reach another device: no remote copies, remote signals or barrier semaphores. Data moves between devices by JAX's collectives and lax.ppermute only.
A program may use at most 64 MiB of HBM per device.

v0:
```python
import jax
import jax.numpy as jnp
from jax import lax
from jax.sharding import PartitionSpec as P

BETA_ONE = 0.9
BETA_TWO = 0.95
STAT_DECAY = 0.95
STEP_COUNT = 10.0
EPSILON = 1e-08
NORM_EPS = 1e-06
HIGH = lax.Precision.HIGHEST


def local(
    grad_parts, adam_v, left_stat, right_stat, left_root, right_root, owner, vec_parts, vec_m, vec_v
):
    shards = lax.axis_size("shard")
    tiles = owner.shape[0]
    grad = lax.psum_scatter(grad_parts[0], "tensor", scatter_dimension=2, tiled=True)
    rows_dev = grad.shape[1]
    cols_dev = grad.shape[2]
    new_adam_v = BETA_TWO * adam_v + (1.0 - BETA_TWO) * grad * grad
    bias_two = 1.0 - BETA_TWO**STEP_COUNT
    adam_dir = grad / (jnp.sqrt(new_adam_v / bias_two) + EPSILON)
    adam_sq = jnp.sum(adam_dir * adam_dir, axis=(1, 2))
    vec_grad = lax.psum(vec_parts[0], "tensor")
    new_vec_m = BETA_ONE * vec_m + (1.0 - BETA_ONE) * vec_grad
    new_vec_v = BETA_TWO * vec_v + (1.0 - BETA_TWO) * vec_grad * vec_grad
    bias_one = 1.0 - BETA_ONE**STEP_COUNT
    vec_step = new_vec_m / bias_one / (jnp.sqrt(new_vec_v / bias_two) + EPSILON)
    slot_hot = (jnp.arange(shards, dtype=jnp.int32)[:, None] == owner[None, :]).astype(jnp.float32)
    outgoing = jnp.dot(slot_hot, grad.reshape(tiles, rows_dev * cols_dev), precision=HIGH)
    outgoing = outgoing.reshape(shards, rows_dev, cols_dev)
    arrived = lax.all_to_all(outgoing, "shard", split_axis=0, concat_axis=1, tiled=True)[0]
    whole = lax.all_gather(arrived, "tensor", axis=1, tiled=True)
    start = lax.axis_index("tensor") * cols_dev
    tile_rows = lax.dynamic_slice_in_dim(whole, start, cols_dev, 0)
    new_left = STAT_DECAY * left_stat[0] + (1.0 - STAT_DECAY) * jnp.dot(
        tile_rows, whole.T, precision=HIGH
    )
    new_right = STAT_DECAY * right_stat[0] + (1.0 - STAT_DECAY) * jnp.dot(
        arrived.T, whole, precision=HIGH
    )
    right_full = lax.all_gather(right_root[0], "tensor", axis=0, tiled=True).astype(jnp.float32)
    left_part = jnp.dot(left_root[0].astype(jnp.float32), whole, precision=HIGH)
    row_block = jnp.dot(left_part, right_full, precision=HIGH)
    direction = lax.all_to_all(row_block[None], "tensor", split_axis=2, concat_axis=1, tiled=True)[
        0
    ]
    returned = lax.all_to_all(
        direction.reshape(shards, rows_dev, cols_dev),
        "shard",
        split_axis=0,
        concat_axis=0,
        tiled=True,
    )
    update = jnp.dot(slot_hot.T, returned.reshape(shards, rows_dev * cols_dev), precision=HIGH)
    update = update.reshape(tiles, rows_dev, cols_dev)
    shampoo_local = jnp.sum(update * update, axis=(1, 2))
    adam_total, shampoo_total = lax.psum((adam_sq, shampoo_local), ("shard", "tensor"))
    graft = jnp.sqrt(adam_total) / (jnp.sqrt(shampoo_total) + NORM_EPS)
    update = graft[:, None, None] * update
    return (update, new_adam_v, new_left[None], new_right[None], new_vec_m, new_vec_v, vec_step)


def solution(mesh):
    in_specs = (
        P("tensor", None, "shard", None),
        P(None, "shard", "tensor"),
        P("shard", "tensor", None),
        P("shard", "tensor", None),
        P("shard", "tensor", None),
        P("shard", "tensor", None),
        P(),
        P("tensor", None, "shard"),
        P(None, "shard"),
        P(None, "shard"),
    )
    out_specs = (
        P(None, "shard", "tensor"),
        P(None, "shard", "tensor"),
        P("shard", "tensor", None),
        P("shard", "tensor", None),
        P(None, "shard"),
        P(None, "shard"),
        P(None, "shard"),
    )
    return jax.shard_map(local, mesh=mesh, in_specs=in_specs, out_specs=out_specs, check_vma=False)
```

profile of v0, /device:TPU:0, one launch (start us, length us, event | category | flops | bytes accessed | tf_op | source)
XLA Modules:
  0.0 205.5 jit_solution(14201237901707531373)
XLA Ops:
  7.2 0.0 copy-start
  7.2 0.0 reduce-scatter.4.cloned.1.call-start
  7.2 1.8 copy.38
  9.0 1.8 reshape.39
  10.8 0.0 reduce-scatter.4.cloned.1.call-update
  10.8 0.0 all-gather.4.cloned.1.call-start
  10.9 28.5 %reduce-scatter.4.cloned.1.call-done = f32[192,384]{1,0:T(8,128)} async-done(((f32[768,384]{1,0:T(8,128)}), f32[192,384]{1,0:T(8,128)}) %reduce-scatter.4.cloned.1.call-update) | async-done | bytes 294928
  39.4 1.2 reshape.40
  40.6 0.2 copy.39
  40.9 0.0 copy-start.2
  40.9 0.2 reshape.35
  41.1 0.2 dot_general.27
  41.3 0.0 copy-done.4
  41.4 0.8 fusion.9
  42.2 0.0 copy-done.2
  42.2 0.3 copy.30
  42.4 25.5 %all_to_all.29 = f32[8,96,192]{2,1,0:T(8,128)S(1)} all-to-all(f32[8,96,192]{2,1,0:T(8,128)S(1)} %copy.30), channel_id=1, replica_groups=mesh['shard'=8,'tensor'=4] {'shard'}, dimensions={0} | all-to-all | bytes 1179648 | tf_op jit(solution)/shard_map/all_to_all | solution.py:35
  67.9 1.1 copy.37
  69.0 0.0 all-gather.4.cloned.1.call-update
  69.0 0.0 all-gather.6.cloned.1.call-start
  69.1 0.7 all-gather.6.cloned.1.call-update
  69.7 21.6 %all-gather.4.cloned.1.call-done = f32[768,768]{0,1:T(8,128)} async-done(((f32[768,192]{0,1:T(8,128)}), f32[768,768]{0,1:T(8,128)}) %all-gather.4.cloned.1.call-update) | async-done | bytes 2359312 | tf_op jit(solution)/shard_map/all_gather | solution.py:36
  91.3 0.0 copy-done
  91.3 3.1 %fusion.11 = f32[768,192]{0,1:T(8,128)S(1)} fusion(f32[768,768]{0,1:T(8,128)} %all-gather.4.cloned.1.call-done, bf16[1,192,768]{2,1,0:T(8,128)(2,1)S(1)} %copy-done), kind=kOutput, calls=%fused_computation.17 | convolution fusion | flops 1358954496 | bytes 3244032 | tf_op jit(solution)/shard_map/dot_general | solution.py:46
  94.4 16.0 %all-gather.6.cloned.1.call-done = bf16[1,768,768]{2,1,0:T(8,128)(2,1)} async-done(((bf16[1,192,768]{2,1,0:T(8,128)(2,1)}), bf16[1,768,768]{2,1,0:T(8,128)(2,1)}) %all-gather.6.cloned.1.call-update) | async-done | bytes 1179664 | tf_op jit(solution)/shard_map/all_gather | solution.py:45
  110.4 2.1 %convolution_bitcast_fusion = f32[1,192,768]{2,1,0:T(8,128)S(1)} fusion(f32[768,192]{0,1:T(8,128)S(1)} %fusion.11, bf16[1,768,768]{2,1,0:T(8,128)(2,1)} %all-gather.6.cloned.1.call-done), kind=kOutput, calls=%fused_computation.6 | convolution fusion | flops 1358954496 | bytes 2359296 | tf_op jit(solution)/shard_map/dot_general | solution.py:47
  112.6 0.6 copy.32
  113.2 14.1 %all_to_all.30 = f32[1,192,768]{1,0,2:T(1,128)S(1)} all-to-all(f32[1,192,768]{1,0,2:T(1,128)S(1)} %copy.32), channel_id=1, replica_groups=mesh['shard'=8,'tensor'=4] {'tensor'}, dimensions={2} | all-to-all | bytes 1179648 | tf_op jit(solution)/shard_map/all_to_all | solution.py:48
  127.2 0.4 copy.33
  127.7 0.0 copy-start.5
  127.7 0.0 copy-start.6
  127.7 0.0 copy-start.7
  127.7 1.5 all_to_all.23
  129.2 2.3 %copy.34 = f32[1,4,192,192]{3,2,1,0:T(8,128)} copy(f32[1,4,192,192]{3,1,2,0:T(4,128)} %bitcast.44) | data formatting | bytes 1179648 | tf_op jit(solution)/shard_map/all_to_all | solution.py:48
  131.5 5.5 %all-to-all-start.2 = ((f32[8,96,192]{2,1,0:T(8,128)}), f32[8,96,192]{2,1,0:T(8,128)}, u32[]{:S(2)}, u32[]{:S(2)}) async-start(f32[8,96,192]{2,1,0:T(8,128)} %bitcast.43), calls=%async_computation.2 | async-start | bytes 1572864 | tf_op jit(solution)/shard_map/all_to_all | solution.py:51
  137.0 0.0 copy-done.5
  137.0 6.2 %psum.23 = f32[4,96]{1,0:T(4,128)S(1)} all-reduce(f32[4,96]{1,0:T(4,128)S(1)} %bitcast.49), channel_id=1, replica_groups=mesh['shard'=8,'tensor'=4] {'tensor'}, use_global_device_ids=true, to_apply=%region_5.0 | all-reduce | flops 384 | bytes 3072 | tf_op jit(solution)/shard_map/psum | solution.py:27
  143.3 0.6 add_divide_fusion
  143.9 2.1 %multiply_reduce_fusion.1 = (f32[4]{0:T(128)S(1)}, f32[4,96,192]{2,1,0:T(8,128)}) fusion(f32[4,96,192]{2,1,0:T(8,128)} %copy-done.2, f32[4,96,192]{2,1,0:T(8,128)} %param.11), kind=kLoop, calls=%fused_computation.16 | loop fusion | flops 663548 | bytes 884752 | tf_op jit(solution)/shard_map/reduce_sum | solution.py:26
  146.0 4.0 %fusion.3 = f32[1,192,768]{2,1,0:T(8,128)} fusion(f32[768,768]{0,1:T(8,128)S(1)} %copy-done.1, s32[]{:T(128)S(6)} %select_n.3, f32[1,192,768]{2,1,0:T(8,128)} %param.12), kind=kOutput, calls=%fused_computation.5 | convolution fusion | flops 1359396864 | bytes 4325380 | tf_op jit(solution)/shard_map/dot_general | solution.py:39
  150.0 4.8 %fusion.1 = f32[1,192,768]{2,1,0:T(8,128)} fusion(f32[768,192]{1,0:T(8,128)S(1)} %bitcast.41, f32[768,768]{0,1:T(8,128)S(1)} %copy-done.1, f32[1,192,768]{2,1,0:T(8,128)S(1)} %copy-done.3), kind=kOutput, calls=%fused_computation.2 | convolution fusion | flops 1359396864 | bytes 4128768 | tf_op jit(solution)/shard_map/dot_general | solution.py:42
  154.8 2.2 %all-to-all-done.2 = f32[8,96,192]{2,1,0:T(8,128)} async-done(((f32[8,96,192]{2,1,0:T(8,128)}), f32[8,96,192]{2,1,0:T(8,128)}, u32[]{:S(2)}, u32[]{:S(2)}) %all-to-all-start.2) | async-done | bytes 589856 | tf_op jit(solution)/shard_map/all_to_all | solution.py:51
  157.0 1.4 reshape.36
  158.5 0.3 dot_general.32
  158.8 1.1 multiply_reduce_fusion
  159.9 38.0 %all-reduce = (f32[4]{0:T(128)S(1)}, f32[4]{0:T(128)S(1)}) all-reduce(f32[4]{0:T(128)S(1)} %get-tuple-element.42, f32[4]{0:T(128)S(1)} %get-tuple-element.40), channel_id=1, replica_groups=mesh['shard'=8,'tensor'=4] {'shard','tensor'}, use_global_device_ids=true, to_apply=%region_4.0 | all-reduce | flops 8 | bytes 64 | tf_op jit(solution)/shard_map/psum | solution.py:61
  198.0 0.1 broadcast_multiply_fusion
  198.1 0.8 copy.36
  (8 shorter events, 0.0 us)
Async XLA Ops:
  7.2 84.1 %copy-start = (bf16[1,192,768]{2,1,0:T(8,128)(2,1)S(1)}, bf16[1,192,768]{2,1,0:T(8,128)(2,1)}, u32[]{:S(2)}) copy-start(bf16[1,192,768]{2,1,0:T(8,128)(2,1)} %param.14) | copy-start | bytes 884740
  7.2 32.2 %reduce-scatter.4.cloned.1.call-start = ((), (), s32[]{:S(2)}) async-start(), calls=%async_computation.6 | async-start | bytes 1474560
  10.8 30.5 %copy-start.4 = (s32[4]{0:T(128)S(1)}, s32[4]{0:T(128)}, u32[]{:S(2)}) copy-start(s32[4]{0:T(128)} %param.16) | copy-start | bytes 52
  10.8 80.5 %all-gather.4.cloned.1.call-start = ((), (), s32[]{:S(2)}) async-start(), calls=%async_computation.4 | async-start | bytes 2949120 | tf_op jit(solution)/shard_map/all_gather | solution.py:36
  40.9 1.3 copy-start.2
  69.0 41.4 %all-gather.6.cloned.1.call-start = ((), (), s32[]{:S(2)}) async-start(), calls=%async_computation.5 | async-start | bytes 1474560 | tf_op jit(solution)/shard_map/all_gather | solution.py:45
  127.7 9.3 %copy-start.5 = (f32[1,4,96]{2,1,0:T(4,128)S(1)}, f32[1,4,96]{2,1,0:T(4,128)}, u32[]{:S(2)}) copy-start(f32[1,4,96]{2,1,0:T(4,128)} %param.17) | copy-start | bytes 4612
  127.7 15.6 %copy-start.6 = (f32[4,96]{1,0:T(4,128)S(1)}, f32[4,96]{1,0:T(4,128)}, u32[]{:S(2)}) copy-start(f32[4,96]{1,0:T(4,128)} %param.19) | copy-start | bytes 4612
  127.7 15.6 %copy-start.7 = (f32[4,96]{1,0:T(4,128)S(1)}, f32[4,96]{1,0:T(4,128)}, u32[]{:S(2)}) copy-start(f32[4,96]{1,0:T(4,128)} %param.18) | copy-start | bytes 4612
  129.2 16.8 %copy-start.1 = (f32[768,768]{0,1:T(8,128)S(1)}, f32[768,768]{0,1:T(8,128)}, u32[]{:S(2)}) copy-start(f32[768,768]{0,1:T(8,128)} %all-gather.4.cloned.1.call-done) | copy-start | bytes 7077892
  131.5 25.5 %all-to-all-start.2 = ((f32[8,96,192]{2,1,0:T(8,128)}), f32[8,96,192]{2,1,0:T(8,128)}, u32[]{:S(2)}, u32[]{:S(2)}) async-start(f32[8,96,192]{2,1,0:T(8,128)} %bitcast.43), calls=%async_computation.2 | async-start | bytes 1572864 | tf_op jit(solution)/shard_map/all_to_all | solution.py:51
  143.9 6.1 %copy-start.3 = (f32[1,192,768]{2,1,0:T(8,128)S(1)}, f32[1,192,768]{2,1,0:T(8,128)}, u32[]{:S(2)}) copy-start(f32[1,192,768]{2,1,0:T(8,128)} %param.13) | copy-start | bytes 1769476
Sparse Core Ops, SparseCore 0:
  11.0 28.4 reduce-scatter.3
  69.1 22.1 all-gather.3
  93.0 17.4 all-gather.5
where the time goes:
time: 206 us; the launch traced here: 205 us
  blocking collectives  83.8 us (41%)
  waiting for transfers between devices  69.1 us (34%)
  matrix products  16 us (8%)
  local copies, waits for them, and re-layouts  14.2 us (7%)
  between operations  13.9 us (7%)
  starting transfers between devices  5.64 us (3%)
  other arithmetic  2.89 us (1%)
    psum x1, blocking collectives, local(): lax.psum((adam_sq, shampoo_local), ('shard', 'tensor'))  38 us
    unnamed x4, waiting for transfers between devices  29.3 us
    all_to_all x1, blocking collectives, local(): lax.all_to_all(outgoing, 'shard', split_axis=0, concat_axis=1, tiled=True)  25.5 us
    all_gather x1, waiting for transfers between devices, local(): whole = lax.all_gather(arrived, 'tensor', axis=1, tiled=True)  21.6 us
    all_gather x1, waiting for transfers between devices, local(): lax.all_gather(right_root[0], 'tensor', axis=0, tiled=True)  16 us
    all_to_all x1, blocking collectives, local(): lax.all_to_all(row_block[None], 'tensor', split_axis=2, concat_axis=1, ti...  14.1 us
    psum x1, blocking collectives, local(): vec_grad = lax.psum(vec_parts[0], 'tensor')  6.25 us
    unnamed x21, local copies, waits for them, and re-layouts  5.86 us
  transfers between devices with their start and end apart: 4, of which 4 were waited for; matrix products, arithmetic and copies ran while one was open for 7% of the time, Pallas kernels for 0%

commit v1 on v0

v1 whole, which is shorter than its diff:
```python
import functools

import jax
import jax.numpy as jnp
from jax import lax
from jax.experimental import pallas as pl
from jax.experimental.pallas import tpu as pltpu
from jax.sharding import PartitionSpec as P

BETA_ONE = 0.9
BETA_TWO = 0.95
STAT_DECAY = 0.95
STEP_COUNT = 10.0
EPSILON = 1e-08
NORM_EPS = 1e-06
BIAS_ONE = 1.0 - BETA_ONE**STEP_COUNT
BIAS_TWO = 1.0 - BETA_TWO**STEP_COUNT
HIGH = lax.Precision.HIGHEST
LANES = 128
EXTRA = 8
F32 = jnp.float32
BF16 = jnp.bfloat16


def plain(
    grad_parts, adam_v, left_stat, right_stat, left_root, right_root, owner, vec_parts, vec_m, vec_v
):
    shards = lax.axis_size("shard")
    tiles = owner.shape[0]
    grad = lax.psum_scatter(grad_parts[0], "tensor", scatter_dimension=2, tiled=True)
    rows_dev = grad.shape[1]
    cols_dev = grad.shape[2]
    new_adam_v = BETA_TWO * adam_v + (1.0 - BETA_TWO) * grad * grad
    adam_dir = grad / (jnp.sqrt(new_adam_v / BIAS_TWO) + EPSILON)
    adam_sq = jnp.sum(adam_dir * adam_dir, axis=(1, 2))
    vec_grad = lax.psum(vec_parts[0], "tensor")
    new_vec_m, new_vec_v, vec_step = vec_update(vec_grad, vec_m, vec_v)
    slot_hot = (jnp.arange(shards, dtype=jnp.int32)[:, None] == owner[None, :]).astype(F32)
    outgoing = jnp.dot(slot_hot, grad.reshape(tiles, rows_dev * cols_dev), precision=HIGH)
    outgoing = outgoing.reshape(shards, rows_dev, cols_dev)
    arrived = lax.all_to_all(outgoing, "shard", split_axis=0, concat_axis=1, tiled=True)[0]
    whole = lax.all_gather(arrived, "tensor", axis=1, tiled=True)
    start = lax.axis_index("tensor") * cols_dev
    tile_rows = lax.dynamic_slice_in_dim(whole, start, cols_dev, 0)
    new_left = STAT_DECAY * left_stat[0] + (1.0 - STAT_DECAY) * jnp.dot(
        tile_rows, whole.T, precision=HIGH
    )
    new_right = STAT_DECAY * right_stat[0] + (1.0 - STAT_DECAY) * jnp.dot(
        arrived.T, whole, precision=HIGH
    )
    left_full = lax.all_gather(left_root[0], "tensor", axis=0, tiled=True).astype(F32)
    right_part = jnp.dot(whole, right_root[0].astype(F32).T, precision=HIGH)
    direction = jnp.dot(left_full, right_part, precision=HIGH)
    returned = lax.all_to_all(
        direction.reshape(shards, rows_dev, cols_dev),
        "shard",
        split_axis=0,
        concat_axis=0,
        tiled=True,
    )
    update = jnp.dot(slot_hot.T, returned.reshape(shards, rows_dev * cols_dev), precision=HIGH)
    update = update.reshape(tiles, rows_dev, cols_dev)
    shampoo_local = jnp.sum(update * update, axis=(1, 2))
    adam_total, shampoo_total = lax.psum((adam_sq, shampoo_local), ("shard", "tensor"))
    graft = jnp.sqrt(adam_total) / (jnp.sqrt(shampoo_total) + NORM_EPS)
    update = graft[:, None, None] * update
    return (update, new_adam_v, new_left[None], new_right[None], new_vec_m, new_vec_v, vec_step)


def vec_update(vec_grad, vec_m, vec_v):
    new_vec_m = BETA_ONE * vec_m + (1.0 - BETA_ONE) * vec_grad
    new_vec_v = BETA_TWO * vec_v + (1.0 - BETA_TWO) * vec_grad * vec_grad
    vec_step = new_vec_m / BIAS_ONE / (jnp.sqrt(new_vec_v / BIAS_TWO) + EPSILON)
    return new_vec_m, new_vec_v, vec_step


def place():
    t = lax.axis_index("tensor")
    return lax.axis_index("shard"), t, t // 2, lax.rem(t, 2)


def lane_tile(index):
    return pl.ds(pl.multiple_of(index * LANES, LANES), LANES)


def swap_halves(a):
    return pltpu.roll(a, LANES // 2, 1)


def low_lanes(rows):
    return lax.broadcasted_iota(jnp.int32, (rows, LANES), 1) < LANES // 2


def fold(mid, core):
    half = mid.shape[0] // 2
    turned = swap_halves(mid)
    first = core == 0
    low = low_lanes(half)
    top = jnp.where(first, mid[:half], turned[:half])
    bottom = jnp.where(first, turned[half:], mid[half:])
    return jnp.where(low, top, bottom)


def unfold(block, rows, core):
    main, side = block[:rows], block[rows:]
    wide = jnp.concatenate([side, swap_halves(side)], axis=0)
    turned = swap_halves(main)
    first = core == 0
    head = jnp.where(first, main, jnp.where(low_lanes(rows), wide, turned))
    return head, jnp.where(first, wide, turned)[:, : LANES // 2]


def split_kernel(rows, tiles, g_ref, vec_ref, sf_ref, sn_ref, kf_ref, kn_ref):
    _, _, chip, core = place()
    packed = rows + rows // 2
    for out, far, own in ((sf_ref, True, False), (sn_ref, False, False), (kf_ref, True, True), (kn_ref, False, True)):
        x = 1 - chip if far else chip
        d = core if own else 1 - core
        for k in range(tiles):
            base = k * packed
            out[base : base + rows] = g_ref[0, k, :, lane_tile(3 * x + 2 * d)]
            out[base + rows : base + packed] = fold(g_ref[0, k, :, lane_tile(3 * x + 1)], d)
        if far:
            out[tiles * packed :] = jnp.zeros((EXTRA, LANES), F32)
            out[tiles * packed : tiles * packed + tiles, : rows] = vec_ref[0]


def tile_of(owner_ref, slot, tiles):
    k = jnp.int32(0)
    for i in range(1, tiles):
        k = jnp.where(owner_ref[i] == slot, i, k)
    return k


def adam_kernel(
    rows, tiles, shards, owner_ref, kn_ref, rn_ref, u_ref, r_ref, v_ref, m_ref, vv_ref, *refs
):
    outs, (nv_ref, vm_ref, vn_ref, vs_ref), (g_ref, ext_ref) = refs[:shards], refs[shards : shards + 4], refs[shards + 4 :]
    shard, _, _, core = place()
    packed = rows + rows // 2

    def one(g, v_old):
        v_new = BETA_TWO * v_old + (1.0 - BETA_TWO) * g * g
        step = g / (jnp.sqrt(v_new / BIAS_TWO) + EPSILON)
        sq = step * step
        return v_new, jnp.sum(sq.reshape(-1, 8, sq.shape[1]), axis=0)

    for k in range(tiles):
        at = slice(k * packed, k * packed + packed)
        g = kn_ref[at] + rn_ref[at] + r_ref[at]
        g_ref[k] = g
        head, tail = unfold(g, rows, core)
        nv_ref[k, :, :LANES], ext_ref[k] = one(head, v_ref[k, :, :LANES])
        nv_ref[k, :, LANES:], sq = one(tail, v_ref[k, :, LANES:])
        ext_ref[k, :, : LANES // 2] += sq
    for j in range(shards):
        k = tile_of(owner_ref, shard ^ j, tiles)
        outs[j][:packed] = g_ref[k]
        outs[j][packed:] = ext_ref[k]
    vec = u_ref[:tiles, :rows] + r_ref[tiles * packed : tiles * packed + tiles, :rows]
    vm_ref[...], vn_ref[...], vs_ref[...] = vec_update(vec, m_ref[...], vv_ref[...])


def roots_kernel(own_ref, core_ref, chip_ref, both_ref, left_ref, right_ref):
    _, t, _, _ = place()
    rows = own_ref.shape[1]
    for mask, ref in enumerate((own_ref, core_ref, chip_ref, both_ref)):
        at = pl.ds(pl.multiple_of((t ^ mask) * rows, rows), rows)
        left_ref[at, :] = ref[0]
        right_ref[at, :] = ref[1]


def halves(a):
    high = a.astype(BF16)
    return high, (a - high.astype(F32)).astype(BF16)


def owner_kernel(rows, shards, *refs):
    pieces, refs = refs[:8], refs[8:]
    left_ref, right_ref, refs = refs[0], refs[1], refs[2:]
    outs, (gh_ref, gl_ref), (zh_ref, zl_ref, dir_ref) = refs[:shards], refs[shards : shards + 2], refs[shards + 2 :]
    shard, _, chip, core = place()
    packed = rows + rows // 2
    half = rows // 2
    group = shards // 2
    low = low_lanes(half)
    adam = jnp.zeros((EXTRA, LANES), F32)
    for g in range(2):
        own, other = pieces[4 * g : 4 * g + 2], pieces[4 * g + 2 : 4 * g + 4]
        for i in range(group):
            to = pl.ds(pl.multiple_of((shard ^ (g * group + i)) * rows, rows), rows)
            base = i * (packed + EXTRA)
            for x, (mine, peer) in ((chip, own), (1 - chip, other)):
                a, b = mine[base : base + packed], peer[base : base + packed]
                adam += mine[base + packed : base + packed + EXTRA]
                adam += peer[base + packed : base + packed + EXTRA]
                first, last = jnp.where(core == 0, a, b), jnp.where(core == 0, b, a)
                fs, ls = first[rows:], last[rows:]
                mid = jnp.concatenate(
                    [
                        jnp.where(low, fs, swap_halves(ls)),
                        jnp.where(low, swap_halves(fs), ls),
                    ],
                    axis=0,
                )
                for n, tile in enumerate((first[:rows], mid, last[:rows])):
                    gh_ref[to, lane_tile(3 * x + n)], gl_ref[to, lane_tile(3 * x + n)] = halves(tile)
    size = gh_ref.shape[0]
    step = 256

    def right(i, carry):
        at = pl.ds(pl.multiple_of(i * step, step), step)
        z = jnp.dot(gh_ref[at, :], right_ref[...], preferred_element_type=F32)
        z += jnp.dot(gl_ref[at, :], right_ref[...], preferred_element_type=F32)
        zh_ref[at, :], zl_ref[at, :] = halves(z)
        return carry

    lax.fori_loop(0, size // step, right, 0)

    def left(i, total):
        at = pl.ds(pl.multiple_of(i * step, step), step)
        d = jnp.dot(left_ref[at, :], zh_ref[...], preferred_element_type=F32)
        d += jnp.dot(left_ref[at, :], zl_ref[...], preferred_element_type=F32)
        dir_ref[at, :] = d
        return total + jnp.sum((d * d).reshape(-1, 8, size), axis=0)

    squares = lax.fori_loop(0, size // step, left, jnp.zeros((8, size), F32))

    def whole(a):
        return jnp.sum(jnp.sum(a, axis=1, keepdims=True), axis=0, keepdims=True)

    graft = jnp.sqrt(whole(adam)) / (jnp.sqrt(whole(squares)) + NORM_EPS)
    for j in range(shards):
        at = pl.ds(pl.multiple_of((shard ^ j) * rows, rows), rows)
        outs[j][:rows] = graft * dir_ref[at, lane_tile(3 * chip + 2 * core)]
        outs[j][rows:] = graft * fold(dir_ref[at, lane_tile(3 * chip + 1)], core)


def stats_kernel(tiles, owner_ref, gh_ref, gl_ref, left_ref, right_ref, nl_ref, nr_ref):
    shard, t, chip, core = place()
    rows = left_ref.shape[1]
    held = owner_ref[0] == shard
    for i in range(1, tiles):
        held = jnp.logical_or(held, owner_ref[i] == shard)

    def product(high, low, dims):
        dot = functools.partial(lax.dot_general, dimension_numbers=(dims, ((), ())), preferred_element_type=F32)
        return dot(high, gh_ref[...]) + dot(high, gl_ref[...]) + dot(low, gh_ref[...])

    def refreshed(old, new):
        return STAT_DECAY * old + (1.0 - STAT_DECAY) * jnp.where(held, new, 0.0)

    at = pl.ds(pl.multiple_of(t * rows, rows), rows)
    nl_ref[0] = refreshed(left_ref[0], product(gh_ref[at, :], gl_ref[at, :], ((1,), (1,))))
    end, mid = lane_tile(3 * chip + 2 * core), lane_tile(3 * chip + 1)
    ends = product(gh_ref[:, end], gl_ref[:, end], ((0,), (0,)))
    mids = product(gh_ref[:, mid], gl_ref[:, mid], ((0,), (0,)))
    half = LANES // 2

    @pl.when(core == 0)
    def _():
        nr_ref[0, :LANES] = refreshed(right_ref[0, :LANES], ends)
        nr_ref[0, LANES:] = refreshed(right_ref[0, LANES:], mids[:half])

    @pl.when(core == 1)
    def _():
        nr_ref[0, :half] = refreshed(right_ref[0, :half], mids[half:])
        nr_ref[0, half:] = refreshed(right_ref[0, half:], ends)


def back_kernel(rows, tiles, shards, owner_ref, *refs):
    blocks, out_ref = refs[:shards], refs[shards]
    shard, _, _, core = place()
    for k in range(tiles):
        for j in range(shards):

            @pl.when((shard ^ j) == owner_ref[k])
            def _(k=k, j=j):
                out_ref[k, :, :LANES], out_ref[k, :, LANES:] = unfold(blocks[j][...], rows, core)


def shape(dims, dtype=F32):
    return jax.ShapeDtypeStruct(dims, dtype)


def kernel_call(body, outs, ins, scratch=(), smem=0, flops=0, mib=16):
    vmem = pl.BlockSpec(memory_space=pltpu.VMEM)
    moved = sum(a.size * a.dtype.itemsize for a in (*ins, *jax.tree.leaves(outs)))
    return pl.pallas_call(
        body,
        out_shape=outs,
        in_specs=[pl.BlockSpec(memory_space=pltpu.SMEM)] * smem + [vmem] * (len(ins) - smem),
        out_specs=jax.tree.map(lambda _: vmem, outs),
        scratch_shapes=list(scratch),
        compiler_params=pltpu.CompilerParams(vmem_limit_bytes=mib << 20),
        cost_estimate=pl.CostEstimate(flops=flops, bytes_accessed=moved, transcendentals=0),
    )(*ins)


def swap(a, axis, mask):
    return lax.ppermute(a, axis, [(i, i ^ mask) for i in range(lax.axis_size(axis))])


def local(
    grad_parts, adam_v, left_stat, right_stat, left_root, right_root, owner, vec_parts, vec_m, vec_v
):
    shards = lax.axis_size("shard")
    tiles, rows, cols = adam_v.shape
    size = grad_parts.shape[3]
    packed = rows + rows // 2

    block = shape((tiles * packed, LANES))
    wide = shape((tiles * packed + EXTRA, LANES))
    sf, sn, kf, kn = kernel_call(
        functools.partial(split_kernel, rows, tiles), (wide, block, wide, block), (grad_parts, vec_parts)
    )
    u = kf + swap(sf, "tensor", 1)
    rn = swap(sn, "tensor", 1)
    r = swap(u, "tensor", 2)
    vec = shape((tiles, rows))
    res = kernel_call(
        functools.partial(adam_kernel, rows, tiles, shards),
        (shape((packed + EXTRA, LANES)),) * shards + (shape(adam_v.shape), vec, vec, vec),
        (owner, kn, rn, u[tiles * packed :], r, adam_v, vec_m, vec_v),
        (pltpu.VMEM((tiles, packed, LANES), F32), pltpu.VMEM((tiles, EXTRA, LANES), F32)),
        smem=1,
    )
    outgoing, (new_adam_v, new_vec_m, new_vec_v, vec_step) = res[:shards], res[shards:]

    roots = jnp.concatenate([left_root, right_root], axis=0)
    roots, outgoing = lax.optimization_barrier((roots, outgoing))
    arrived = [outgoing[0]] + [swap(outgoing[j], "shard", j) for j in range(1, shards)]
    roots_chip, roots_core = swap(roots, "tensor", 2), swap(roots, "tensor", 1)
    full = shape((size, size), BF16)
    left_full, right_full = kernel_call(
        roots_kernel, (full, full), (roots, roots_core, roots_chip, swap(roots_chip, "tensor", 1))
    )
    pieces = []
    for part in (arrived[: shards // 2], arrived[shards // 2 :]):
        mine = jnp.concatenate(part, axis=0)
        across = swap(mine, "tensor", 2)
        pieces += [mine, swap(mine, "tensor", 1), across, swap(across, "tensor", 1)]
    res = kernel_call(
        functools.partial(owner_kernel, rows, shards),
        (shape((packed, LANES)),) * shards + (full, full),
        (*pieces, left_full, right_full),
        (pltpu.VMEM((size, size), BF16), pltpu.VMEM((size, size), BF16), pltpu.VMEM((size, size), F32)),
        flops=8 * size**3,
        mib=32,
    )
    ready, (high, low) = res[:shards], res[shards:]
    back = [ready[0]] + [swap(ready[j], "shard", j) for j in range(1, shards)]
    new_left, new_right = kernel_call(
        functools.partial(stats_kernel, tiles),
        (shape(left_stat.shape), shape(right_stat.shape)),
        (owner, high, low, left_stat, right_stat),
        smem=1,
        flops=12 * cols * size**2,
        mib=32,
    )
    update = kernel_call(
        functools.partial(back_kernel, rows, tiles, shards), shape(adam_v.shape), (owner, *back), smem=1
    )
    return (update, new_adam_v, new_left, new_right, new_vec_m, new_vec_v, vec_step)


def solution(mesh):
    in_specs = (
        P("tensor", None, "shard", None),
        P(None, "shard", "tensor"),
        P("shard", "tensor", None),
        P("shard", "tensor", None),
        P("shard", "tensor", None),
        P("shard", "tensor", None),
        P(),
        P("tensor", None, "shard"),
        P(None, "shard"),
        P(None, "shard"),
    )
    out_specs = (
        P(None, "shard", "tensor"),
        P(None, "shard", "tensor"),
        P("shard", "tensor", None),
        P("shard", "tensor", None),
        P(None, "shard"),
        P(None, "shard"),
        P(None, "shard"),
    )
    packs = mesh.shape["tensor"] == 4 and mesh.shape["shard"] == 8
    return jax.shard_map(
        local if packs else plain, mesh=mesh, in_specs=in_specs, out_specs=out_specs, check_vma=False
    )
```

time: 206 us -> 77.1 us (0.37)
  blocking collectives: 83.8 us -> 0 us
  waiting for transfers between devices: 69.1 us -> 28.4 us
  starting transfers between devices: 5.64 us -> 32.1 us
  matrix products: 16 us -> 0 us
  Pallas kernels: 0 us -> 13.4 us
  between operations: 13.9 us -> 0.79 us
  local copies, waits for them, and re-layouts: 14.2 us -> 2.04 us
  other arithmetic: 2.89 us -> 0.09 us
    psum x2 -> x0, blocking collectives: 44.3 us -> none  [the longest x1 38 us: local(): lax.psum((adam_sq, shampoo_local), ('shard', 'tensor'))]
    all_to_all x2 -> x0, blocking collectives: 39.5 us -> none  [the longest x1 25.5 us: local(): lax.all_to_all(outgoing, 'shard', split_axis=0, concat_axis=1, tiled=True)]
    all_gather x2 -> x0, waiting for transfers between devices: 37.6 us -> none  [the longest x1 21.6 us: local(): whole = lax.all_gather(arrived, 'tensor', axis=1, tiled=True)]
    ppermute x0 -> x26, starting transfers between devices: none -> 32.1 us  [swap(): lax.ppermute(a, axis, [(i, i ^ mask) for i in range(lax.axis_size(axis))])]
    unnamed x4 -> x0, waiting for transfers between devices: 29.3 us -> none
    ppermute x0 -> x26, waiting for transfers between devices: none -> 28.4 us  [swap(): lax.ppermute(a, axis, [(i, i ^ mask) for i in range(lax.axis_size(axis))])]
    dot_general x6 -> x0, matrix products: 16 us -> none  [the longest x1 4.76 us: local(): jnp.dot(arrived.T, whole, precision=HIGH)]
    pallas_call x0 -> x6, Pallas kernels: none -> 13.4 us  [kernel_call(): pl.pallas_call(body, out_shape=outs, in_specs=[pl.BlockSpec(memory_space=...]
  transfers between devices with their start and end apart: 4 -> 26, of which waited for: 4 -> 12; matrix products, arithmetic and copies ran while one was open for 7% -> 0% of each run, Pallas kernels for 0% -> 5%
where the time goes in v1:
time: 77.1 us; the launch traced here: 76.7 us
  starting transfers between devices  32.1 us (42%)
  waiting for transfers between devices  28.4 us (37%)
  Pallas kernels  13.4 us (17%)
  local copies, waits for them, and re-layouts  2.04 us (3%)
  between operations  0.79 us (1%)
    ppermute x26, starting transfers between devices, swap(): lax.ppermute(a, axis, [(i, i ^ mask) for i in range(lax.axis_size(axis))])  32.1 us
    ppermute x26, waiting for transfers between devices, swap(): lax.ppermute(a, axis, [(i, i ^ mask) for i in range(lax.axis_size(axis))])  28.4 us
    pallas_call x6, Pallas kernels, kernel_call(): pl.pallas_call(body, out_shape=outs, in_specs=[pl.BlockSpec(memory_space=...  13.4 us
    unnamed x26, local copies, waits for them, and re-layouts  2.02 us
  transfers between devices with their start and end apart: 26, of which 12 were waited for; matrix products, arithmetic and copies ran while one was open for 0% of the time, Pallas kernels for 5%

profile of v1, /device:TPU:0, one launch (start us, length us, event | category | flops | bytes accessed | tf_op | source)
XLA Modules:
  0.0 76.7 jit_solution(3983443725364787749)
XLA Ops:
  0.6 1.3 %copy-done = f32[1,4,96,768]{3,2,1,0:T(8,128)S(1)} copy-done((f32[1,4,96,768]{3,2,1,0:T(8,128)S(1)}, f32[1,4,96,768]{3,2,1,0:T(8,128)}, u32[]{:S(2)}) %copy-start) | copy-done | bytes 1179672
  1.9 0.7 copy-done.3
  2.6 0.3 shard_map.153
  2.9 0.0 copy-start.1
  2.9 0.0 copy-start.2
  2.9 0.0 copy-start.4
  2.9 0.0 copy-start.5
  2.9 0.5 collective-permute-start.1
  3.4 1.2 %collective-permute-done.1 = f32[584,128]{1,0:T(8,128)S(1)} collective-permute-done((f32[584,128]{1,0:T(8,128)S(1)}, f32[584,128]{1,0:T(8,128)S(1)}, u32[]{:S(2)}, u32[]{:S(2)}) %collective-permute-start.1) | collective-permute-done | bytes 299040 | tf_op jit(solution)/shard_map/ppermute | solution.py:301
  4.7 2.9 %collective-permute-start.2 = (f32[584,128]{1,0:T(8,128)S(1)}, f32[584,128]{1,0:T(8,128)S(1)}, u32[]{:S(2)}, u32[]{:S(2)}) collective-permute-start(f32[584,128]{1,0:T(8,128)S(1)} %add.3), channel_id=1, source_target_pairs={{0,2},{1,3},{2,0},{3,1},{4,6},{5,7},{6,4},{7,5},{8,10},{9,11},{10,... | collective-permute-start | bytes 897032 | tf_op jit(solution)/shard_map/ppermute | solution.py:301
  7.6 0.0 collective-permute-start
  7.6 0.1 pad_maximum_fusion.own_ref
  7.7 1.5 %collective-permute-done.rn_ref = f32[576,128]{1,0:T(8,128)S(1)} collective-permute-done((f32[576,128]{1,0:T(8,128)S(1)}, f32[576,128]{1,0:T(8,128)S(1)}, u32[]{:S(2)}, u32[]{:S(2)}) %collective-permute-start) | collective-permute-done | bytes 294944 | tf_op jit(solution)/shard_map/ppermute | solution.py:301
  9.2 5.8 %collective-permute-done.2.r_ref = f32[584,128]{1,0:T(8,128)S(1)} collective-permute-done((f32[584,128]{1,0:T(8,128)S(1)}, f32[584,128]{1,0:T(8,128)S(1)}, u32[]{:S(2)}, u32[]{:S(2)}) %collective-permute-start.2) | collective-permute-done | bytes 299040 | tf_op jit(solution)/shard_map/ppermute | solution.py:301
  15.0 1.7 %shard_map.154 = (f32[152,128]{1,0:T(8,128)S(1)}, f32[152,128]{1,0:T(8,128)S(1)}, f32[152,128]{1,0:T(8,128)S(1)}, f32[152,128]{1,0:T(8,128)S(1)}, f32[152,128]{1...) custom-call(s32[4]{0:T(128)S(1)} %copy-done.2, ...), custom_call_target="tpu_custom_call" | custom-call | bytes 2113040 | tf_op jit(solution)/shard_map/pallas_call | solution.py:289
  16.7 1.7 %collective-permute-start.17 = (bf16[2,192,768]{2,1,0:T(8,128)(2,1)S(1)}, bf16[2,192,768]{2,1,0:T(8,128)(2,1)S(1)}, u32[]{:S(2)}, u32[]{:S(2)}) collective-permute-start(bf16[2,192,768]{2,1,0:T(8,128)(2,1)S(1)} %pad_maximum_fusion.own_ref), channel_id=1, source_target_pairs={{0,2},{1,3},{2,0},{3,1},{4,6},{5,7},{6,4},{7,5},{8,10},{9,11},{10,... | collective-permute-start | bytes 1769480 | tf_op jit(solution)/shard_map/ppermute | solution.py:301
  18.5 0.0 collective-permute-start.16
  18.5 1.5 %collective-permute-start.3 = (f32[152,128]{1,0:T(8,128)S(1)}, f32[152,128]{1,0:T(8,128)S(1)}, u32[]{:S(2)}, u32[]{:S(2)}) collective-permute-start(f32[152,128]{1,0:T(8,128)S(1)} %get-tuple-element.59), channel_id=1, source_target_pairs={{0,4},{4,0},{8,12},{12,8},{16,20},{20,16},{24,28},{28,24},{1,5},{5... | collective-permute-start | bytes 233480 | tf_op jit(solution)/shard_map/ppermute | solution.py:301
  20.0 1.6 %collective-permute-start.4 = (f32[152,128]{1,0:T(8,128)S(1)}, f32[152,128]{1,0:T(8,128)S(1)}, u32[]{:S(2)}, u32[]{:S(2)}) collective-permute-start(f32[152,128]{1,0:T(8,128)S(1)} %get-tuple-element.60), channel_id=1, source_target_pairs={{0,8},{4,12},{8,0},{12,4},{16,24},{20,28},{24,16},{28,20},{1,9},{5... | collective-permute-start | bytes 233480 | tf_op jit(solution)/shard_map/ppermute | solution.py:301
  21.6 2.6 %collective-permute-start.9 = (f32[152,128]{1,0:T(8,128)S(1)}, f32[152,128]{1,0:T(8,128)S(1)}, u32[]{:S(2)}, u32[]{:S(2)}) collective-permute-start(f32[152,128]{1,0:T(8,128)S(1)} %get-tuple-element.62), channel_id=1, source_target_pairs={{0,16},{4,20},{8,24},{12,28},{16,0},{20,4},{24,8},{28,12},{1,17},{... | collective-permute-start | bytes 233480 | tf_op jit(solution)/shard_map/ppermute | solution.py:301
  24.2 4.3 %collective-permute-done.9 = f32[152,128]{1,0:T(8,128)S(1)} collective-permute-done((f32[152,128]{1,0:T(8,128)S(1)}, f32[152,128]{1,0:T(8,128)S(1)}, u32[]{:S(2)}, u32[]{:S(2)}) %collective-permute-start.9) | collective-permute-done | bytes 77856 | tf_op jit(solution)/shard_map/ppermute | solution.py:301
  28.4 0.4 collective-permute-start.5
  28.8 3.8 %collective-permute-start.10 = (f32[152,128]{1,0:T(8,128)S(1)}, f32[152,128]{1,0:T(8,128)S(1)}, u32[]{:S(2)}, u32[]{:S(2)}) collective-permute-start(f32[152,128]{1,0:T(8,128)S(1)} %get-tuple-element.63), channel_id=1, source_target_pairs={{0,20},{4,16},{8,28},{12,24},{16,4},{20,0},{24,12},{28,8},{1,21},{... | collective-permute-start | bytes 233480 | tf_op jit(solution)/shard_map/ppermute | solution.py:301
  32.6 1.3 %collective-permute-start.11 = (f32[152,128]{1,0:T(8,128)S(1)}, f32[152,128]{1,0:T(8,128)S(1)}, u32[]{:S(2)}, u32[]{:S(2)}) collective-permute-start(f32[152,128]{1,0:T(8,128)S(1)} %get-tuple-element.64), channel_id=1, source_target_pairs={{0,24},{4,28},{8,16},{12,20},{16,8},{20,12},{24,0},{28,4},{1,25},{... | collective-permute-start | bytes 233480 | tf_op jit(solution)/shard_map/ppermute | solution.py:301
  33.9 1.7 %collective-permute-done.5 = f32[152,128]{1,0:T(8,128)S(1)} collective-permute-done((f32[152,128]{1,0:T(8,128)S(1)}, f32[152,128]{1,0:T(8,128)S(1)}, u32[]{:S(2)}, u32[]{:S(2)}) %collective-permute-start.5) | collective-permute-done | bytes 77856 | tf_op jit(solution)/shard_map/ppermute | solution.py:301
  35.5 2.5 %collective-permute-start.12 = (f32[152,128]{1,0:T(8,128)S(1)}, f32[152,128]{1,0:T(8,128)S(1)}, u32[]{:S(2)}, u32[]{:S(2)}) collective-permute-start(f32[152,128]{1,0:T(8,128)S(1)} %get-tuple-element.65), channel_id=1, source_target_pairs={{0,28},{4,24},{8,20},{12,16},{16,12},{20,8},{24,4},{28,0},{1,29},{... | collective-permute-start | bytes 233480 | tf_op jit(solution)/shard_map/ppermute | solution.py:301
  38.0 1.0 %collective-permute-done.10 = f32[152,128]{1,0:T(8,128)S(1)} collective-permute-done((f32[152,128]{1,0:T(8,128)S(1)}, f32[152,128]{1,0:T(8,128)S(1)}, u32[]{:S(2)}, u32[]{:S(2)}) %collective-permute-start.10) | collective-permute-done | bytes 77856 | tf_op jit(solution)/shard_map/ppermute | solution.py:301
  39.0 0.5 collective-permute-start.7
  39.6 3.1 %collective-permute-done.12 = f32[152,128]{1,0:T(8,128)S(1)} collective-permute-done((f32[152,128]{1,0:T(8,128)S(1)}, f32[152,128]{1,0:T(8,128)S(1)}, u32[]{:S(2)}, u32[]{:S(2)}) %collective-permute-start.12) | collective-permute-done | bytes 77856 | tf_op jit(solution)/shard_map/ppermute | solution.py:301
  42.6 0.5 collective-permute-start.14
  43.2 0.5 collective-permute-start.6
  43.7 2.7 %collective-permute-done.7.refs_2_ = f32[608,128]{1,0:T(8,128)S(1)} collective-permute-done((f32[608,128]{1,0:T(8,128)S(1)}, f32[608,128]{1,0:T(8,128)S(1)}, u32[]{:S(2)}, u32[]{:S(2)}) %collective-permute-start.7) | collective-permute-done | bytes 311328 | tf_op jit(solution)/shard_map/ppermute | solution.py:301
  46.4 3.3 %collective-permute-done.14.refs_6_ = f32[608,128]{1,0:T(8,128)S(1)} collective-permute-done((f32[608,128]{1,0:T(8,128)S(1)}, f32[608,128]{1,0:T(8,128)S(1)}, u32[]{:S(2)}, u32[]{:S(2)}) %collective-permute-start.14) | collective-permute-done | bytes 311328 | tf_op jit(solution)/shard_map/ppermute | solution.py:301
  49.8 0.5 collective-permute-start.15
  50.3 0.2 shard_map.155
  50.5 0.9 %collective-permute-done.8.refs_3_ = f32[608,128]{1,0:T(8,128)S(1)} collective-permute-done((f32[608,128]{1,0:T(8,128)S(1)}, f32[608,128]{1,0:T(8,128)S(1)}, u32[]{:S(2)}, u32[]{:S(2)}) %collective-permute-start.8) | collective-permute-done | bytes 311328 | tf_op jit(solution)/shard_map/ppermute | solution.py:301
  51.4 0.4 collective-permute-done.15.refs_7_
  51.8 5.5 %shard_map.156 = (f32[144,128]{1,0:T(8,128)S(1)}, f32[144,128]{1,0:T(8,128)S(1)}, f32[144,128]{1,0:T(8,128)S(1)}, f32[144,128]{1,0:T(8,128)S(1)}, f32[144,128]{1...) custom-call(f32[608,128]{1,0:T(8,128)S(1)} %constant_dynamic-update-, ...), custom_call_target="tpu_custom_call" | custom-call | flops 3623878656 | bytes 7798784 | tf_op jit(solution)/shard_map/pallas_call | solution.py:289
  57.3 1.3 %collective-permute-start.19 = (f32[144,128]{1,0:T(8,128)S(1)}, f32[144,128]{1,0:T(8,128)S(1)}, u32[]{:S(2)}, u32[]{:S(2)}) collective-permute-start(f32[144,128]{1,0:T(8,128)S(1)} %get-tuple-element.70), channel_id=1, source_target_pairs={{0,4},{4,0},{8,12},{12,8},{16,20},{20,16},{24,28},{28,24},{1,5},{5... | collective-permute-start | bytes 221192 | tf_op jit(solution)/shard_map/ppermute | solution.py:301
  58.6 1.5 %collective-permute-start.20 = (f32[144,128]{1,0:T(8,128)S(1)}, f32[144,128]{1,0:T(8,128)S(1)}, u32[]{:S(2)}, u32[]{:S(2)}) collective-permute-start(f32[144,128]{1,0:T(8,128)S(1)} %get-tuple-element.71), channel_id=1, source_target_pairs={{0,8},{4,12},{8,0},{12,4},{16,24},{20,28},{24,16},{28,20},{1,9},{5... | collective-permute-start | bytes 221192 | tf_op jit(solution)/shard_map/ppermute | solution.py:301
  60.1 0.7 collective-permute-start.21
  60.9 2.3 %collective-permute-start.22 = (f32[144,128]{1,0:T(8,128)S(1)}, f32[144,128]{1,0:T(8,128)S(1)}, u32[]{:S(2)}, u32[]{:S(2)}) collective-permute-start(f32[144,128]{1,0:T(8,128)S(1)} %get-tuple-element.73), channel_id=1, source_target_pairs={{0,16},{4,20},{8,24},{12,28},{16,0},{20,4},{24,8},{28,12},{1,17},{... | collective-permute-start | bytes 221192 | tf_op jit(solution)/shard_map/ppermute | solution.py:301
  63.1 1.3 %collective-permute-start.23 = (f32[144,128]{1,0:T(8,128)S(1)}, f32[144,128]{1,0:T(8,128)S(1)}, u32[]{:S(2)}, u32[]{:S(2)}) collective-permute-start(f32[144,128]{1,0:T(8,128)S(1)} %get-tuple-element.74), channel_id=1, source_target_pairs={{0,20},{4,16},{8,28},{12,24},{16,4},{20,0},{24,12},{28,8},{1,21},{... | collective-permute-start | bytes 221192 | tf_op jit(solution)/shard_map/ppermute | solution.py:301
  64.5 2.1 %collective-permute-start.24 = (f32[144,128]{1,0:T(8,128)S(1)}, f32[144,128]{1,0:T(8,128)S(1)}, u32[]{:S(2)}, u32[]{:S(2)}) collective-permute-start(f32[144,128]{1,0:T(8,128)S(1)} %get-tuple-element.75), channel_id=1, source_target_pairs={{0,24},{4,28},{8,16},{12,20},{16,8},{20,12},{24,0},{28,4},{1,25},{... | collective-permute-start | bytes 221192 | tf_op jit(solution)/shard_map/ppermute | solution.py:301
  66.6 1.9 %collective-permute-start.25 = (f32[144,128]{1,0:T(8,128)S(1)}, f32[144,128]{1,0:T(8,128)S(1)}, u32[]{:S(2)}, u32[]{:S(2)}) collective-permute-start(f32[144,128]{1,0:T(8,128)S(1)} %get-tuple-element.76), channel_id=1, source_target_pairs={{0,28},{4,24},{8,20},{12,16},{16,12},{20,8},{24,4},{28,0},{1,29},{... | collective-permute-start | bytes 221192 | tf_op jit(solution)/shard_map/ppermute | solution.py:301
  68.5 3.9 %shard_map.158 = (f32[1,192,768]{2,1,0:T(8,128)}, f32[1,192,768]{2,1,0:T(8,128)}) custom-call(s32[4]{0:T(128)S(1)} %copy-done.2, bf16[768,768]{1,0:T(8,128)(2,1)S(1)} %get-tuple-element.78.gh_ref, bf16[768,768]{1,0:T(8,128)(2,1)S(1)} %get-tuple-element.79.gl_ref, f32[1,192,768]{2,1,0:T(8,128)S(1)} %copy-done.6, f32[1,192,768]{2,1,0:T(8,128)S(1)} %copy-done.7), custom_call_target="tpu_custom_call" | custom-call | flops 1358954496 | bytes 4718608 | tf_op jit(solution)/shard_map/pallas_call | solution.py:289
  72.4 2.4 %collective-permute-done.23.refs_5_ = f32[144,128]{1,0:T(8,128)S(1)} collective-permute-done((f32[144,128]{1,0:T(8,128)S(1)}, f32[144,128]{1,0:T(8,128)S(1)}, u32[]{:S(2)}, u32[]{:S(2)}) %collective-permute-start.23) | collective-permute-done | bytes 73760 | tf_op jit(solution)/shard_map/ppermute | solution.py:301
  74.9 1.9 %shard_map.157 = f32[4,96,192]{2,1,0:T(8,128)} custom-call(s32[4]{0:T(128)S(1)} %copy-done.2, f32[144,128]{1,0:T(8,128)S(1)} %get-tuple-element.69.refs_0_, f32[144,128]{1,0:T(8,128)S(1)} %collective-permute-done.19.refs_1_, f32[144,128]{1,0:T(8,128)S(1)} %collective-permute-done.20.refs_2_, f32[144,128]{1,0:T(8,128)S(1)} %collective-permute-done.21.refs_3_, ...), custom_call_target="tpu_custom_call" | custom-call | bytes 884752 | tf_op jit(solution)/shard_map/pallas_call | solution.py:289
  (41 shorter events, 0.2 us)
Async XLA Ops:
  0.6 1.3 %copy-start = (f32[1,4,96,768]{3,2,1,0:T(8,128)S(1)}, f32[1,4,96,768]{3,2,1,0:T(8,128)}, u32[]{:S(2)}) copy-start(f32[1,4,96,768]{3,2,1,0:T(8,128)} %g_ref.1) | copy-start | bytes 3538948
  1.9 0.7 copy-start.3
  2.6 5.0 %copy-start.8 = (bf16[1,192,768]{2,1,0:T(8,128)(2,1)S(1)}, bf16[1,192,768]{2,1,0:T(8,128)(2,1)}, u32[]{:S(2)}) copy-start(bf16[1,192,768]{2,1,0:T(8,128)(2,1)} %param.15) | copy-start | bytes 884740
  2.6 5.0 %copy-start.9 = (bf16[1,192,768]{2,1,0:T(8,128)(2,1)S(1)}, bf16[1,192,768]{2,1,0:T(8,128)(2,1)}, u32[]{:S(2)}) copy-start(bf16[1,192,768]{2,1,0:T(8,128)(2,1)} %param.14) | copy-start | bytes 884740
  2.9 12.1 %copy-start.1 = (f32[4,96,192]{2,1,0:T(8,128)S(1)}, f32[4,96,192]{2,1,0:T(8,128)}, u32[]{:S(2)}) copy-start(f32[4,96,192]{2,1,0:T(8,128)} %v_ref.1) | copy-start | bytes 884740
  2.9 12.1 %copy-start.2 = (s32[4]{0:T(128)S(1)}, s32[4]{0:T(128)}, u32[]{:S(2)}) copy-start(s32[4]{0:T(128)} %owner_ref.5) | copy-start | bytes 52
  2.9 12.1 %copy-start.4 = (f32[4,96]{1,0:T(4,128)S(1)}, f32[4,96]{1,0:T(4,128)}, u32[]{:S(2)}) copy-start(f32[4,96]{1,0:T(4,128)} %m_ref.1) | copy-start | bytes 4612
  2.9 12.1 %copy-start.5 = (f32[4,96]{1,0:T(4,128)S(1)}, f32[4,96]{1,0:T(4,128)}, u32[]{:S(2)}) copy-start(f32[4,96]{1,0:T(4,128)} %vv_ref.1) | copy-start | bytes 4612
  2.9 1.7 %collective-permute-start.1 = (f32[584,128]{1,0:T(8,128)S(1)}, f32[584,128]{1,0:T(8,128)S(1)}, u32[]{:S(2)}, u32[]{:S(2)}) collective-permute-start(f32[584,128]{1,0:T(8,128)S(1)} %get-tuple-element.49), channel_id=1, source_target_pairs={{0,1},{1,0},{2,3},{3,2},{4,5},{5,4},{6,7},{7,6},{8,9},{9,8},{10,11... | collective-permute-start | bytes 897032 | tf_op jit(solution)/shard_map/ppermute | solution.py:301
  4.7 10.3 %collective-permute-start.2 = (f32[584,128]{1,0:T(8,128)S(1)}, f32[584,128]{1,0:T(8,128)S(1)}, u32[]{:S(2)}, u32[]{:S(2)}) collective-permute-start(f32[584,128]{1,0:T(8,128)S(1)} %add.3), channel_id=1, source_target_pairs={{0,2},{1,3},{2,0},{3,1},{4,6},{5,7},{6,4},{7,5},{8,10},{9,11},{10,... | collective-permute-start | bytes 897032 | tf_op jit(solution)/shard_map/ppermute | solution.py:301
  7.6 1.6 %collective-permute-start = (f32[576,128]{1,0:T(8,128)S(1)}, f32[576,128]{1,0:T(8,128)S(1)}, u32[]{:S(2)}, u32[]{:S(2)}) collective-permute-start(f32[576,128]{1,0:T(8,128)S(1)} %get-tuple-element.47), channel_id=1, source_target_pairs={{0,1},{1,0},{2,3},{3,2},{4,5},{5,4},{6,7},{7,6},{8,9},{9,8},{10,11... | collective-permute-start | bytes 884744 | tf_op jit(solution)/shard_map/ppermute | solution.py:301
  16.7 26.5 %collective-permute-start.17 = (bf16[2,192,768]{2,1,0:T(8,128)(2,1)S(1)}, bf16[2,192,768]{2,1,0:T(8,128)(2,1)S(1)}, u32[]{:S(2)}, u32[]{:S(2)}) collective-permute-start(bf16[2,192,768]{2,1,0:T(8,128)(2,1)S(1)} %pad_maximum_fusion.own_ref), channel_id=1, source_target_pairs={{0,2},{1,3},{2,0},{3,1},{4,6},{5,7},{6,4},{7,5},{8,10},{9,11},{10,... | collective-permute-start | bytes 1769480 | tf_op jit(solution)/shard_map/ppermute | solution.py:301
  18.5 31.3 %collective-permute-start.16 = (bf16[2,192,768]{2,1,0:T(8,128)(2,1)S(1)}, bf16[2,192,768]{2,1,0:T(8,128)(2,1)S(1)}, u32[]{:S(2)}, u32[]{:S(2)}) collective-permute-start(bf16[2,192,768]{2,1,0:T(8,128)(2,1)S(1)} %pad_maximum_fusion.own_ref), channel_id=1, source_target_pairs={{0,1},{1,0},{2,3},{3,2},{4,5},{5,4},{6,7},{7,6},{8,9},{9,8},{10,11... | collective-permute-start | bytes 1769480 | tf_op jit(solution)/shard_map/ppermute | solution.py:301
  18.5 10.3 %collective-permute-start.3 = (f32[152,128]{1,0:T(8,128)S(1)}, f32[152,128]{1,0:T(8,128)S(1)}, u32[]{:S(2)}, u32[]{:S(2)}) collective-permute-start(f32[152,128]{1,0:T(8,128)S(1)} %get-tuple-element.59), channel_id=1, source_target_pairs={{0,4},{4,0},{8,12},{12,8},{16,20},{20,16},{24,28},{28,24},{1,5},{5... | collective-permute-start | bytes 233480 | tf_op jit(solution)/shard_map/ppermute | solution.py:301
  20.0 12.6 %collective-permute-start.4 = (f32[152,128]{1,0:T(8,128)S(1)}, f32[152,128]{1,0:T(8,128)S(1)}, u32[]{:S(2)}, u32[]{:S(2)}) collective-permute-start(f32[152,128]{1,0:T(8,128)S(1)} %get-tuple-element.60), channel_id=1, source_target_pairs={{0,8},{4,12},{8,0},{12,4},{16,24},{20,28},{24,16},{28,20},{1,9},{5... | collective-permute-start | bytes 233480 | tf_op jit(solution)/shard_map/ppermute | solution.py:301
  21.6 6.8 %collective-permute-start.9 = (f32[152,128]{1,0:T(8,128)S(1)}, f32[152,128]{1,0:T(8,128)S(1)}, u32[]{:S(2)}, u32[]{:S(2)}) collective-permute-start(f32[152,128]{1,0:T(8,128)S(1)} %get-tuple-element.62), channel_id=1, source_target_pairs={{0,16},{4,20},{8,24},{12,28},{16,0},{20,4},{24,8},{28,12},{1,17},{... | collective-permute-start | bytes 233480 | tf_op jit(solution)/shard_map/ppermute | solution.py:301
  28.4 7.1 %collective-permute-start.5 = (f32[152,128]{1,0:T(8,128)S(1)}, f32[152,128]{1,0:T(8,128)S(1)}, u32[]{:S(2)}, u32[]{:S(2)}) collective-permute-start(f32[152,128]{1,0:T(8,128)S(1)} %get-tuple-element.61), channel_id=1, source_target_pairs={{0,12},{4,8},{8,4},{12,0},{16,28},{20,24},{24,20},{28,16},{1,13},{... | collective-permute-start | bytes 233480 | tf_op jit(solution)/shard_map/ppermute | solution.py:301
  28.8 10.2 %collective-permute-start.10 = (f32[152,128]{1,0:T(8,128)S(1)}, f32[152,128]{1,0:T(8,128)S(1)}, u32[]{:S(2)}, u32[]{:S(2)}) collective-permute-start(f32[152,128]{1,0:T(8,128)S(1)} %get-tuple-element.63), channel_id=1, source_target_pairs={{0,20},{4,16},{8,28},{12,24},{16,4},{20,0},{24,12},{28,8},{1,21},{... | collective-permute-start | bytes 233480 | tf_op jit(solution)/shard_map/ppermute | solution.py:301
  32.6 7.0 %collective-permute-start.11 = (f32[152,128]{1,0:T(8,128)S(1)}, f32[152,128]{1,0:T(8,128)S(1)}, u32[]{:S(2)}, u32[]{:S(2)}) collective-permute-start(f32[152,128]{1,0:T(8,128)S(1)} %get-tuple-element.64), channel_id=1, source_target_pairs={{0,24},{4,28},{8,16},{12,20},{16,8},{20,12},{24,0},{28,4},{1,25},{... | collective-permute-start | bytes 233480 | tf_op jit(solution)/shard_map/ppermute | solution.py:301
  35.5 7.1 %collective-permute-start.12 = (f32[152,128]{1,0:T(8,128)S(1)}, f32[152,128]{1,0:T(8,128)S(1)}, u32[]{:S(2)}, u32[]{:S(2)}) collective-permute-start(f32[152,128]{1,0:T(8,128)S(1)} %get-tuple-element.65), channel_id=1, source_target_pairs={{0,28},{4,24},{8,20},{12,16},{16,12},{20,8},{24,4},{28,0},{1,29},{... | collective-permute-start | bytes 233480 | tf_op jit(solution)/shard_map/ppermute | solution.py:301
  39.0 7.4 %collective-permute-start.7 = (f32[608,128]{1,0:T(8,128)S(1)}, f32[608,128]{1,0:T(8,128)S(1)}, u32[]{:S(2)}, u32[]{:S(2)}) collective-permute-start(f32[608,128]{1,0:T(8,128)S(1)} %constant_dynamic-update-slice_fusion.refs_0_), channel_id=1, source_target_pairs={{0,2},{1,3},{2,0},{3,1},{4,6},{5,7},{6,4},{7,5},{8,10},{9,11},{10,... | collective-permute-start | bytes 933896 | tf_op jit(solution)/shard_map/ppermute | solution.py:301
  42.6 7.1 %collective-permute-start.14 = (f32[608,128]{1,0:T(8,128)S(1)}, f32[608,128]{1,0:T(8,128)S(1)}, u32[]{:S(2)}, u32[]{:S(2)}) collective-permute-start(f32[608,128]{1,0:T(8,128)S(1)} %constant_dynamic-update-slice_fusion.4.refs_4_), channel_id=1, source_target_pairs={{0,2},{1,3},{2,0},{3,1},{4,6},{5,7},{6,4},{7,5},{8,10},{9,11},{10,... | collective-permute-start | bytes 933896 | tf_op jit(solution)/shard_map/ppermute | solution.py:301
  43.2 7.1 %collective-permute-start.18 = (bf16[2,192,768]{2,1,0:T(8,128)(2,1)S(1)}, bf16[2,192,768]{2,1,0:T(8,128)(2,1)S(1)}, u32[]{:S(2)}, u32[]{:S(2)}) collective-permute-start(bf16[2,192,768]{2,1,0:T(8,128)(2,1)S(1)} %collective-permute-done.17.chip_ref), channel_id=1, source_target_pairs={{0,1},{1,0},{2,3},{3,2},{4,5},{5,4},{6,7},{7,6},{8,9},{9,8},{10,11... | collective-permute-start | bytes 1769480 | tf_op jit(solution)/shard_map/ppermute | solution.py:301
  43.2 7.2 %collective-permute-start.6 = (f32[608,128]{1,0:T(8,128)S(1)}, f32[608,128]{1,0:T(8,128)S(1)}, u32[]{:S(2)}, u32[]{:S(2)}) collective-permute-start(f32[608,128]{1,0:T(8,128)S(1)} %constant_dynamic-update-slice_fusion.refs_0_), channel_id=1, source_target_pairs={{0,1},{1,0},{2,3},{3,2},{4,5},{5,4},{6,7},{7,6},{8,9},{9,8},{10,11... | collective-permute-start | bytes 933896 | tf_op jit(solution)/shard_map/ppermute | solution.py:301
  46.4 4.0 %collective-permute-start.13 = (f32[608,128]{1,0:T(8,128)S(1)}, f32[608,128]{1,0:T(8,128)S(1)}, u32[]{:S(2)}, u32[]{:S(2)}) collective-permute-start(f32[608,128]{1,0:T(8,128)S(1)} %constant_dynamic-update-slice_fusion.4.refs_4_), channel_id=1, source_target_pairs={{0,1},{1,0},{2,3},{3,2},{4,5},{5,4},{6,7},{7,6},{8,9},{9,8},{10,11... | collective-permute-start | bytes 933896 | tf_op jit(solution)/shard_map/ppermute | solution.py:301
  49.8 1.6 %collective-permute-start.8 = (f32[608,128]{1,0:T(8,128)S(1)}, f32[608,128]{1,0:T(8,128)S(1)}, u32[]{:S(2)}, u32[]{:S(2)}) collective-permute-start(f32[608,128]{1,0:T(8,128)S(1)} %collective-permute-done.7.refs_2_), channel_id=1, source_target_pairs={{0,1},{1,0},{2,3},{3,2},{4,5},{5,4},{6,7},{7,6},{8,9},{9,8},{10,11... | collective-permute-start | bytes 933896 | tf_op jit(solution)/shard_map/ppermute | solution.py:301
  49.8 2.0 %collective-permute-start.15 = (f32[608,128]{1,0:T(8,128)S(1)}, f32[608,128]{1,0:T(8,128)S(1)}, u32[]{:S(2)}, u32[]{:S(2)}) collective-permute-start(f32[608,128]{1,0:T(8,128)S(1)} %collective-permute-done.14.refs_6_), channel_id=1, source_target_pairs={{0,1},{1,0},{2,3},{3,2},{4,5},{5,4},{6,7},{7,6},{8,9},{9,8},{10,11... | collective-permute-start | bytes 933896 | tf_op jit(solution)/shard_map/ppermute | solution.py:301
  51.8 16.7 %copy-start.6 = (f32[1,192,768]{2,1,0:T(8,128)S(1)}, f32[1,192,768]{2,1,0:T(8,128)}, u32[]{:S(2)}) copy-start(f32[1,192,768]{2,1,0:T(8,128)} %left_ref.1) | copy-start | bytes 1769476
  51.8 16.7 %copy-start.7 = (f32[1,192,768]{2,1,0:T(8,128)S(1)}, f32[1,192,768]{2,1,0:T(8,128)}, u32[]{:S(2)}) copy-start(f32[1,192,768]{2,1,0:T(8,128)} %right_ref.1) | copy-start | bytes 1769476
  57.3 7.1 %collective-permute-start.19 = (f32[144,128]{1,0:T(8,128)S(1)}, f32[144,128]{1,0:T(8,128)S(1)}, u32[]{:S(2)}, u32[]{:S(2)}) collective-permute-start(f32[144,128]{1,0:T(8,128)S(1)} %get-tuple-element.70), channel_id=1, source_target_pairs={{0,4},{4,0},{8,12},{12,8},{16,20},{20,16},{24,28},{28,24},{1,5},{5... | collective-permute-start | bytes 221192 | tf_op jit(solution)/shard_map/ppermute | solution.py:301
  58.6 8.0 %collective-permute-start.20 = (f32[144,128]{1,0:T(8,128)S(1)}, f32[144,128]{1,0:T(8,128)S(1)}, u32[]{:S(2)}, u32[]{:S(2)}) collective-permute-start(f32[144,128]{1,0:T(8,128)S(1)} %get-tuple-element.71), channel_id=1, source_target_pairs={{0,8},{4,12},{8,0},{12,4},{16,24},{20,28},{24,16},{28,20},{1,9},{5... | collective-permute-start | bytes 221192 | tf_op jit(solution)/shard_map/ppermute | solution.py:301
  60.1 12.3 %collective-permute-start.21 = (f32[144,128]{1,0:T(8,128)S(1)}, f32[144,128]{1,0:T(8,128)S(1)}, u32[]{:S(2)}, u32[]{:S(2)}) collective-permute-start(f32[144,128]{1,0:T(8,128)S(1)} %get-tuple-element.72), channel_id=1, source_target_pairs={{0,12},{4,8},{8,4},{12,0},{16,28},{20,24},{24,20},{28,16},{1,13},{... | collective-permute-start | bytes 221192 | tf_op jit(solution)/shard_map/ppermute | solution.py:301
  60.9 11.6 %collective-permute-start.22 = (f32[144,128]{1,0:T(8,128)S(1)}, f32[144,128]{1,0:T(8,128)S(1)}, u32[]{:S(2)}, u32[]{:S(2)}) collective-permute-start(f32[144,128]{1,0:T(8,128)S(1)} %get-tuple-element.73), channel_id=1, source_target_pairs={{0,16},{4,20},{8,24},{12,28},{16,0},{20,4},{24,8},{28,12},{1,17},{... | collective-permute-start | bytes 221192 | tf_op jit(solution)/shard_map/ppermute | solution.py:301
  63.1 11.8 %collective-permute-start.23 = (f32[144,128]{1,0:T(8,128)S(1)}, f32[144,128]{1,0:T(8,128)S(1)}, u32[]{:S(2)}, u32[]{:S(2)}) collective-permute-start(f32[144,128]{1,0:T(8,128)S(1)} %get-tuple-element.74), channel_id=1, source_target_pairs={{0,20},{4,16},{8,28},{12,24},{16,4},{20,0},{24,12},{28,8},{1,21},{... | collective-permute-start | bytes 221192 | tf_op jit(solution)/shard_map/ppermute | solution.py:301
  64.5 10.4 %collective-permute-start.24 = (f32[144,128]{1,0:T(8,128)S(1)}, f32[144,128]{1,0:T(8,128)S(1)}, u32[]{:S(2)}, u32[]{:S(2)}) collective-permute-start(f32[144,128]{1,0:T(8,128)S(1)} %get-tuple-element.75), channel_id=1, source_target_pairs={{0,24},{4,28},{8,16},{12,20},{16,8},{20,12},{24,0},{28,4},{1,25},{... | collective-permute-start | bytes 221192 | tf_op jit(solution)/shard_map/ppermute | solution.py:301
  66.6 8.3 %collective-permute-start.25 = (f32[144,128]{1,0:T(8,128)S(1)}, f32[144,128]{1,0:T(8,128)S(1)}, u32[]{:S(2)}, u32[]{:S(2)}) collective-permute-start(f32[144,128]{1,0:T(8,128)S(1)} %get-tuple-element.76), channel_id=1, source_target_pairs={{0,28},{4,24},{8,20},{12,16},{16,12},{20,8},{24,4},{28,0},{1,29},{... | collective-permute-start | bytes 221192 | tf_op jit(solution)/shard_map/ppermute | solution.py:301

commit v2 on v1

--- a/solution.py
+++ b/solution.py
@@ -17,6 +17,7 @@
 BIAS_TWO = 1.0 - BETA_TWO**STEP_COUNT
 HIGH = lax.Precision.HIGHEST
 LANES = 128
+BACK = (1, 2, 4, 5, 6, 7, 3, 0)
 EXTRA = 8
 F32 = jnp.float32
 BF16 = jnp.bfloat16
@@ -162,12 +163,21 @@
 
 
 def roots_kernel(own_ref, core_ref, chip_ref, both_ref, left_ref, right_ref):
-    _, t, _, _ = place()
-    rows = own_ref.shape[1]
-    for mask, ref in enumerate((own_ref, core_ref, chip_ref, both_ref)):
-        at = pl.ds(pl.multiple_of((t ^ mask) * rows, rows), rows)
-        left_ref[at, :] = ref[0]
-        right_ref[at, :] = ref[1]
+    _, t, chip, _ = place()
+    rows, size = own_ref.shape[1], left_ref.shape[0]
+    half = size // 2
+    here = pl.ds(pl.multiple_of(chip * half, half), half)
+    there = pl.ds(pl.multiple_of((1 - chip) * half, half), half)
+
+    def block(mask):
+        return pl.ds(pl.multiple_of((t ^ mask) * rows, rows), rows)
+
+    for n, ref in enumerate((left_ref, right_ref)):
+        ref[block(0), :] = own_ref[n]
+        ref[block(1), :] = core_ref[n]
+        ref[block(2), there] = chip_ref[n]
+        ref[block(3), there] = both_ref[n]
+        ref[there, here] = ref[here, there].T
 
 
 def halves(a):
@@ -175,75 +185,103 @@
     return high, (a - high.astype(F32)).astype(BF16)
 
 
-def owner_kernel(rows, shards, *refs):
-    pieces, refs = refs[:8], refs[8:]
-    left_ref, right_ref, refs = refs[0], refs[1], refs[2:]
-    outs, (gh_ref, gl_ref), (zh_ref, zl_ref, dir_ref) = refs[:shards], refs[shards : shards + 2], refs[shards + 2 :]
+def laid_out(mine, peer, i, rows, core):
+    packed = rows + rows // 2
+    base = i * (packed + EXTRA)
+    a, b = mine[base : base + packed], peer[base : base + packed]
+    extra = mine[base + packed : base + packed + EXTRA] + peer[base + packed : base + packed + EXTRA]
+    first, last = jnp.where(core == 0, a, b), jnp.where(core == 0, b, a)
+    fs, ls = first[rows:], last[rows:]
+    low = low_lanes(rows // 2)
+    mid = jnp.concatenate([jnp.where(low, fs, swap_halves(ls)), jnp.where(low, swap_halves(fs), ls)], axis=0)
+    return (first[:rows], mid, last[:rows]), extra
+
+
+def product(a, b):
+    return jnp.dot(a, b, preferred_element_type=F32)
+
+
+def near_kernel(
+    rows, shards, mine_ref, peer_ref, chip_ref, both_ref, far_ref, far_peer_ref, left_ref, right_ref,
+    ah_ref, al_ref, bh_ref, bl_ref, z_ref, dir_ref, adam_ref, zh_ref, zl_ref
+):
     shard, _, chip, core = place()
-    packed = rows + rows // 2
-    half = rows // 2
     group = shards // 2
-    low = low_lanes(half)
+    half = group * rows
     adam = jnp.zeros((EXTRA, LANES), F32)
-    for g in range(2):
-        own, other = pieces[4 * g : 4 * g + 2], pieces[4 * g + 2 : 4 * g + 4]
-        for i in range(group):
-            to = pl.ds(pl.multiple_of((shard ^ (g * group + i)) * rows, rows), rows)
-            base = i * (packed + EXTRA)
-            for x, (mine, peer) in ((chip, own), (1 - chip, other)):
-                a, b = mine[base : base + packed], peer[base : base + packed]
-                adam += mine[base + packed : base + packed + EXTRA]
-                adam += peer[base + packed : base + packed + EXTRA]
-                first, last = jnp.where(core == 0, a, b), jnp.where(core == 0, b, a)
-                fs, ls = first[rows:], last[rows:]
-                mid = jnp.concatenate(
-                    [
-                        jnp.where(low, fs, swap_halves(ls)),
-                        jnp.where(low, swap_halves(fs), ls),
-                    ],
-                    axis=0,
-                )
-                for n, tile in enumerate((first[:rows], mid, last[:rows])):
-                    gh_ref[to, lane_tile(3 * x + n)], gl_ref[to, lane_tile(3 * x + n)] = halves(tile)
-    size = gh_ref.shape[0]
-    step = 256
-
-    def right(i, carry):
-        at = pl.ds(pl.multiple_of(i * step, step), step)
-        z = jnp.dot(gh_ref[at, :], right_ref[...], preferred_element_type=F32)
-        z += jnp.dot(gl_ref[at, :], right_ref[...], preferred_element_type=F32)
-        zh_ref[at, :], zl_ref[at, :] = halves(z)
-        return carry
-
-    lax.fori_loop(0, size // step, right, 0)
-
-    def left(i, total):
-        at = pl.ds(pl.multiple_of(i * step, step), step)
-        d = jnp.dot(left_ref[at, :], zh_ref[...], preferred_element_type=F32)
-        d += jnp.dot(left_ref[at, :], zl_ref[...], preferred_element_type=F32)
-        dir_ref[at, :] = d
-        return total + jnp.sum((d * d).reshape(-1, 8, size), axis=0)
-
-    squares = lax.fori_loop(0, size // step, left, jnp.zeros((8, size), F32))
+    for i in range(group):
+        to = pl.ds(pl.multiple_of((lax.rem(shard, group) ^ i) * rows, rows), rows)
+        for x, mine, peer in ((chip, mine_ref, peer_ref), (1 - chip, chip_ref, both_ref)):
+            parts, extra = laid_out(mine, peer, i, rows, core)
+            adam += extra
+            for n, tile in enumerate(parts):
+                ah_ref[to, lane_tile(3 * x + n)], al_ref[to, lane_tile(3 * x + n)] = halves(tile)
+        parts, extra = laid_out(far_ref, far_peer_ref, i, rows, core)
+        adam += extra
+        for n, tile in enumerate(parts):
+            bh_ref[to, n * LANES : (n + 1) * LANES], bl_ref[to, n * LANES : (n + 1) * LANES] = halves(tile)
+    adam_ref[...] = adam
+    z = product(ah_ref[...], right_ref[...]) + product(al_ref[...], right_ref[...])
+    zh_ref[...], zl_ref[...] = halves(z)
+    here = pl.ds(pl.multiple_of(chip * half, half), half)
+    z_ref[...] = product(bh_ref[...], right_ref[here, :]) + product(bl_ref[...], right_ref[here, :])
+    near = pl.ds(pl.multiple_of(shard // group * half, half), half)
+    for n in range(2):
+        at = slice(n * half, (n + 1) * half)
+        dir_ref[at] = product(left_ref[at, near], zh_ref[...]) + product(left_ref[at, near], zl_ref[...])
+
+
+def owner_kernel(rows, shards, chip_ref, both_ref, z_ref, part_ref, adam_ref, left_ref, right_ref, *refs):
+    (bh_ref, bl_ref), outs, (zh_ref, zl_ref, dir_ref) = refs[:2], refs[2 : shards + 2], refs[shards + 2 :]
+    shard, _, chip, core = place()
+    group = shards // 2
+    half = group * rows
+    adam = adam_ref[...]
+    for i in range(group):
+        to = pl.ds(pl.multiple_of((lax.rem(shard, group) ^ i) * rows, rows), rows)
+        parts, extra = laid_out(chip_ref, both_ref, i, rows, core)
+        adam += extra
+        for n, tile in enumerate(parts):
+            bh_ref[to, n * LANES : (n + 1) * LANES], bl_ref[to, n * LANES : (n + 1) * LANES] = halves(tile)
+    there = pl.ds(pl.multiple_of((1 - chip) * half, half), half)
+    z = z_ref[...] + product(bh_ref[...], right_ref[there, :]) + product(bl_ref[...], right_ref[there, :])
+    zh_ref[...], zl_ref[...] = halves(z)
+    far = pl.ds(pl.multiple_of((1 - shard // group) * half, half), half)
+    squares = jnp.zeros((8, 2 * half), F32)
+    for n in range(2):
+        at = slice(n * half, (n + 1) * half)
+        d = part_ref[at] + product(left_ref[at, far], zh_ref[...]) + product(left_ref[at, far], zl_ref[...])
+        dir_ref[at] = d
+        squares += jnp.sum((d * d).reshape(-1, 8, 2 * half), axis=0)
 
     def whole(a):
         return jnp.sum(jnp.sum(a, axis=1, keepdims=True), axis=0, keepdims=True)
 
     graft = jnp.sqrt(whole(adam)) / (jnp.sqrt(whole(squares)) + NORM_EPS)
-    for j in range(shards):
+    for j, out in zip(BACK, outs):
         at = pl.ds(pl.multiple_of((shard ^ j) * rows, rows), rows)
-        outs[j][:rows] = graft * dir_ref[at, lane_tile(3 * chip + 2 * core)]
-        outs[j][rows:] = graft * fold(dir_ref[at, lane_tile(3 * chip + 1)], core)
-
-
-def stats_kernel(tiles, owner_ref, gh_ref, gl_ref, left_ref, right_ref, nl_ref, nr_ref):
+        out[:rows] = graft * dir_ref[at, lane_tile(3 * chip + 2 * core)]
+        out[rows:] = graft * fold(dir_ref[at, lane_tile(3 * chip + 1)], core)
+
+
+def stats_kernel(tiles, shards, owner_ref, ah_ref, al_ref, bh_ref, bl_ref, ch_ref, cl_ref, left_ref, right_ref, nl_ref, nr_ref, gh_ref, gl_ref):
     shard, t, chip, core = place()
     rows = left_ref.shape[1]
+    half = ah_ref.shape[0]
+    side = shard // (shards // 2)
+
+    def part(index):
+        return pl.ds(pl.multiple_of(index * half, half), half)
+
+    for ref, a, b, c in ((gh_ref, ah_ref, bh_ref, ch_ref), (gl_ref, al_ref, bl_ref, cl_ref)):
+        ref[part(side), :] = a[...]
+        ref[part(1 - side), part(chip)] = b[...]
+        ref[part(1 - side), part(1 - chip)] = c[...]
     held = owner_ref[0] == shard
     for i in range(1, tiles):
         held = jnp.logical_or(held, owner_ref[i] == shard)
 
-    def product(high, low, dims):
+    def three(high, low, dims):
         dot = functools.partial(lax.dot_general, dimension_numbers=(dims, ((), ())), preferred_element_type=F32)
         return dot(high, gh_ref[...]) + dot(high, gl_ref[...]) + dot(low, gh_ref[...])
 
@@ -251,10 +289,10 @@
         return STAT_DECAY * old + (1.0 - STAT_DECAY) * jnp.where(held, new, 0.0)
 
     at = pl.ds(pl.multiple_of(t * rows, rows), rows)
-    nl_ref[0] = refreshed(left_ref[0], product(gh_ref[at, :], gl_ref[at, :], ((1,), (1,))))
+    nl_ref[0] = refreshed(left_ref[0], three(gh_ref[at, :], gl_ref[at, :], ((1,), (1,))))
     end, mid = lane_tile(3 * chip + 2 * core), lane_tile(3 * chip + 1)
-    ends = product(gh_ref[:, end], gl_ref[:, end], ((0,), (0,)))
-    mids = product(gh_ref[:, mid], gl_ref[:, mid], ((0,), (0,)))
+    ends = three(gh_ref[:, end], gl_ref[:, end], ((0,), (0,)))
+    mids = three(gh_ref[:, mid], gl_ref[:, mid], ((0,), (0,)))
     half = LANES // 2
 
     @pl.when(core == 0)
@@ -272,11 +310,11 @@
     blocks, out_ref = refs[:shards], refs[shards]
     shard, _, _, core = place()
     for k in range(tiles):
-        for j in range(shards):
+        for j, block in zip(BACK, blocks):
 
             @pl.when((shard ^ j) == owner_ref[k])
-            def _(k=k, j=j):
-                out_ref[k, :, :LANES], out_ref[k, :, LANES:] = unfold(blocks[j][...], rows, core)
+            def _(k=k, block=block):
+                out_ref[k, :, :LANES], out_ref[k, :, LANES:] = unfold(block[...], rows, core)
 
 
 def shape(dims, dtype=F32):
@@ -317,6 +355,11 @@
     u = kf + swap(sf, "tensor", 1)
     rn = swap(sn, "tensor", 1)
     r = swap(u, "tensor", 2)
+    roots = jnp.concatenate([left_root, right_root], axis=0)
+    quadrant = lax.axis_index("tensor") // 2 * (size // 2)
+    crossing = lax.dynamic_slice_in_dim(roots, quadrant, size // 2, 2)
+    roots_core = swap(roots, "tensor", 1)
+    r, roots, roots_core, crossing = lax.optimization_barrier((r, roots, roots_core, crossing))
     vec = shape((tiles, rows))
     res = kernel_call(
         functools.partial(adam_kernel, rows, tiles, shards),
@@ -327,33 +370,42 @@
     )
     outgoing, (new_adam_v, new_vec_m, new_vec_v, vec_step) = res[:shards], res[shards:]
 
-    roots = jnp.concatenate([left_root, right_root], axis=0)
-    roots, outgoing = lax.optimization_barrier((roots, outgoing))
     arrived = [outgoing[0]] + [swap(outgoing[j], "shard", j) for j in range(1, shards)]
-    roots_chip, roots_core = swap(roots, "tensor", 2), swap(roots, "tensor", 1)
+    roots_chip = swap(crossing, "tensor", 2)
     full = shape((size, size), BF16)
     left_full, right_full = kernel_call(
-        roots_kernel, (full, full), (roots, roots_core, roots_chip, swap(roots_chip, "tensor", 1))
-    )
-    pieces = []
-    for part in (arrived[: shards // 2], arrived[shards // 2 :]):
-        mine = jnp.concatenate(part, axis=0)
-        across = swap(mine, "tensor", 2)
-        pieces += [mine, swap(mine, "tensor", 1), across, swap(across, "tensor", 1)]
-    res = kernel_call(
+        roots_kernel, (full, full), (roots, roots_core, roots_chip, swap(roots_chip, "tensor", 1)), mib=24
+    )
+    near = jnp.concatenate(arrived[: shards // 2], axis=0)
+    far = jnp.concatenate(arrived[shards // 2 :], axis=0)
+    near_across = swap(near, "tensor", 2)
+    near = near, swap(near, "tensor", 1), near_across, swap(near_across, "tensor", 1)
+    far_across = swap(far, "tensor", 2)
+    half = size // 2
+    tall, square = shape((half, size), BF16), shape((half, half), BF16)
+    ah, al, bh, bl, z, part, adam = kernel_call(
+        functools.partial(near_kernel, rows, shards),
+        (tall, tall, square, square, shape((half, size)), shape((size, size)), shape((EXTRA, LANES))),
+        (*near, far, swap(far, "tensor", 1), left_full, right_full),
+        (pltpu.VMEM((half, size), BF16),) * 2,
+        flops=5 * size**3,
+        mib=32,
+    )
+    far_across, adam = lax.optimization_barrier((far_across, adam))
+    ch, cl, *ready = kernel_call(
         functools.partial(owner_kernel, rows, shards),
-        (shape((packed, LANES)),) * shards + (full, full),
-        (*pieces, left_full, right_full),
-        (pltpu.VMEM((size, size), BF16), pltpu.VMEM((size, size), BF16), pltpu.VMEM((size, size), F32)),
-        flops=8 * size**3,
+        (square, square) + (shape((packed, LANES)),) * shards,
+        (far_across, swap(far_across, "tensor", 1), z, part, adam, left_full, right_full),
+        (pltpu.VMEM((half, size), BF16),) * 2 + (pltpu.VMEM((size, size), F32),),
+        flops=3 * size**3,
         mib=32,
     )
-    ready, (high, low) = res[:shards], res[shards:]
-    back = [ready[0]] + [swap(ready[j], "shard", j) for j in range(1, shards)]
+    back = [swap(block, "shard", j) if j else block for j, block in zip(BACK, ready)]
     new_left, new_right = kernel_call(
-        functools.partial(stats_kernel, tiles),
+        functools.partial(stats_kernel, tiles, shards),
         (shape(left_stat.shape), shape(right_stat.shape)),
-        (owner, high, low, left_stat, right_stat),
+        (owner, ah, al, bh, bl, ch, cl, left_stat, right_stat),
+        (pltpu.VMEM((size, size), BF16),) * 2,
         smem=1,
         flops=12 * cols * size**2,
         mib=32,

time: 77.1 us -> 72.8 us (0.944)
  waiting for transfers between devices: 28.4 us -> 23.1 us
    ppermute x26, waiting for transfers between devices: 28.4 us -> 23.1 us  [swap(): lax.ppermute(a, axis, [(i, i ^ mask) for i in range(lax.axis_size(axis))])]
    pallas_call x6 -> x7, Pallas kernels: 13.4 us -> 14 us  [kernel_call(): pl.pallas_call(body, out_shape=outs, in_specs=[pl.BlockSpec(memory_space=...]
    unnamed x26 -> x27, local copies, waits for them, and re-layouts: 2.02 us -> 2.25 us
  transfers between devices with their start and end apart: 26 -> 26, of which waited for: 12 -> 10; matrix products, arithmetic and copies ran while one was open for 0% -> 0% of each run, Pallas kernels for 5% -> 13%
where the time goes in v2:
time: 72.8 us; the launch traced here: 72.6 us
  starting transfers between devices  32.3 us (44%)
  waiting for transfers between devices  23.1 us (32%)
  Pallas kernels  14 us (19%)
  local copies, waits for them, and re-layouts  2.32 us (3%)
  between operations  0.84 us (1%)
    ppermute x26, starting transfers between devices, swap(): lax.ppermute(a, axis, [(i, i ^ mask) for i in range(lax.axis_size(axis))])  32.3 us
    ppermute x26, waiting for transfers between devices, swap(): lax.ppermute(a, axis, [(i, i ^ mask) for i in range(lax.axis_size(axis))])  23.1 us
    pallas_call x7, Pallas kernels, kernel_call(): pl.pallas_call(body, out_shape=outs, in_specs=[pl.BlockSpec(memory_space=...  14 us
    unnamed x27, local copies, waits for them, and re-layouts  2.25 us
  transfers between devices with their start and end apart: 26, of which 10 were waited for; matrix products, arithmetic and copies ran while one was open for 0% of the time, Pallas kernels for 13%

profile of v2, /device:TPU:0, one launch (start us, length us, event | category | flops | bytes accessed | tf_op | source)
XLA Modules:
  0.0 72.6 jit_solution(2497177672274359012)
XLA Ops:
  0.6 1.3 %copy-done = f32[1,4,96,768]{3,2,1,0:T(8,128)S(1)} copy-done((f32[1,4,96,768]{3,2,1,0:T(8,128)S(1)}, f32[1,4,96,768]{3,2,1,0:T(8,128)}, u32[]{:S(2)}) %copy-start) | copy-done | bytes 1179672
  1.9 0.7 copy-done.3
  2.6 0.3 shard_map.153
  2.9 0.5 collective-permute-start.1
  3.4 0.2 copy-done.8
  3.6 0.1 copy-done.9
  3.7 0.5 collective-permute-start.3
  4.2 0.4 collective-permute-done.1
  4.6 2.9 %collective-permute-start.2 = (f32[584,128]{1,0:T(8,128)S(1)}, f32[584,128]{1,0:T(8,128)S(1)}, u32[]{:S(2)}, u32[]{:S(2)}) collective-permute-start(f32[584,128]{1,0:T(8,128)S(1)} %add.7), channel_id=1, source_target_pairs={{0,2},{1,3},{2,0},{3,1},{4,6},{5,7},{6,4},{7,5},{8,10},{9,11},{10,... | collective-permute-start | bytes 897032 | tf_op jit(solution)/shard_map/ppermute | solution.py:339
  7.6 7.3 %collective-permute-done.2.r_ref = f32[584,128]{1,0:T(8,128)S(1)} collective-permute-done((f32[584,128]{1,0:T(8,128)S(1)}, f32[584,128]{1,0:T(8,128)S(1)}, u32[]{:S(2)}, u32[]{:S(2)}) %collective-permute-start.2) | collective-permute-done | bytes 299040 | tf_op jit(solution)/shard_map/ppermute | solution.py:339
  15.0 1.7 %collective-permute-start.16 = (bf16[2,192,384]{2,1,0:T(8,128)(2,1)S(1)}, bf16[2,192,384]{2,1,0:T(8,128)(2,1)S(1)}, u32[]{:S(2)}, u32[]{:S(2)}) collective-permute-start(bf16[2,192,384]{2,1,0:T(8,128)(2,1)S(1)} %constant_dynamic-slice_fusion), channel_id=1, source_target_pairs={{0,2},{1,3},{2,0},{3,1},{4,6},{5,7},{6,4},{7,5},{8,10},{9,11},{10,... | collective-permute-start | bytes 884744 | tf_op jit(solution)/shard_map/ppermute | solution.py:339
  16.7 1.7 %shard_map.154 = (f32[152,128]{1,0:T(8,128)S(1)}, f32[152,128]{1,0:T(8,128)S(1)}, f32[152,128]{1,0:T(8,128)S(1)}, f32[152,128]{1,0:T(8,128)S(1)}, f32[152,128]{1...) custom-call(s32[4]{0:T(128)S(1)} %copy-done.2, ...), custom_call_target="tpu_custom_call" | custom-call | bytes 2113040 | tf_op jit(solution)/shard_map/pallas_call | solution.py:327
  18.4 1.5 %collective-permute-start.9 = (f32[152,128]{1,0:T(8,128)S(1)}, f32[152,128]{1,0:T(8,128)S(1)}, u32[]{:S(2)}, u32[]{:S(2)}) collective-permute-start(f32[152,128]{1,0:T(8,128)S(1)} %get-tuple-element.60), channel_id=1, source_target_pairs={{0,4},{4,0},{8,12},{12,8},{16,20},{20,16},{24,28},{28,24},{1,5},{5... | collective-permute-start | bytes 233480 | tf_op jit(solution)/shard_map/ppermute | solution.py:339
  20.0 1.6 %collective-permute-start.10 = (f32[152,128]{1,0:T(8,128)S(1)}, f32[152,128]{1,0:T(8,128)S(1)}, u32[]{:S(2)}, u32[]{:S(2)}) collective-permute-start(f32[152,128]{1,0:T(8,128)S(1)} %get-tuple-element.61), channel_id=1, source_target_pairs={{0,8},{4,12},{8,0},{12,4},{16,24},{20,28},{24,16},{28,20},{1,9},{5... | collective-permute-start | bytes 233480 | tf_op jit(solution)/shard_map/ppermute | solution.py:339
  21.5 0.4 collective-permute-start.11
  21.9 2.6 %collective-permute-start.4 = (f32[152,128]{1,0:T(8,128)S(1)}, f32[152,128]{1,0:T(8,128)S(1)}, u32[]{:S(2)}, u32[]{:S(2)}) collective-permute-start(f32[152,128]{1,0:T(8,128)S(1)} %get-tuple-element.55), channel_id=1, source_target_pairs={{0,16},{4,20},{8,24},{12,28},{16,0},{20,4},{24,8},{28,12},{1,17},{... | collective-permute-start | bytes 233480 | tf_op jit(solution)/shard_map/ppermute | solution.py:339
  24.5 2.7 %collective-permute-start.5 = (f32[152,128]{1,0:T(8,128)S(1)}, f32[152,128]{1,0:T(8,128)S(1)}, u32[]{:S(2)}, u32[]{:S(2)}) collective-permute-start(f32[152,128]{1,0:T(8,128)S(1)} %get-tuple-element.56), channel_id=1, source_target_pairs={{0,20},{4,16},{8,28},{12,24},{16,4},{20,0},{24,12},{28,8},{1,21},{... | collective-permute-start | bytes 233480 | tf_op jit(solution)/shard_map/ppermute | solution.py:339
  27.2 0.0 collective-permute-done.10
  27.2 2.3 %collective-permute-start.6 = (f32[152,128]{1,0:T(8,128)S(1)}, f32[152,128]{1,0:T(8,128)S(1)}, u32[]{:S(2)}, u32[]{:S(2)}) collective-permute-start(f32[152,128]{1,0:T(8,128)S(1)} %get-tuple-element.57), channel_id=1, source_target_pairs={{0,24},{4,28},{8,16},{12,20},{16,8},{20,12},{24,0},{28,4},{1,25},{... | collective-permute-start | bytes 233480 | tf_op jit(solution)/shard_map/ppermute | solution.py:339
  29.6 0.0 collective-permute-done.11
  29.6 1.4 %collective-permute-start.7 = (f32[152,128]{1,0:T(8,128)S(1)}, f32[152,128]{1,0:T(8,128)S(1)}, u32[]{:S(2)}, u32[]{:S(2)}) collective-permute-start(f32[152,128]{1,0:T(8,128)S(1)} %get-tuple-element.58), channel_id=1, source_target_pairs={{0,28},{4,24},{8,20},{12,16},{16,12},{20,8},{24,4},{28,0},{1,29},{... | collective-permute-start | bytes 233480 | tf_op jit(solution)/shard_map/ppermute | solution.py:339
  31.0 0.0 collective-permute-done.4
  31.0 0.6 collective-permute-start.13
  31.6 5.6 %collective-permute-done.5 = f32[152,128]{1,0:T(8,128)S(1)} collective-permute-done((f32[152,128]{1,0:T(8,128)S(1)}, f32[152,128]{1,0:T(8,128)S(1)}, u32[]{:S(2)}, u32[]{:S(2)}) %collective-permute-start.5) | collective-permute-done | bytes 77856 | tf_op jit(solution)/shard_map/ppermute | solution.py:339
  37.2 0.0 collective-permute-start.12
  37.2 0.0 collective-permute-done.6
  37.2 0.0 collective-permute-done.7
  37.2 0.6 collective-permute-start.15
  37.8 0.1 collective-permute-done.13.chip_ref
  38.0 0.0 collective-permute-start.14
  38.0 0.5 collective-permute-start.17
  38.5 0.5 collective-permute-start.8
  39.0 1.1 %collective-permute-done.17.both_ref = bf16[2,192,384]{2,1,0:T(8,128)(2,1)S(1)} collective-permute-done((bf16[2,192,384]{2,1,0:T(8,128)(2,1)S(1)}, bf16[2,192,384]{2,1,0:T(8,128)(2,1)S(1)}, u32[]{:S(2)}, u32[]{:S(2)}) %collective-permute-start.17) | collective-permute-done | bytes 294944 | tf_op jit(solution)/shard_map/ppermute | solution.py:339
  40.1 0.3 shard_map.155
  40.4 3.3 %shard_map.156 = (bf16[384,768]{1,0:T(8,128)(2,1)S(1)}, bf16[384,768]{1,0:T(8,128)(2,1)S(1)}, bf16[384,384]{1,0:T(8,128)(2,1)S(1)}, bf16[384,384]{1,0:T(8,128)(2...) custom-call(f32[608,128]{1,0:T(8,128)S(1)} %constant_dynamic-update-slice_fusion.6.mine_ref, ...), custom_call_target="tpu_custom_call" | custom-call | flops 2264924160 | bytes 9539584 | tf_op jit(solution)/shard_map/pallas_call | solution.py:327
  43.7 4.0 %collective-permute-done.8.chip_ref = f32[608,128]{1,0:T(8,128)S(1)} collective-permute-done((f32[608,128]{1,0:T(8,128)S(1)}, f32[608,128]{1,0:T(8,128)S(1)}, u32[]{:S(2)}, u32[]{:S(2)}) %collective-permute-start.8) | collective-permute-done | bytes 311328 | tf_op jit(solution)/shard_map/ppermute | solution.py:339
  47.7 1.6 %collective-permute-done.18.both_ref = f32[608,128]{1,0:T(8,128)S(1)} collective-permute-done((f32[608,128]{1,0:T(8,128)S(1)}, f32[608,128]{1,0:T(8,128)S(1)}, u32[]{:S(2)}, u32[]{:S(2)}) %collective-permute-start.18) | collective-permute-done | bytes 311328 | tf_op jit(solution)/shard_map/ppermute | solution.py:339
  49.4 2.5 %shard_map.157 = (bf16[384,384]{1,0:T(8,128)(2,1)S(1)}, bf16[384,384]{1,0:T(8,128)(2,1)S(1)}, f32[144,128]{1,0:T(8,128)S(1)}, f32[144,128]{1,0:T(8,128)S(1)}, f3...) custom-call(f32[608,128]{1,0:T(8,128)S(1)} %collective-permute-done., ...), custom_call_target="tpu_custom_call" | custom-call | flops 1358954496 | bytes 7704576 | tf_op jit(solution)/shard_map/pallas_call | solution.py:327
  51.9 4.2 %collective-permute-start.19 = (f32[144,128]{1,0:T(8,128)S(1)}, f32[144,128]{1,0:T(8,128)S(1)}, u32[]{:S(2)}, u32[]{:S(2)}) collective-permute-start(f32[144,128]{1,0:T(8,128)S(1)} %get-tuple-element.73), channel_id=1, source_target_pairs={{0,4},{4,0},{8,12},{12,8},{16,20},{20,16},{24,28},{28,24},{1,5},{5... | collective-permute-start | bytes 221192 | tf_op jit(solution)/shard_map/ppermute | solution.py:339
  56.1 2.6 %collective-permute-start.21 = (f32[144,128]{1,0:T(8,128)S(1)}, f32[144,128]{1,0:T(8,128)S(1)}, u32[]{:S(2)}, u32[]{:S(2)}) collective-permute-start(f32[144,128]{1,0:T(8,128)S(1)} %get-tuple-element.75), channel_id=1, source_target_pairs={{0,16},{4,20},{8,24},{12,28},{16,0},{20,4},{24,8},{28,12},{1,17},{... | collective-permute-start | bytes 221192 | tf_op jit(solution)/shard_map/ppermute | solution.py:339
  58.7 0.3 collective-permute-start.22
  59.1 2.4 %collective-permute-start.23 = (f32[144,128]{1,0:T(8,128)S(1)}, f32[144,128]{1,0:T(8,128)S(1)}, u32[]{:S(2)}, u32[]{:S(2)}) collective-permute-start(f32[144,128]{1,0:T(8,128)S(1)} %get-tuple-element.77), channel_id=1, source_target_pairs={{0,24},{4,28},{8,16},{12,20},{16,8},{20,12},{24,0},{28,4},{1,25},{... | collective-permute-start | bytes 221192 | tf_op jit(solution)/shard_map/ppermute | solution.py:339
  61.4 2.4 %collective-permute-start.24 = (f32[144,128]{1,0:T(8,128)S(1)}, f32[144,128]{1,0:T(8,128)S(1)}, u32[]{:S(2)}, u32[]{:S(2)}) collective-permute-start(f32[144,128]{1,0:T(8,128)S(1)} %get-tuple-element.78), channel_id=1, source_target_pairs={{0,28},{4,24},{8,20},{12,16},{16,12},{20,8},{24,4},{28,0},{1,29},{... | collective-permute-start | bytes 221192 | tf_op jit(solution)/shard_map/ppermute | solution.py:339
  63.8 4.1 %shard_map.159 = (f32[1,192,768]{2,1,0:T(8,128)}, f32[1,192,768]{2,1,0:T(8,128)}) custom-call(s32[4]{0:T(128)S(1)} %copy-done.2, bf16[384,768]{1,0:T(8,128)(2,1)S(1)} %get-tuple-element.82.ah_ref, bf16[384,768]{1,0:T(8,128)(2,1)S(1)} %get-tuple-element.83.al_ref, bf16[384,384]{1,0:T(8,128)(2,1)S(1)} %get-tuple-element.84.bh_ref, ...), custom_call_target="tpu_custom_call" | custom-call | flops 1358954496 | bytes 4718608 | tf_op jit(solution)/shard_map/pallas_call | solution.py:327
  67.9 0.5 collective-permute-done.21.refs_2_
  68.4 1.1 %collective-permute-done.22.refs_3_ = f32[144,128]{1,0:T(8,128)S(1)} collective-permute-done((f32[144,128]{1,0:T(8,128)S(1)}, f32[144,128]{1,0:T(8,128)S(1)}, u32[]{:S(2)}, u32[]{:S(2)}) %collective-permute-start.22) | collective-permute-done | bytes 73760 | tf_op jit(solution)/shard_map/ppermute | solution.py:339
  69.5 1.2 %collective-permute-done.25.refs_6_ = f32[144,128]{1,0:T(8,128)S(1)} collective-permute-done((f32[144,128]{1,0:T(8,128)S(1)}, f32[144,128]{1,0:T(8,128)S(1)}, u32[]{:S(2)}, u32[]{:S(2)}) %collective-permute-start.25) | collective-permute-done | bytes 73760 | tf_op jit(solution)/shard_map/ppermute | solution.py:339
  70.8 1.9 %shard_map.158 = f32[4,96,192]{2,1,0:T(8,128)} custom-call(s32[4]{0:T(128)S(1)} %copy-done.2, f32[144,128]{1,0:T(8,128)S(1)} %collective-permute-done.19.refs_0_, f32[144,128]{1,0:T(8,128)S(1)} %collective-permute-done.20.refs_1_, f32[144,128]{1,0:T(8,128)S(1)} %collective-permute-done.21.refs_2_, f32[144,128]{1,0:T(8,128)S(1)} %collective-permute-done.22.refs_3_, ...), custom_call_target="tpu_custom_call" | custom-call | bytes 884752 | tf_op jit(solution)/shard_map/pallas_call | solution.py:327
  (44 shorter events, 0.2 us)
Async XLA Ops:
  0.6 1.3 %copy-start = (f32[1,4,96,768]{3,2,1,0:T(8,128)S(1)}, f32[1,4,96,768]{3,2,1,0:T(8,128)}, u32[]{:S(2)}) copy-start(f32[1,4,96,768]{3,2,1,0:T(8,128)} %g_ref.1) | copy-start | bytes 3538948
  1.9 0.7 copy-start.3
  2.6 1.0 %copy-start.8 = (bf16[1,192,768]{2,1,0:T(8,128)(2,1)S(1)}, bf16[1,192,768]{2,1,0:T(8,128)(2,1)}, u32[]{:S(2)}) copy-start(bf16[1,192,768]{2,1,0:T(8,128)(2,1)} %param.14) | copy-start | bytes 884740
  2.6 1.0 %copy-start.9 = (bf16[1,192,768]{2,1,0:T(8,128)(2,1)S(1)}, bf16[1,192,768]{2,1,0:T(8,128)(2,1)}, u32[]{:S(2)}) copy-start(bf16[1,192,768]{2,1,0:T(8,128)(2,1)} %param.15) | copy-start | bytes 884740
  2.9 1.7 %collective-permute-start.1 = (f32[584,128]{1,0:T(8,128)S(1)}, f32[584,128]{1,0:T(8,128)S(1)}, u32[]{:S(2)}, u32[]{:S(2)}) collective-permute-start(f32[584,128]{1,0:T(8,128)S(1)} %get-tuple-element.53), channel_id=1, source_target_pairs={{0,1},{1,0},{2,3},{3,2},{4,5},{5,4},{6,7},{7,6},{8,9},{9,8},{10,11... | collective-permute-start | bytes 897032 | tf_op jit(solution)/shard_map/ppermute | solution.py:339
  3.6 13.1 %copy-start.1 = (f32[4,96,192]{2,1,0:T(8,128)S(1)}, f32[4,96,192]{2,1,0:T(8,128)}, u32[]{:S(2)}) copy-start(f32[4,96,192]{2,1,0:T(8,128)} %v_ref.1) | copy-start | bytes 884740
  3.6 13.1 %copy-start.2 = (s32[4]{0:T(128)S(1)}, s32[4]{0:T(128)}, u32[]{:S(2)}) copy-start(s32[4]{0:T(128)} %owner_ref.5) | copy-start | bytes 52
  3.6 13.1 %copy-start.4 = (f32[4,96]{1,0:T(4,128)S(1)}, f32[4,96]{1,0:T(4,128)}, u32[]{:S(2)}) copy-start(f32[4,96]{1,0:T(4,128)} %m_ref.1) | copy-start | bytes 4612
  3.6 13.1 %copy-start.5 = (f32[4,96]{1,0:T(4,128)S(1)}, f32[4,96]{1,0:T(4,128)}, u32[]{:S(2)}) copy-start(f32[4,96]{1,0:T(4,128)} %vv_ref.1) | copy-start | bytes 4612
  3.7 3.9 %collective-permute-start.3 = (bf16[2,192,768]{2,1,0:T(8,128)(2,1)S(1)}, bf16[2,192,768]{2,1,0:T(8,128)(2,1)S(1)}, u32[]{:S(2)}, u32[]{:S(2)}) collective-permute-start(bf16[2,192,768]{2,1,0:T(8,128)(2,1)S(1)} %constant_dynamic-update-slice_fusion.own_ref), channel_id=1, source_target_pairs={{0,1},{1,0},{2,3},{3,2},{4,5},{5,4},{6,7},{7,6},{8,9},{9,8},{10,11... | collective-permute-start | bytes 1769480 | tf_op jit(solution)/shard_map/ppermute | solution.py:339
  4.6 10.3 %collective-permute-start.2 = (f32[584,128]{1,0:T(8,128)S(1)}, f32[584,128]{1,0:T(8,128)S(1)}, u32[]{:S(2)}, u32[]{:S(2)}) collective-permute-start(f32[584,128]{1,0:T(8,128)S(1)} %add.7), channel_id=1, source_target_pairs={{0,2},{1,3},{2,0},{3,1},{4,6},{5,7},{6,4},{7,5},{8,10},{9,11},{10,... | collective-permute-start | bytes 897032 | tf_op jit(solution)/shard_map/ppermute | solution.py:339
  7.6 9.1 %collective-permute-start = (f32[576,128]{1,0:T(8,128)S(1)}, f32[576,128]{1,0:T(8,128)S(1)}, u32[]{:S(2)}, u32[]{:S(2)}) collective-permute-start(f32[576,128]{1,0:T(8,128)S(1)} %get-tuple-element.51), channel_id=1, source_target_pairs={{0,1},{1,0},{2,3},{3,2},{4,5},{5,4},{6,7},{7,6},{8,9},{9,8},{10,11... | collective-permute-start | bytes 884744 | tf_op jit(solution)/shard_map/ppermute | solution.py:339
  15.0 23.0 %collective-permute-start.16 = (bf16[2,192,384]{2,1,0:T(8,128)(2,1)S(1)}, bf16[2,192,384]{2,1,0:T(8,128)(2,1)S(1)}, u32[]{:S(2)}, u32[]{:S(2)}) collective-permute-start(bf16[2,192,384]{2,1,0:T(8,128)(2,1)S(1)} %constant_dynamic-slice_fusion), channel_id=1, source_target_pairs={{0,2},{1,3},{2,0},{3,1},{4,6},{5,7},{6,4},{7,5},{8,10},{9,11},{10,... | collective-permute-start | bytes 884744 | tf_op jit(solution)/shard_map/ppermute | solution.py:339
  18.4 6.1 %collective-permute-start.9 = (f32[152,128]{1,0:T(8,128)S(1)}, f32[152,128]{1,0:T(8,128)S(1)}, u32[]{:S(2)}, u32[]{:S(2)}) collective-permute-start(f32[152,128]{1,0:T(8,128)S(1)} %get-tuple-element.60), channel_id=1, source_target_pairs={{0,4},{4,0},{8,12},{12,8},{16,20},{20,16},{24,28},{28,24},{1,5},{5... | collective-permute-start | bytes 233480 | tf_op jit(solution)/shard_map/ppermute | solution.py:339
  20.0 7.3 %collective-permute-start.10 = (f32[152,128]{1,0:T(8,128)S(1)}, f32[152,128]{1,0:T(8,128)S(1)}, u32[]{:S(2)}, u32[]{:S(2)}) collective-permute-start(f32[152,128]{1,0:T(8,128)S(1)} %get-tuple-element.61), channel_id=1, source_target_pairs={{0,8},{4,12},{8,0},{12,4},{16,24},{20,28},{24,16},{28,20},{1,9},{5... | collective-permute-start | bytes 233480 | tf_op jit(solution)/shard_map/ppermute | solution.py:339
  21.5 8.0 %collective-permute-start.11 = (f32[152,128]{1,0:T(8,128)S(1)}, f32[152,128]{1,0:T(8,128)S(1)}, u32[]{:S(2)}, u32[]{:S(2)}) collective-permute-start(f32[152,128]{1,0:T(8,128)S(1)} %get-tuple-element.62), channel_id=1, source_target_pairs={{0,12},{4,8},{8,4},{12,0},{16,28},{20,24},{24,20},{28,16},{1,13},{... | collective-permute-start | bytes 233480 | tf_op jit(solution)/shard_map/ppermute | solution.py:339
  21.9 9.1 %collective-permute-start.4 = (f32[152,128]{1,0:T(8,128)S(1)}, f32[152,128]{1,0:T(8,128)S(1)}, u32[]{:S(2)}, u32[]{:S(2)}) collective-permute-start(f32[152,128]{1,0:T(8,128)S(1)} %get-tuple-element.55), channel_id=1, source_target_pairs={{0,16},{4,20},{8,24},{12,28},{16,0},{20,4},{24,8},{28,12},{1,17},{... | collective-permute-start | bytes 233480 | tf_op jit(solution)/shard_map/ppermute | solution.py:339
  24.5 12.7 %collective-permute-start.5 = (f32[152,128]{1,0:T(8,128)S(1)}, f32[152,128]{1,0:T(8,128)S(1)}, u32[]{:S(2)}, u32[]{:S(2)}) collective-permute-start(f32[152,128]{1,0:T(8,128)S(1)} %get-tuple-element.56), channel_id=1, source_target_pairs={{0,20},{4,16},{8,28},{12,24},{16,4},{20,0},{24,12},{28,8},{1,21},{... | collective-permute-start | bytes 233480 | tf_op jit(solution)/shard_map/ppermute | solution.py:339
  27.2 10.0 %collective-permute-start.6 = (f32[152,128]{1,0:T(8,128)S(1)}, f32[152,128]{1,0:T(8,128)S(1)}, u32[]{:S(2)}, u32[]{:S(2)}) collective-permute-start(f32[152,128]{1,0:T(8,128)S(1)} %get-tuple-element.57), channel_id=1, source_target_pairs={{0,24},{4,28},{8,16},{12,20},{16,8},{20,12},{24,0},{28,4},{1,25},{... | collective-permute-start | bytes 233480 | tf_op jit(solution)/shard_map/ppermute | solution.py:339
  29.6 7.6 %collective-permute-start.7 = (f32[152,128]{1,0:T(8,128)S(1)}, f32[152,128]{1,0:T(8,128)S(1)}, u32[]{:S(2)}, u32[]{:S(2)}) collective-permute-start(f32[152,128]{1,0:T(8,128)S(1)} %get-tuple-element.58), channel_id=1, source_target_pairs={{0,28},{4,24},{8,20},{12,16},{16,12},{20,8},{24,4},{28,0},{1,29},{... | collective-permute-start | bytes 233480 | tf_op jit(solution)/shard_map/ppermute | solution.py:339
  31.0 7.0 %collective-permute-start.13 = (f32[608,128]{1,0:T(8,128)S(1)}, f32[608,128]{1,0:T(8,128)S(1)}, u32[]{:S(2)}, u32[]{:S(2)}) collective-permute-start(f32[608,128]{1,0:T(8,128)S(1)} %constant_dynamic-update-slice_fusion.6.mine_ref), channel_id=1, source_target_pairs={{0,2},{1,3},{2,0},{3,1},{4,6},{5,7},{6,4},{7,5},{8,10},{9,11},{10,... | collective-permute-start | bytes 933896 | tf_op jit(solution)/shard_map/ppermute | solution.py:339
  37.2 3.2 %collective-permute-start.12 = (f32[608,128]{1,0:T(8,128)S(1)}, f32[608,128]{1,0:T(8,128)S(1)}, u32[]{:S(2)}, u32[]{:S(2)}) collective-permute-start(f32[608,128]{1,0:T(8,128)S(1)} %constant_dynamic-update-slice_fusion.6.mine_ref), channel_id=1, source_target_pairs={{0,1},{1,0},{2,3},{3,2},{4,5},{5,4},{6,7},{7,6},{8,9},{9,8},{10,11... | collective-permute-start | bytes 933896 | tf_op jit(solution)/shard_map/ppermute | solution.py:339
  37.2 3.2 %collective-permute-start.15 = (f32[608,128]{1,0:T(8,128)S(1)}, f32[608,128]{1,0:T(8,128)S(1)}, u32[]{:S(2)}, u32[]{:S(2)}) collective-permute-start(f32[608,128]{1,0:T(8,128)S(1)} %constant_dynamic-update-slice_fusion.2.far_ref), channel_id=1, source_target_pairs={{0,1},{1,0},{2,3},{3,2},{4,5},{5,4},{6,7},{7,6},{8,9},{9,8},{10,11... | collective-permute-start | bytes 933896 | tf_op jit(solution)/shard_map/ppermute | solution.py:339
  38.0 2.5 %collective-permute-start.14 = (f32[608,128]{1,0:T(8,128)S(1)}, f32[608,128]{1,0:T(8,128)S(1)}, u32[]{:S(2)}, u32[]{:S(2)}) collective-permute-start(f32[608,128]{1,0:T(8,128)S(1)} %collective-permute-done.13.chip_ref), channel_id=1, source_target_pairs={{0,1},{1,0},{2,3},{3,2},{4,5},{5,4},{6,7},{7,6},{8,9},{9,8},{10,11... | collective-permute-start | bytes 933896 | tf_op jit(solution)/shard_map/ppermute | solution.py:339
  38.0 2.1 %collective-permute-start.17 = (bf16[2,192,384]{2,1,0:T(8,128)(2,1)S(1)}, bf16[2,192,384]{2,1,0:T(8,128)(2,1)S(1)}, u32[]{:S(2)}, u32[]{:S(2)}) collective-permute-start(bf16[2,192,384]{2,1,0:T(8,128)(2,1)S(1)} %collective-permute-done.16.chip_ref), channel_id=1, source_target_pairs={{0,1},{1,0},{2,3},{3,2},{4,5},{5,4},{6,7},{7,6},{8,9},{9,8},{10,11... | collective-permute-start | bytes 884744 | tf_op jit(solution)/shard_map/ppermute | solution.py:339
  38.5 9.3 %collective-permute-start.8 = (f32[608,128]{1,0:T(8,128)S(1)}, f32[608,128]{1,0:T(8,128)S(1)}, u32[]{:S(2)}, u32[]{:S(2)}) collective-permute-start(f32[608,128]{1,0:T(8,128)S(1)} %constant_dynamic-update-slice_fusion.2.far_ref), channel_id=1, source_target_pairs={{0,2},{1,3},{2,0},{3,1},{4,6},{5,7},{6,4},{7,5},{8,10},{9,11},{10,... | collective-permute-start | bytes 933896 | tf_op jit(solution)/shard_map/ppermute | solution.py:339
  47.7 1.6 %collective-permute-start.18 = (f32[608,128]{1,0:T(8,128)S(1)}, f32[608,128]{1,0:T(8,128)S(1)}, u32[]{:S(2)}, u32[]{:S(2)}) collective-permute-start(f32[608,128]{1,0:T(8,128)S(1)} %collective-permute-done.8.chip_ref), channel_id=1, source_target_pairs={{0,1},{1,0},{2,3},{3,2},{4,5},{5,4},{6,7},{7,6},{8,9},{9,8},{10,11... | collective-permute-start | bytes 933896 | tf_op jit(solution)/shard_map/ppermute | solution.py:339
  49.3 14.5 %copy-start.6 = (f32[1,192,768]{2,1,0:T(8,128)S(1)}, f32[1,192,768]{2,1,0:T(8,128)}, u32[]{:S(2)}) copy-start(f32[1,192,768]{2,1,0:T(8,128)} %left_ref.1) | copy-start | bytes 1769476
  49.3 14.5 %copy-start.7 = (f32[1,192,768]{2,1,0:T(8,128)S(1)}, f32[1,192,768]{2,1,0:T(8,128)}, u32[]{:S(2)}) copy-start(f32[1,192,768]{2,1,0:T(8,128)} %right_ref.1) | copy-start | bytes 1769476
  51.9 9.5 %collective-permute-start.19 = (f32[144,128]{1,0:T(8,128)S(1)}, f32[144,128]{1,0:T(8,128)S(1)}, u32[]{:S(2)}, u32[]{:S(2)}) collective-permute-start(f32[144,128]{1,0:T(8,128)S(1)} %get-tuple-element.73), channel_id=1, source_target_pairs={{0,4},{4,0},{8,12},{12,8},{16,20},{20,16},{24,28},{28,24},{1,5},{5... | collective-permute-start | bytes 221192 | tf_op jit(solution)/shard_map/ppermute | solution.py:339
  56.1 7.7 %collective-permute-start.20 = (f32[144,128]{1,0:T(8,128)S(1)}, f32[144,128]{1,0:T(8,128)S(1)}, u32[]{:S(2)}, u32[]{:S(2)}) collective-permute-start(f32[144,128]{1,0:T(8,128)S(1)} %get-tuple-element.74), channel_id=1, source_target_pairs={{0,8},{4,12},{8,0},{12,4},{16,24},{20,28},{24,16},{28,20},{1,9},{5... | collective-permute-start | bytes 221192 | tf_op jit(solution)/shard_map/ppermute | solution.py:339
  56.1 12.3 %collective-permute-start.21 = (f32[144,128]{1,0:T(8,128)S(1)}, f32[144,128]{1,0:T(8,128)S(1)}, u32[]{:S(2)}, u32[]{:S(2)}) collective-permute-start(f32[144,128]{1,0:T(8,128)S(1)} %get-tuple-element.75), channel_id=1, source_target_pairs={{0,16},{4,20},{8,24},{12,28},{16,0},{20,4},{24,8},{28,12},{1,17},{... | collective-permute-start | bytes 221192 | tf_op jit(solution)/shard_map/ppermute | solution.py:339
  58.7 10.8 %collective-permute-start.22 = (f32[144,128]{1,0:T(8,128)S(1)}, f32[144,128]{1,0:T(8,128)S(1)}, u32[]{:S(2)}, u32[]{:S(2)}) collective-permute-start(f32[144,128]{1,0:T(8,128)S(1)} %get-tuple-element.76), channel_id=1, source_target_pairs={{0,20},{4,16},{8,28},{12,24},{16,4},{20,0},{24,12},{28,8},{1,21},{... | collective-permute-start | bytes 221192 | tf_op jit(solution)/shard_map/ppermute | solution.py:339
  59.1 10.5 %collective-permute-start.23 = (f32[144,128]{1,0:T(8,128)S(1)}, f32[144,128]{1,0:T(8,128)S(1)}, u32[]{:S(2)}, u32[]{:S(2)}) collective-permute-start(f32[144,128]{1,0:T(8,128)S(1)} %get-tuple-element.77), channel_id=1, source_target_pairs={{0,24},{4,28},{8,16},{12,20},{16,8},{20,12},{24,0},{28,4},{1,25},{... | collective-permute-start | bytes 221192 | tf_op jit(solution)/shard_map/ppermute | solution.py:339
  61.4 8.1 %collective-permute-start.24 = (f32[144,128]{1,0:T(8,128)S(1)}, f32[144,128]{1,0:T(8,128)S(1)}, u32[]{:S(2)}, u32[]{:S(2)}) collective-permute-start(f32[144,128]{1,0:T(8,128)S(1)} %get-tuple-element.78), channel_id=1, source_target_pairs={{0,28},{4,24},{8,20},{12,16},{16,12},{20,8},{24,4},{28,0},{1,29},{... | collective-permute-start | bytes 221192 | tf_op jit(solution)/shard_map/ppermute | solution.py:339
  63.8 7.0 %collective-permute-start.25 = (f32[144,128]{1,0:T(8,128)S(1)}, f32[144,128]{1,0:T(8,128)S(1)}, u32[]{:S(2)}, u32[]{:S(2)}) collective-permute-start(f32[144,128]{1,0:T(8,128)S(1)} %get-tuple-element.79), channel_id=1, source_target_pairs={{0,12},{4,8},{8,4},{12,0},{16,28},{20,24},{24,20},{28,16},{1,13},{... | collective-permute-start | bytes 221192 | tf_op jit(solution)/shard_map/ppermute | solution.py:339

commit v3 on v2

--- a/solution.py
+++ b/solution.py
@@ -17,7 +17,7 @@
 BIAS_TWO = 1.0 - BETA_TWO**STEP_COUNT
 HIGH = lax.Precision.HIGHEST
 LANES = 128
-BACK = (1, 2, 4, 5, 6, 7, 3, 0)
+BACK = (4, 1, 5, 2, 6, 3, 7, 0)
 EXTRA = 8
 F32 = jnp.float32
 BF16 = jnp.bfloat16
@@ -111,19 +111,19 @@
     return head, jnp.where(first, wide, turned)[:, : LANES // 2]
 
 
-def split_kernel(rows, tiles, g_ref, vec_ref, sf_ref, sn_ref, kf_ref, kn_ref):
+def split_kernel(rows, tiles, far, g_ref, *refs):
+    vec_ref, send_ref, keep_ref = refs if len(refs) == 3 else (None, *refs)
     _, _, chip, core = place()
     packed = rows + rows // 2
-    for out, far, own in ((sf_ref, True, False), (sn_ref, False, False), (kf_ref, True, True), (kn_ref, False, True)):
-        x = 1 - chip if far else chip
-        d = core if own else 1 - core
+    x = 1 - chip if far else chip
+    for out, d in ((send_ref, 1 - core), (keep_ref, core)):
         for k in range(tiles):
             base = k * packed
             out[base : base + rows] = g_ref[0, k, :, lane_tile(3 * x + 2 * d)]
             out[base + rows : base + packed] = fold(g_ref[0, k, :, lane_tile(3 * x + 1)], d)
-        if far:
+        if vec_ref is not None:
             out[tiles * packed :] = jnp.zeros((EXTRA, LANES), F32)
-            out[tiles * packed : tiles * packed + tiles, : rows] = vec_ref[0]
+            out[tiles * packed : tiles * packed + tiles, :rows] = vec_ref[0]
 
 
 def tile_of(owner_ref, slot, tiles):
@@ -134,15 +134,15 @@
 
 
 def adam_kernel(
-    rows, tiles, shards, owner_ref, kn_ref, rn_ref, u_ref, r_ref, v_ref, m_ref, vv_ref, *refs
+    rows, tiles, shards, owner_ref, kn_ref, rn_ref, r_ref, v_ref, *refs
 ):
-    outs, (nv_ref, vm_ref, vn_ref, vs_ref), (g_ref, ext_ref) = refs[:shards], refs[shards : shards + 4], refs[shards + 4 :]
+    outs, (nv_ref, vec_ref, g_ref, ext_ref) = refs[:shards], refs[shards:]
     shard, _, _, core = place()
     packed = rows + rows // 2
 
     def one(g, v_old):
         v_new = BETA_TWO * v_old + (1.0 - BETA_TWO) * g * g
-        step = g / (jnp.sqrt(v_new / BIAS_TWO) + EPSILON)
+        step = g / (jnp.sqrt(v_new * (1.0 / BIAS_TWO)) + EPSILON)
         sq = step * step
         return v_new, jnp.sum(sq.reshape(-1, 8, sq.shape[1]), axis=0)
 
@@ -158,8 +158,7 @@
         k = tile_of(owner_ref, shard ^ j, tiles)
         outs[j][:packed] = g_ref[k]
         outs[j][packed:] = ext_ref[k]
-    vec = u_ref[:tiles, :rows] + r_ref[tiles * packed : tiles * packed + tiles, :rows]
-    vm_ref[...], vn_ref[...], vs_ref[...] = vec_update(vec, m_ref[...], vv_ref[...])
+    vec_ref[...] = kn_ref[tiles * packed :] + rn_ref[tiles * packed :]
 
 
 def roots_kernel(own_ref, core_ref, chip_ref, both_ref, left_ref, right_ref):
@@ -203,7 +202,8 @@
 
 def near_kernel(
     rows, shards, mine_ref, peer_ref, chip_ref, both_ref, far_ref, far_peer_ref, left_ref, right_ref,
-    ah_ref, al_ref, bh_ref, bl_ref, z_ref, dir_ref, adam_ref, zh_ref, zl_ref
+    m_ref, v_ref, adam_new, ah_ref, al_ref, bh_ref, bl_ref, z_ref, dir_ref, adam_ref, nm_ref, nv_ref, step_ref,
+    adam_out, zh_ref, zl_ref
 ):
     shard, _, chip, core = place()
     group = shards // 2
@@ -221,6 +221,11 @@
         for n, tile in enumerate(parts):
             bh_ref[to, n * LANES : (n + 1) * LANES], bl_ref[to, n * LANES : (n + 1) * LANES] = halves(tile)
     adam_ref[...] = adam
+    end = group * (rows + rows // 2 + EXTRA)
+    vecs, wide = m_ref.shape
+    vec = mine_ref[end : end + vecs, :wide] + chip_ref[end : end + vecs, :wide]
+    nm_ref[...], nv_ref[...], step_ref[...] = vec_update(vec, m_ref[...], v_ref[...])
+    adam_out[...] = adam_new[...]
     z = product(ah_ref[...], right_ref[...]) + product(al_ref[...], right_ref[...])
     zh_ref[...], zl_ref[...] = halves(z)
     here = pl.ds(pl.multiple_of(chip * half, half), half)
@@ -309,12 +314,12 @@
 def back_kernel(rows, tiles, shards, owner_ref, *refs):
     blocks, out_ref = refs[:shards], refs[shards]
     shard, _, _, core = place()
-    for k in range(tiles):
-        for j, block in zip(BACK, blocks):
-
-            @pl.when((shard ^ j) == owner_ref[k])
-            def _(k=k, block=block):
-                out_ref[k, :, :LANES], out_ref[k, :, LANES:] = unfold(block[...], rows, core)
+    for j, block in zip(BACK, blocks):
+        k = tile_of(owner_ref, shard ^ j, tiles)
+
+        @pl.when(owner_ref[k] == (shard ^ j))
+        def _(k=k, block=block):
+            out_ref[k, :, :LANES], out_ref[k, :, LANES:] = unfold(block[...], rows, core)
 
 
 def shape(dims, dtype=F32):
@@ -349,9 +354,8 @@
 
     block = shape((tiles * packed, LANES))
     wide = shape((tiles * packed + EXTRA, LANES))
-    sf, sn, kf, kn = kernel_call(
-        functools.partial(split_kernel, rows, tiles), (wide, block, wide, block), (grad_parts, vec_parts)
-    )
+    sf, kf = kernel_call(functools.partial(split_kernel, rows, tiles, True), (block, block), (grad_parts,))
+    sn, kn = kernel_call(functools.partial(split_kernel, rows, tiles, False), (wide, wide), (grad_parts, vec_parts))
     u = kf + swap(sf, "tensor", 1)
     rn = swap(sn, "tensor", 1)
     r = swap(u, "tensor", 2)
@@ -360,15 +364,14 @@
     crossing = lax.dynamic_slice_in_dim(roots, quadrant, size // 2, 2)
     roots_core = swap(roots, "tensor", 1)
     r, roots, roots_core, crossing = lax.optimization_barrier((r, roots, roots_core, crossing))
-    vec = shape((tiles, rows))
     res = kernel_call(
         functools.partial(adam_kernel, rows, tiles, shards),
-        (shape((packed + EXTRA, LANES)),) * shards + (shape(adam_v.shape), vec, vec, vec),
-        (owner, kn, rn, u[tiles * packed :], r, adam_v, vec_m, vec_v),
+        (shape((packed + EXTRA, LANES)),) * shards + (shape(adam_v.shape), shape((EXTRA, LANES))),
+        (owner, kn, rn, r, adam_v),
         (pltpu.VMEM((tiles, packed, LANES), F32), pltpu.VMEM((tiles, EXTRA, LANES), F32)),
         smem=1,
     )
-    outgoing, (new_adam_v, new_vec_m, new_vec_v, vec_step) = res[:shards], res[shards:]
+    outgoing, (adam_new, vec_pair) = res[:shards], res[shards:]
 
     arrived = [outgoing[0]] + [swap(outgoing[j], "shard", j) for j in range(1, shards)]
     roots_chip = swap(crossing, "tensor", 2)
@@ -376,17 +379,18 @@
     left_full, right_full = kernel_call(
         roots_kernel, (full, full), (roots, roots_core, roots_chip, swap(roots_chip, "tensor", 1)), mib=24
     )
-    near = jnp.concatenate(arrived[: shards // 2], axis=0)
+    near = jnp.concatenate([*arrived[: shards // 2], vec_pair], axis=0)
     far = jnp.concatenate(arrived[shards // 2 :], axis=0)
     near_across = swap(near, "tensor", 2)
     near = near, swap(near, "tensor", 1), near_across, swap(near_across, "tensor", 1)
     far_across = swap(far, "tensor", 2)
     half = size // 2
     tall, square = shape((half, size), BF16), shape((half, half), BF16)
-    ah, al, bh, bl, z, part, adam = kernel_call(
+    vec = shape(vec_m.shape)
+    ah, al, bh, bl, z, part, adam, new_vec_m, new_vec_v, vec_step, new_adam_v = kernel_call(
         functools.partial(near_kernel, rows, shards),
-        (tall, tall, square, square, shape((half, size)), shape((size, size)), shape((EXTRA, LANES))),
-        (*near, far, swap(far, "tensor", 1), left_full, right_full),
+        (tall, tall, square, square, shape((half, size)), shape((size, size)), shape((EXTRA, LANES)), vec, vec, vec, shape(adam_v.shape)),
+        (*near, far, swap(far, "tensor", 1), left_full, right_full, vec_m, vec_v, adam_new),
         (pltpu.VMEM((half, size), BF16),) * 2,
         flops=5 * size**3,
         mib=32,

time: 72.8 us -> 71.3 us (0.979)
  waiting for transfers between devices: 23.1 us -> 21.8 us
    ppermute x26, waiting for transfers between devices: 23.1 us -> 21.8 us  [swap(): lax.ppermute(a, axis, [(i, i ^ mask) for i in range(lax.axis_size(axis))])]
    unnamed x27 -> x28, local copies, waits for them, and re-layouts: 2.25 us -> 1.7 us
    pallas_call x7 -> x8, Pallas kernels: 14 us -> 14 us  [kernel_call(): pl.pallas_call(body, out_shape=outs, in_specs=[pl.BlockSpec(memory_space=...]
  transfers between devices with their start and end apart: 26 -> 26, of which waited for: 10 -> 8; matrix products, arithmetic and copies ran while one was open for 0% -> 0% of each run, Pallas kernels for 13% -> 13%
where the time goes in v3:
time: 71.3 us; the launch traced here: 71.1 us
  starting transfers between devices  32.7 us (46%)
  waiting for transfers between devices  21.8 us (31%)
  Pallas kernels  14 us (20%)
  local copies, waits for them, and re-layouts  1.76 us (2%)
  between operations  0.84 us (1%)
    ppermute x26, starting transfers between devices, swap(): lax.ppermute(a, axis, [(i, i ^ mask) for i in range(lax.axis_size(axis))])  32.7 us
    ppermute x26, waiting for transfers between devices, swap(): lax.ppermute(a, axis, [(i, i ^ mask) for i in range(lax.axis_size(axis))])  21.8 us
    pallas_call x8, Pallas kernels, kernel_call(): pl.pallas_call(body, out_shape=outs, in_specs=[pl.BlockSpec(memory_space=...  14 us
    unnamed x28, local copies, waits for them, and re-layouts  1.7 us
  transfers between devices with their start and end apart: 26, of which 8 were waited for; matrix products, arithmetic and copies ran while one was open for 0% of the time, Pallas kernels for 13%

profile of v3, /device:TPU:0, one launch (start us, length us, event | category | flops | bytes accessed | tf_op | source)
XLA Modules:
  0.0 71.1 jit_solution(3937250083227529907)
XLA Ops:
  0.6 1.3 %copy-done = f32[1,4,96,768]{3,2,1,0:T(8,128)S(1)} copy-done((f32[1,4,96,768]{3,2,1,0:T(8,128)S(1)}, f32[1,4,96,768]{3,2,1,0:T(8,128)}, u32[]{:S(2)}) %copy-start) | copy-done | bytes 1179672
  1.9 0.2 shard_map.154
  2.1 0.5 collective-permute-start.1
  2.6 0.3 copy-done.8
  2.9 0.1 copy-done.9
  3.0 0.0 copy-start.1
  3.0 0.0 copy-start.2
  3.0 0.5 collective-permute-start.3
  3.5 0.2 shard_map.153
  3.7 0.1 collective-permute-start
  3.9 3.0 %collective-permute-start.2 = (f32[576,128]{1,0:T(8,128)S(1)}, f32[576,128]{1,0:T(8,128)S(1)}, u32[]{:S(2)}, u32[]{:S(2)}) collective-permute-start(f32[576,128]{1,0:T(8,128)S(1)} %add.7), channel_id=1, source_target_pairs={{0,2},{1,3},{2,0},{3,1},{4,6},{5,7},{6,4},{7,5},{8,10},{9,11},{10,... | collective-permute-start | bytes 884744 | tf_op jit(solution)/shard_map/ppermute | solution.py:344
  6.9 7.2 %collective-permute-done.2.r_ref = f32[576,128]{1,0:T(8,128)S(1)} collective-permute-done((f32[576,128]{1,0:T(8,128)S(1)}, f32[576,128]{1,0:T(8,128)S(1)}, u32[]{:S(2)}, u32[]{:S(2)}) %collective-permute-start.2) | collective-permute-done | bytes 294944 | tf_op jit(solution)/shard_map/ppermute | solution.py:344
  14.1 0.0 collective-permute-done.3.core_ref
  14.1 1.7 %collective-permute-start.16 = (bf16[2,192,384]{2,1,0:T(8,128)(2,1)S(1)}, bf16[2,192,384]{2,1,0:T(8,128)(2,1)S(1)}, u32[]{:S(2)}, u32[]{:S(2)}) collective-permute-start(bf16[2,192,384]{2,1,0:T(8,128)(2,1)S(1)} %constant_dynamic-slice_fusion), channel_id=1, source_target_pairs={{0,2},{1,3},{2,0},{3,1},{4,6},{5,7},{6,4},{7,5},{8,10},{9,11},{10,... | collective-permute-start | bytes 884744 | tf_op jit(solution)/shard_map/ppermute | solution.py:344
  15.8 0.0 collective-permute-done.rn_ref
  15.8 1.0 %shard_map.155 = (f32[152,128]{1,0:T(8,128)S(1)}, f32[152,128]{1,0:T(8,128)S(1)}, f32[152,128]{1,0:T(8,128)S(1)}, f32[152,128]{1,0:T(8,128)S(1)}, f32[152,128]{1...) custom-call(s32[4]{0:T(128)S(1)} %copy-done.2, ...), custom_call_target="tpu_custom_call" | custom-call | bytes 2109456 | tf_op jit(solution)/shard_map/pallas_call | solution.py:332
  16.8 1.6 %collective-permute-start.9 = (f32[152,128]{1,0:T(8,128)S(1)}, f32[152,128]{1,0:T(8,128)S(1)}, u32[]{:S(2)}, u32[]{:S(2)}) collective-permute-start(f32[152,128]{1,0:T(8,128)S(1)} %get-tuple-element.62), channel_id=1, source_target_pairs={{0,4},{4,0},{8,12},{12,8},{16,20},{20,16},{24,28},{28,24},{1,5},{5... | collective-permute-start | bytes 233480 | tf_op jit(solution)/shard_map/ppermute | solution.py:344
  18.4 1.6 %collective-permute-start.10 = (f32[152,128]{1,0:T(8,128)S(1)}, f32[152,128]{1,0:T(8,128)S(1)}, u32[]{:S(2)}, u32[]{:S(2)}) collective-permute-start(f32[152,128]{1,0:T(8,128)S(1)} %get-tuple-element.63), channel_id=1, source_target_pairs={{0,8},{4,12},{8,0},{12,4},{16,24},{20,28},{24,16},{28,20},{1,9},{5... | collective-permute-start | bytes 233480 | tf_op jit(solution)/shard_map/ppermute | solution.py:344
  20.0 0.4 collective-permute-start.11
  20.4 2.6 %collective-permute-start.4 = (f32[152,128]{1,0:T(8,128)S(1)}, f32[152,128]{1,0:T(8,128)S(1)}, u32[]{:S(2)}, u32[]{:S(2)}) collective-permute-start(f32[152,128]{1,0:T(8,128)S(1)} %get-tuple-element.57), channel_id=1, source_target_pairs={{0,16},{4,20},{8,24},{12,28},{16,0},{20,4},{24,8},{28,12},{1,17},{... | collective-permute-start | bytes 233480 | tf_op jit(solution)/shard_map/ppermute | solution.py:344
  23.0 2.7 %collective-permute-start.5 = (f32[152,128]{1,0:T(8,128)S(1)}, f32[152,128]{1,0:T(8,128)S(1)}, u32[]{:S(2)}, u32[]{:S(2)}) collective-permute-start(f32[152,128]{1,0:T(8,128)S(1)} %get-tuple-element.58), channel_id=1, source_target_pairs={{0,20},{4,16},{8,28},{12,24},{16,4},{20,0},{24,12},{28,8},{1,21},{... | collective-permute-start | bytes 233480 | tf_op jit(solution)/shard_map/ppermute | solution.py:344
  25.7 2.3 %collective-permute-start.6 = (f32[152,128]{1,0:T(8,128)S(1)}, f32[152,128]{1,0:T(8,128)S(1)}, u32[]{:S(2)}, u32[]{:S(2)}) collective-permute-start(f32[152,128]{1,0:T(8,128)S(1)} %get-tuple-element.59), channel_id=1, source_target_pairs={{0,24},{4,28},{8,16},{12,20},{16,8},{20,12},{24,0},{28,4},{1,25},{... | collective-permute-start | bytes 233480 | tf_op jit(solution)/shard_map/ppermute | solution.py:344
  28.0 1.5 %collective-permute-start.7 = (f32[152,128]{1,0:T(8,128)S(1)}, f32[152,128]{1,0:T(8,128)S(1)}, u32[]{:S(2)}, u32[]{:S(2)}) collective-permute-start(f32[152,128]{1,0:T(8,128)S(1)} %get-tuple-element.60), channel_id=1, source_target_pairs={{0,28},{4,24},{8,20},{12,16},{16,12},{20,8},{24,4},{28,0},{1,29},{... | collective-permute-start | bytes 233480 | tf_op jit(solution)/shard_map/ppermute | solution.py:344
  29.5 0.0 copy-start.6
  29.5 0.0 copy-start.7
  29.6 0.6 collective-permute-start.13
  30.2 5.4 %collective-permute-done.5 = f32[152,128]{1,0:T(8,128)S(1)} collective-permute-done((f32[152,128]{1,0:T(8,128)S(1)}, f32[152,128]{1,0:T(8,128)S(1)}, u32[]{:S(2)}, u32[]{:S(2)}) %collective-permute-start.5) | collective-permute-done | bytes 77856 | tf_op jit(solution)/shard_map/ppermute | solution.py:344
  35.6 1.0 %collective-permute-done.13.chip_ref = f32[616,128]{1,0:T(8,128)S(1)} collective-permute-done((f32[616,128]{1,0:T(8,128)S(1)}, f32[616,128]{1,0:T(8,128)S(1)}, u32[]{:S(2)}, u32[]{:S(2)}) %collective-permute-start.13) | collective-permute-done | bytes 315424 | tf_op jit(solution)/shard_map/ppermute | solution.py:344
  36.6 0.6 collective-permute-start.15
  37.2 0.1 collective-permute-start.17
  37.3 0.5 collective-permute-start.8
  37.8 1.3 %collective-permute-done.17.both_ref = bf16[2,192,384]{2,1,0:T(8,128)(2,1)S(1)} collective-permute-done((bf16[2,192,384]{2,1,0:T(8,128)(2,1)S(1)}, bf16[2,192,384]{2,1,0:T(8,128)(2,1)S(1)}, u32[]{:S(2)}, u32[]{:S(2)}) %collective-permute-start.17) | collective-permute-done | bytes 294944 | tf_op jit(solution)/shard_map/ppermute | solution.py:344
  39.1 0.3 shard_map.156
  39.4 4.0 %shard_map.157 = (bf16[384,768]{1,0:T(8,128)(2,1)S(1)}, bf16[384,768]{1,0:T(8,128)(2,1)S(1)}, bf16[384,384]{1,0:T(8,128)(2,1)S(1)}, bf16[384,384]{1,0:T(8,128)(2...) custom-call(f32[616,128]{1,0:T(8,128)S(1)} %constant_dynamic-update-, ...), custom_call_target="tpu_custom_call" | custom-call | flops 2264924160 | bytes 10153472 | tf_op jit(solution)/shard_map/pallas_call | solution.py:332
  43.4 3.5 %collective-permute-done.8.chip_ref = f32[608,128]{1,0:T(8,128)S(1)} collective-permute-done((f32[608,128]{1,0:T(8,128)S(1)}, f32[608,128]{1,0:T(8,128)S(1)}, u32[]{:S(2)}, u32[]{:S(2)}) %collective-permute-start.8) | collective-permute-done | bytes 311328 | tf_op jit(solution)/shard_map/ppermute | solution.py:344
  47.0 1.6 %collective-permute-done.18.both_ref = f32[608,128]{1,0:T(8,128)S(1)} collective-permute-done((f32[608,128]{1,0:T(8,128)S(1)}, f32[608,128]{1,0:T(8,128)S(1)}, u32[]{:S(2)}, u32[]{:S(2)}) %collective-permute-start.18) | collective-permute-done | bytes 311328 | tf_op jit(solution)/shard_map/ppermute | solution.py:344
  48.6 2.5 %shard_map.158 = (bf16[384,384]{1,0:T(8,128)(2,1)S(1)}, bf16[384,384]{1,0:T(8,128)(2,1)S(1)}, f32[144,128]{1,0:T(8,128)S(1)}, f32[144,128]{1,0:T(8,128)S(1)}, f3...) custom-call(f32[608,128]{1,0:T(8,128)S(1)} %collective-permute-done., ...), custom_call_target="tpu_custom_call" | custom-call | flops 1358954496 | bytes 7704576 | tf_op jit(solution)/shard_map/pallas_call | solution.py:332
  51.1 1.8 %collective-permute-start.19 = (f32[144,128]{1,0:T(8,128)S(1)}, f32[144,128]{1,0:T(8,128)S(1)}, u32[]{:S(2)}, u32[]{:S(2)}) collective-permute-start(f32[144,128]{1,0:T(8,128)S(1)} %get-tuple-element.77), channel_id=1, source_target_pairs={{0,16},{4,20},{8,24},{12,28},{16,0},{20,4},{24,8},{28,12},{1,17},{... | collective-permute-start | bytes 221192 | tf_op jit(solution)/shard_map/ppermute | solution.py:344
  52.9 2.3 %collective-permute-start.20 = (f32[144,128]{1,0:T(8,128)S(1)}, f32[144,128]{1,0:T(8,128)S(1)}, u32[]{:S(2)}, u32[]{:S(2)}) collective-permute-start(f32[144,128]{1,0:T(8,128)S(1)} %get-tuple-element.78), channel_id=1, source_target_pairs={{0,4},{4,0},{8,12},{12,8},{16,20},{20,16},{24,28},{28,24},{1,5},{5... | collective-permute-start | bytes 221192 | tf_op jit(solution)/shard_map/ppermute | solution.py:344
  55.2 2.3 %collective-permute-start.21 = (f32[144,128]{1,0:T(8,128)S(1)}, f32[144,128]{1,0:T(8,128)S(1)}, u32[]{:S(2)}, u32[]{:S(2)}) collective-permute-start(f32[144,128]{1,0:T(8,128)S(1)} %get-tuple-element.79), channel_id=1, source_target_pairs={{0,20},{4,16},{8,28},{12,24},{16,4},{20,0},{24,12},{28,8},{1,21},{... | collective-permute-start | bytes 221192 | tf_op jit(solution)/shard_map/ppermute | solution.py:344
  57.5 0.7 %collective-permute-start.22 = (f32[144,128]{1,0:T(8,128)S(1)}, f32[144,128]{1,0:T(8,128)S(1)}, u32[]{:S(2)}, u32[]{:S(2)}) collective-permute-start(f32[144,128]{1,0:T(8,128)S(1)} %get-tuple-element.80), channel_id=1, source_target_pairs={{0,8},{4,12},{8,0},{12,4},{16,24},{20,28},{24,16},{28,20},{1,9},{5... | collective-permute-start | bytes 221192 | tf_op jit(solution)/shard_map/ppermute | solution.py:344
  58.3 2.3 %collective-permute-start.23 = (f32[144,128]{1,0:T(8,128)S(1)}, f32[144,128]{1,0:T(8,128)S(1)}, u32[]{:S(2)}, u32[]{:S(2)}) collective-permute-start(f32[144,128]{1,0:T(8,128)S(1)} %get-tuple-element.81), channel_id=1, source_target_pairs={{0,24},{4,28},{8,16},{12,20},{16,8},{20,12},{24,0},{28,4},{1,25},{... | collective-permute-start | bytes 221192 | tf_op jit(solution)/shard_map/ppermute | solution.py:344
  60.5 1.7 %collective-permute-start.24 = (f32[144,128]{1,0:T(8,128)S(1)}, f32[144,128]{1,0:T(8,128)S(1)}, u32[]{:S(2)}, u32[]{:S(2)}) collective-permute-start(f32[144,128]{1,0:T(8,128)S(1)} %get-tuple-element.82), channel_id=1, source_target_pairs={{0,12},{4,8},{8,4},{12,0},{16,28},{20,24},{24,20},{28,16},{1,13},{... | collective-permute-start | bytes 221192 | tf_op jit(solution)/shard_map/ppermute | solution.py:344
  62.2 1.2 %collective-permute-start.25 = (f32[144,128]{1,0:T(8,128)S(1)}, f32[144,128]{1,0:T(8,128)S(1)}, u32[]{:S(2)}, u32[]{:S(2)}) collective-permute-start(f32[144,128]{1,0:T(8,128)S(1)} %get-tuple-element.83), channel_id=1, source_target_pairs={{0,28},{4,24},{8,20},{12,16},{16,12},{20,8},{24,4},{28,0},{1,29},{... | collective-permute-start | bytes 221192 | tf_op jit(solution)/shard_map/ppermute | solution.py:344
  63.5 4.1 %shard_map.160 = (f32[1,192,768]{2,1,0:T(8,128)}, f32[1,192,768]{2,1,0:T(8,128)}) custom-call(s32[4]{0:T(128)S(1)} %copy-done.2, bf16[384,768]{1,0:T(8,128)(2,1)S(1)} %get-tuple-element.86.ah_ref, bf16[384,768]{1,0:T(8,128)(2,1)S(1)} %get-tuple-element.87.al_ref, bf16[384,384]{1,0:T(8,128)(2,1)S(1)} %get-tuple-element.88.bh_ref, ...), custom_call_target="tpu_custom_call" | custom-call | flops 1358954496 | bytes 4718608 | tf_op jit(solution)/shard_map/pallas_call | solution.py:332
  67.6 0.4 collective-permute-done.24.refs_5_
  68.0 1.4 %collective-permute-done.25.refs_6_ = f32[144,128]{1,0:T(8,128)S(1)} collective-permute-done((f32[144,128]{1,0:T(8,128)S(1)}, f32[144,128]{1,0:T(8,128)S(1)}, u32[]{:S(2)}, u32[]{:S(2)}) %collective-permute-start.25) | collective-permute-done | bytes 73760 | tf_op jit(solution)/shard_map/ppermute | solution.py:344
  69.4 1.7 %shard_map.159 = f32[4,96,192]{2,1,0:T(8,128)} custom-call(s32[4]{0:T(128)S(1)} %copy-done.2, f32[144,128]{1,0:T(8,128)S(1)} %collective-permute-done.19.refs_0_, f32[144,128]{1,0:T(8,128)S(1)} %collective-permute-done.20.refs_1_, f32[144,128]{1,0:T(8,128)S(1)} %collective-permute-done.21.refs_2_, f32[144,128]{1,0:T(8,128)S(1)} %collective-permute-done.22.refs_3_, ...), custom_call_target="tpu_custom_call" | custom-call | bytes 884752 | tf_op jit(solution)/shard_map/pallas_call | solution.py:332
  (45 shorter events, 0.2 us)
Async XLA Ops:
  0.6 1.3 %copy-start = (f32[1,4,96,768]{3,2,1,0:T(8,128)S(1)}, f32[1,4,96,768]{3,2,1,0:T(8,128)}, u32[]{:S(2)}) copy-start(f32[1,4,96,768]{3,2,1,0:T(8,128)} %g_ref.3) | copy-start | bytes 3538948
  1.9 1.0 %copy-start.8 = (bf16[1,192,768]{2,1,0:T(8,128)(2,1)S(1)}, bf16[1,192,768]{2,1,0:T(8,128)(2,1)}, u32[]{:S(2)}) copy-start(bf16[1,192,768]{2,1,0:T(8,128)(2,1)} %param.14) | copy-start | bytes 884740
  1.9 1.0 %copy-start.9 = (bf16[1,192,768]{2,1,0:T(8,128)(2,1)S(1)}, bf16[1,192,768]{2,1,0:T(8,128)(2,1)}, u32[]{:S(2)}) copy-start(bf16[1,192,768]{2,1,0:T(8,128)(2,1)} %param.15) | copy-start | bytes 884740
  1.9 1.6 %copy-start.3 = (f32[1,4,96]{2,1,0:T(4,128)S(1)}, f32[1,4,96]{2,1,0:T(4,128)}, u32[]{:S(2)}) copy-start(f32[1,4,96]{2,1,0:T(4,128)} %refs_0_.1) | copy-start | bytes 4612
  2.1 1.7 %collective-permute-start.1 = (f32[576,128]{1,0:T(8,128)S(1)}, f32[576,128]{1,0:T(8,128)S(1)}, u32[]{:S(2)}, u32[]{:S(2)}) collective-permute-start(f32[576,128]{1,0:T(8,128)S(1)} %get-tuple-element.55), channel_id=1, source_target_pairs={{0,1},{1,0},{2,3},{3,2},{4,5},{5,4},{6,7},{7,6},{8,9},{9,8},{10,11... | collective-permute-start | bytes 884744 | tf_op jit(solution)/shard_map/ppermute | solution.py:344
  3.0 12.9 %copy-start.1 = (f32[4,96,192]{2,1,0:T(8,128)S(1)}, f32[4,96,192]{2,1,0:T(8,128)}, u32[]{:S(2)}) copy-start(f32[4,96,192]{2,1,0:T(8,128)} %v_ref.2) | copy-start | bytes 884740
  3.0 12.8 %copy-start.2 = (s32[4]{0:T(128)S(1)}, s32[4]{0:T(128)}, u32[]{:S(2)}) copy-start(s32[4]{0:T(128)} %owner_ref.5) | copy-start | bytes 52
  3.0 11.1 %collective-permute-start.3 = (bf16[2,192,768]{2,1,0:T(8,128)(2,1)S(1)}, bf16[2,192,768]{2,1,0:T(8,128)(2,1)S(1)}, u32[]{:S(2)}, u32[]{:S(2)}) collective-permute-start(bf16[2,192,768]{2,1,0:T(8,128)(2,1)S(1)} %constant_dynamic-update-slice_fusion.own_ref), channel_id=1, source_target_pairs={{0,1},{1,0},{2,3},{3,2},{4,5},{5,4},{6,7},{7,6},{8,9},{9,8},{10,11... | collective-permute-start | bytes 1769480 | tf_op jit(solution)/shard_map/ppermute | solution.py:344
  3.7 12.1 %collective-permute-start = (f32[584,128]{1,0:T(8,128)S(1)}, f32[584,128]{1,0:T(8,128)S(1)}, u32[]{:S(2)}, u32[]{:S(2)}) collective-permute-start(f32[584,128]{1,0:T(8,128)S(1)} %get-tuple-element.53), channel_id=1, source_target_pairs={{0,1},{1,0},{2,3},{3,2},{4,5},{5,4},{6,7},{7,6},{8,9},{9,8},{10,11... | collective-permute-start | bytes 897032 | tf_op jit(solution)/shard_map/ppermute | solution.py:344
  3.9 10.2 %collective-permute-start.2 = (f32[576,128]{1,0:T(8,128)S(1)}, f32[576,128]{1,0:T(8,128)S(1)}, u32[]{:S(2)}, u32[]{:S(2)}) collective-permute-start(f32[576,128]{1,0:T(8,128)S(1)} %add.7), channel_id=1, source_target_pairs={{0,2},{1,3},{2,0},{3,1},{4,6},{5,7},{6,4},{7,5},{8,10},{9,11},{10,... | collective-permute-start | bytes 884744 | tf_op jit(solution)/shard_map/ppermute | solution.py:344
  14.1 23.1 %collective-permute-start.16 = (bf16[2,192,384]{2,1,0:T(8,128)(2,1)S(1)}, bf16[2,192,384]{2,1,0:T(8,128)(2,1)S(1)}, u32[]{:S(2)}, u32[]{:S(2)}) collective-permute-start(bf16[2,192,384]{2,1,0:T(8,128)(2,1)S(1)} %constant_dynamic-slice_fusion), channel_id=1, source_target_pairs={{0,2},{1,3},{2,0},{3,1},{4,6},{5,7},{6,4},{7,5},{8,10},{9,11},{10,... | collective-permute-start | bytes 884744 | tf_op jit(solution)/shard_map/ppermute | solution.py:344
  16.8 6.2 %collective-permute-start.9 = (f32[152,128]{1,0:T(8,128)S(1)}, f32[152,128]{1,0:T(8,128)S(1)}, u32[]{:S(2)}, u32[]{:S(2)}) collective-permute-start(f32[152,128]{1,0:T(8,128)S(1)} %get-tuple-element.62), channel_id=1, source_target_pairs={{0,4},{4,0},{8,12},{12,8},{16,20},{20,16},{24,28},{28,24},{1,5},{5... | collective-permute-start | bytes 233480 | tf_op jit(solution)/shard_map/ppermute | solution.py:344
  18.4 7.3 %collective-permute-start.10 = (f32[152,128]{1,0:T(8,128)S(1)}, f32[152,128]{1,0:T(8,128)S(1)}, u32[]{:S(2)}, u32[]{:S(2)}) collective-permute-start(f32[152,128]{1,0:T(8,128)S(1)} %get-tuple-element.63), channel_id=1, source_target_pairs={{0,8},{4,12},{8,0},{12,4},{16,24},{20,28},{24,16},{28,20},{1,9},{5... | collective-permute-start | bytes 233480 | tf_op jit(solution)/shard_map/ppermute | solution.py:344
  20.0 8.0 %collective-permute-start.11 = (f32[152,128]{1,0:T(8,128)S(1)}, f32[152,128]{1,0:T(8,128)S(1)}, u32[]{:S(2)}, u32[]{:S(2)}) collective-permute-start(f32[152,128]{1,0:T(8,128)S(1)} %get-tuple-element.64), channel_id=1, source_target_pairs={{0,12},{4,8},{8,4},{12,0},{16,28},{20,24},{24,20},{28,16},{1,13},{... | collective-permute-start | bytes 233480 | tf_op jit(solution)/shard_map/ppermute | solution.py:344
  20.4 9.2 %collective-permute-start.4 = (f32[152,128]{1,0:T(8,128)S(1)}, f32[152,128]{1,0:T(8,128)S(1)}, u32[]{:S(2)}, u32[]{:S(2)}) collective-permute-start(f32[152,128]{1,0:T(8,128)S(1)} %get-tuple-element.57), channel_id=1, source_target_pairs={{0,16},{4,20},{8,24},{12,28},{16,0},{20,4},{24,8},{28,12},{1,17},{... | collective-permute-start | bytes 233480 | tf_op jit(solution)/shard_map/ppermute | solution.py:344
  23.0 12.6 %collective-permute-start.5 = (f32[152,128]{1,0:T(8,128)S(1)}, f32[152,128]{1,0:T(8,128)S(1)}, u32[]{:S(2)}, u32[]{:S(2)}) collective-permute-start(f32[152,128]{1,0:T(8,128)S(1)} %get-tuple-element.58), channel_id=1, source_target_pairs={{0,20},{4,16},{8,28},{12,24},{16,4},{20,0},{24,12},{28,8},{1,21},{... | collective-permute-start | bytes 233480 | tf_op jit(solution)/shard_map/ppermute | solution.py:344
  25.7 9.9 %collective-permute-start.6 = (f32[152,128]{1,0:T(8,128)S(1)}, f32[152,128]{1,0:T(8,128)S(1)}, u32[]{:S(2)}, u32[]{:S(2)}) collective-permute-start(f32[152,128]{1,0:T(8,128)S(1)} %get-tuple-element.59), channel_id=1, source_target_pairs={{0,24},{4,28},{8,16},{12,20},{16,8},{20,12},{24,0},{28,4},{1,25},{... | collective-permute-start | bytes 233480 | tf_op jit(solution)/shard_map/ppermute | solution.py:344
  28.0 8.6 %collective-permute-start.7 = (f32[152,128]{1,0:T(8,128)S(1)}, f32[152,128]{1,0:T(8,128)S(1)}, u32[]{:S(2)}, u32[]{:S(2)}) collective-permute-start(f32[152,128]{1,0:T(8,128)S(1)} %get-tuple-element.60), channel_id=1, source_target_pairs={{0,28},{4,24},{8,20},{12,16},{16,12},{20,8},{24,4},{28,0},{1,29},{... | collective-permute-start | bytes 233480 | tf_op jit(solution)/shard_map/ppermute | solution.py:344
  29.5 9.9 %copy-start.6 = (f32[4,96]{1,0:T(4,128)S(1)}, f32[4,96]{1,0:T(4,128)}, u32[]{:S(2)}) copy-start(f32[4,96]{1,0:T(4,128)} %m_ref.1) | copy-start | bytes 4612
  29.5 9.9 %copy-start.7 = (f32[4,96]{1,0:T(4,128)S(1)}, f32[4,96]{1,0:T(4,128)}, u32[]{:S(2)}) copy-start(f32[4,96]{1,0:T(4,128)} %v_ref.3) | copy-start | bytes 4612
  29.6 7.0 %collective-permute-start.13 = (f32[616,128]{1,0:T(8,128)S(1)}, f32[616,128]{1,0:T(8,128)S(1)}, u32[]{:S(2)}, u32[]{:S(2)}) collective-permute-start(f32[616,128]{1,0:T(8,128)S(1)} %constant_dynamic-update-slice_fusion.6.mine_ref), channel_id=1, source_target_pairs={{0,2},{1,3},{2,0},{3,1},{4,6},{5,7},{6,4},{7,5},{8,10},{9,11},{10,... | collective-permute-start | bytes 946184 | tf_op jit(solution)/shard_map/ppermute | solution.py:344
  35.6 3.8 %collective-permute-start.12 = (f32[616,128]{1,0:T(8,128)S(1)}, f32[616,128]{1,0:T(8,128)S(1)}, u32[]{:S(2)}, u32[]{:S(2)}) collective-permute-start(f32[616,128]{1,0:T(8,128)S(1)} %constant_dynamic-update-slice_fusion.6.mine_ref), channel_id=1, source_target_pairs={{0,1},{1,0},{2,3},{3,2},{4,5},{5,4},{6,7},{7,6},{8,9},{9,8},{10,11... | collective-permute-start | bytes 946184 | tf_op jit(solution)/shard_map/ppermute | solution.py:344
  36.6 2.8 %collective-permute-start.14 = (f32[616,128]{1,0:T(8,128)S(1)}, f32[616,128]{1,0:T(8,128)S(1)}, u32[]{:S(2)}, u32[]{:S(2)}) collective-permute-start(f32[616,128]{1,0:T(8,128)S(1)} %collective-permute-done.13.chip_ref), channel_id=1, source_target_pairs={{0,1},{1,0},{2,3},{3,2},{4,5},{5,4},{6,7},{7,6},{8,9},{9,8},{10,11... | collective-permute-start | bytes 946184 | tf_op jit(solution)/shard_map/ppermute | solution.py:344
  36.6 2.8 %collective-permute-start.15 = (f32[608,128]{1,0:T(8,128)S(1)}, f32[608,128]{1,0:T(8,128)S(1)}, u32[]{:S(2)}, u32[]{:S(2)}) collective-permute-start(f32[608,128]{1,0:T(8,128)S(1)} %constant_dynamic-update-slice_fusion.2.far_ref), channel_id=1, source_target_pairs={{0,1},{1,0},{2,3},{3,2},{4,5},{5,4},{6,7},{7,6},{8,9},{9,8},{10,11... | collective-permute-start | bytes 933896 | tf_op jit(solution)/shard_map/ppermute | solution.py:344
  37.2 1.9 %collective-permute-start.17 = (bf16[2,192,384]{2,1,0:T(8,128)(2,1)S(1)}, bf16[2,192,384]{2,1,0:T(8,128)(2,1)S(1)}, u32[]{:S(2)}, u32[]{:S(2)}) collective-permute-start(bf16[2,192,384]{2,1,0:T(8,128)(2,1)S(1)} %collective-permute-done.16.chip_ref), channel_id=1, source_target_pairs={{0,1},{1,0},{2,3},{3,2},{4,5},{5,4},{6,7},{7,6},{8,9},{9,8},{10,11... | collective-permute-start | bytes 884744 | tf_op jit(solution)/shard_map/ppermute | solution.py:344
  37.3 9.7 %collective-permute-start.8 = (f32[608,128]{1,0:T(8,128)S(1)}, f32[608,128]{1,0:T(8,128)S(1)}, u32[]{:S(2)}, u32[]{:S(2)}) collective-permute-start(f32[608,128]{1,0:T(8,128)S(1)} %constant_dynamic-update-slice_fusion.2.far_ref), channel_id=1, source_target_pairs={{0,2},{1,3},{2,0},{3,1},{4,6},{5,7},{6,4},{7,5},{8,10},{9,11},{10,... | collective-permute-start | bytes 933896 | tf_op jit(solution)/shard_map/ppermute | solution.py:344
  47.0 1.6 %collective-permute-start.18 = (f32[608,128]{1,0:T(8,128)S(1)}, f32[608,128]{1,0:T(8,128)S(1)}, u32[]{:S(2)}, u32[]{:S(2)}) collective-permute-start(f32[608,128]{1,0:T(8,128)S(1)} %collective-permute-done.8.chip_ref), channel_id=1, source_target_pairs={{0,1},{1,0},{2,3},{3,2},{4,5},{5,4},{6,7},{7,6},{8,9},{9,8},{10,11... | collective-permute-start | bytes 933896 | tf_op jit(solution)/shard_map/ppermute | solution.py:344
  48.6 14.9 %copy-start.4 = (f32[1,192,768]{2,1,0:T(8,128)S(1)}, f32[1,192,768]{2,1,0:T(8,128)}, u32[]{:S(2)}) copy-start(f32[1,192,768]{2,1,0:T(8,128)} %left_ref.1) | copy-start | bytes 1769476
  48.6 14.9 %copy-start.5 = (f32[1,192,768]{2,1,0:T(8,128)S(1)}, f32[1,192,768]{2,1,0:T(8,128)}, u32[]{:S(2)}) copy-start(f32[1,192,768]{2,1,0:T(8,128)} %right_ref.1) | copy-start | bytes 1769476
  51.1 9.4 %collective-permute-start.19 = (f32[144,128]{1,0:T(8,128)S(1)}, f32[144,128]{1,0:T(8,128)S(1)}, u32[]{:S(2)}, u32[]{:S(2)}) collective-permute-start(f32[144,128]{1,0:T(8,128)S(1)} %get-tuple-element.77), channel_id=1, source_target_pairs={{0,16},{4,20},{8,24},{12,28},{16,0},{20,4},{24,8},{28,12},{1,17},{... | collective-permute-start | bytes 221192 | tf_op jit(solution)/shard_map/ppermute | solution.py:344
  52.9 9.3 %collective-permute-start.20 = (f32[144,128]{1,0:T(8,128)S(1)}, f32[144,128]{1,0:T(8,128)S(1)}, u32[]{:S(2)}, u32[]{:S(2)}) collective-permute-start(f32[144,128]{1,0:T(8,128)S(1)} %get-tuple-element.78), channel_id=1, source_target_pairs={{0,4},{4,0},{8,12},{12,8},{16,20},{20,16},{24,28},{28,24},{1,5},{5... | collective-permute-start | bytes 221192 | tf_op jit(solution)/shard_map/ppermute | solution.py:344
  55.2 12.3 %collective-permute-start.21 = (f32[144,128]{1,0:T(8,128)S(1)}, f32[144,128]{1,0:T(8,128)S(1)}, u32[]{:S(2)}, u32[]{:S(2)}) collective-permute-start(f32[144,128]{1,0:T(8,128)S(1)} %get-tuple-element.79), channel_id=1, source_target_pairs={{0,20},{4,16},{8,28},{12,24},{16,4},{20,0},{24,12},{28,8},{1,21},{... | collective-permute-start | bytes 221192 | tf_op jit(solution)/shard_map/ppermute | solution.py:344
  57.5 10.1 %collective-permute-start.22 = (f32[144,128]{1,0:T(8,128)S(1)}, f32[144,128]{1,0:T(8,128)S(1)}, u32[]{:S(2)}, u32[]{:S(2)}) collective-permute-start(f32[144,128]{1,0:T(8,128)S(1)} %get-tuple-element.80), channel_id=1, source_target_pairs={{0,8},{4,12},{8,0},{12,4},{16,24},{20,28},{24,16},{28,20},{1,9},{5... | collective-permute-start | bytes 221192 | tf_op jit(solution)/shard_map/ppermute | solution.py:344
  58.3 9.3 %collective-permute-start.23 = (f32[144,128]{1,0:T(8,128)S(1)}, f32[144,128]{1,0:T(8,128)S(1)}, u32[]{:S(2)}, u32[]{:S(2)}) collective-permute-start(f32[144,128]{1,0:T(8,128)S(1)} %get-tuple-element.81), channel_id=1, source_target_pairs={{0,24},{4,28},{8,16},{12,20},{16,8},{20,12},{24,0},{28,4},{1,25},{... | collective-permute-start | bytes 221192 | tf_op jit(solution)/shard_map/ppermute | solution.py:344
  60.5 7.4 %collective-permute-start.24 = (f32[144,128]{1,0:T(8,128)S(1)}, f32[144,128]{1,0:T(8,128)S(1)}, u32[]{:S(2)}, u32[]{:S(2)}) collective-permute-start(f32[144,128]{1,0:T(8,128)S(1)} %get-tuple-element.82), channel_id=1, source_target_pairs={{0,12},{4,8},{8,4},{12,0},{16,28},{20,24},{24,20},{28,16},{1,13},{... | collective-permute-start | bytes 221192 | tf_op jit(solution)/shard_map/ppermute | solution.py:344
  62.2 7.2 %collective-permute-start.25 = (f32[144,128]{1,0:T(8,128)S(1)}, f32[144,128]{1,0:T(8,128)S(1)}, u32[]{:S(2)}, u32[]{:S(2)}) collective-permute-start(f32[144,128]{1,0:T(8,128)S(1)} %get-tuple-element.83), channel_id=1, source_target_pairs={{0,28},{4,24},{8,20},{12,16},{16,12},{20,8},{24,4},{28,0},{1,29},{... | collective-permute-start | bytes 221192 | tf_op jit(solution)/shard_map/ppermute | solution.py:344

commit v4 on v3

--- a/solution.py
+++ b/solution.py
@@ -374,13 +374,15 @@
     outgoing, (adam_new, vec_pair) = res[:shards], res[shards:]
 
     arrived = [outgoing[0]] + [swap(outgoing[j], "shard", j) for j in range(1, shards)]
+    crossing, vec_pair = lax.optimization_barrier((crossing, vec_pair))
     roots_chip = swap(crossing, "tensor", 2)
+    near = jnp.concatenate([*arrived[: shards // 2], vec_pair], axis=0)
+    far = jnp.concatenate(arrived[shards // 2 :], axis=0)
+    near, roots_chip = lax.optimization_barrier((near, roots_chip))
     full = shape((size, size), BF16)
     left_full, right_full = kernel_call(
         roots_kernel, (full, full), (roots, roots_core, roots_chip, swap(roots_chip, "tensor", 1)), mib=24
     )
-    near = jnp.concatenate([*arrived[: shards // 2], vec_pair], axis=0)
-    far = jnp.concatenate(arrived[shards // 2 :], axis=0)
     near_across = swap(near, "tensor", 2)
     near = near, swap(near, "tensor", 1), near_across, swap(near_across, "tensor", 1)
     far_across = swap(far, "tensor", 2)

time: 71.3 us -> 68.9 us (0.966)
  waiting for transfers between devices: 21.8 us -> 19.6 us
    ppermute x26, waiting for transfers between devices: 21.8 us -> 19.6 us  [swap(): lax.ppermute(a, axis, [(i, i ^ mask) for i in range(lax.axis_size(axis))])]
  transfers between devices with their start and end apart: 26 -> 26, of which waited for: 8 -> 7; matrix products, arithmetic and copies ran while one was open for 0% -> 0% of each run, Pallas kernels for 13% -> 12%
where the time goes in v4:
time: 68.9 us; the launch traced here: 68.8 us
  starting transfers between devices  32.6 us (47%)
  waiting for transfers between devices  19.6 us (28%)
  Pallas kernels  14 us (20%)
  local copies, waits for them, and re-layouts  1.76 us (3%)
  between operations  0.86 us (1%)
    ppermute x26, starting transfers between devices, swap(): lax.ppermute(a, axis, [(i, i ^ mask) for i in range(lax.axis_size(axis))])  32.6 us
    ppermute x26, waiting for transfers between devices, swap(): lax.ppermute(a, axis, [(i, i ^ mask) for i in range(lax.axis_size(axis))])  19.6 us
    pallas_call x8, Pallas kernels, kernel_call(): pl.pallas_call(body, out_shape=outs, in_specs=[pl.BlockSpec(memory_space=...  14 us
    unnamed x28, local copies, waits for them, and re-layouts  1.7 us
  transfers between devices with their start and end apart: 26, of which 7 were waited for; matrix products, arithmetic and copies ran while one was open for 0% of the time, Pallas kernels for 12%

profile of v4, /device:TPU:0, one launch (start us, length us, event | category | flops | bytes accessed | tf_op | source)
XLA Modules:
  0.0 68.8 jit_solution(6313239935465748525)
XLA Ops:
  0.6 1.3 %copy-done = f32[1,4,96,768]{3,2,1,0:T(8,128)S(1)} copy-done((f32[1,4,96,768]{3,2,1,0:T(8,128)S(1)}, f32[1,4,96,768]{3,2,1,0:T(8,128)}, u32[]{:S(2)}) %copy-start) | copy-done | bytes 1179672
  1.9 0.2 shard_map.154
  2.1 0.5 collective-permute-start.1
  2.6 0.3 copy-done.8
  2.9 0.1 copy-done.9
  3.0 0.0 copy-start.1
  3.0 0.0 copy-start.2
  3.0 0.5 collective-permute-start.3
  3.5 0.2 shard_map.153
  3.7 0.1 collective-permute-start
  3.8 0.0 collective-permute-done.1
  3.9 3.0 %collective-permute-start.2 = (f32[576,128]{1,0:T(8,128)S(1)}, f32[576,128]{1,0:T(8,128)S(1)}, u32[]{:S(2)}, u32[]{:S(2)}) collective-permute-start(f32[576,128]{1,0:T(8,128)S(1)} %add.7), channel_id=1, source_target_pairs={{0,2},{1,3},{2,0},{3,1},{4,6},{5,7},{6,4},{7,5},{8,10},{9,11},{10,... | collective-permute-start | bytes 884744 | tf_op jit(solution)/shard_map/ppermute | solution.py:344
  6.9 7.2 %collective-permute-done.2.r_ref = f32[576,128]{1,0:T(8,128)S(1)} collective-permute-done((f32[576,128]{1,0:T(8,128)S(1)}, f32[576,128]{1,0:T(8,128)S(1)}, u32[]{:S(2)}, u32[]{:S(2)}) %collective-permute-start.2) | collective-permute-done | bytes 294944 | tf_op jit(solution)/shard_map/ppermute | solution.py:344
  14.1 0.0 collective-permute-done.rn_ref
  14.1 1.0 %shard_map.155 = (f32[152,128]{1,0:T(8,128)S(1)}, f32[152,128]{1,0:T(8,128)S(1)}, f32[152,128]{1,0:T(8,128)S(1)}, f32[152,128]{1,0:T(8,128)S(1)}, f32[152,128]{1...) custom-call(s32[4]{0:T(128)S(1)} %copy-done.2, ...), custom_call_target="tpu_custom_call" | custom-call | bytes 2109456 | tf_op jit(solution)/shard_map/pallas_call | solution.py:332
  15.1 1.8 %collective-permute-start.9 = (f32[152,128]{1,0:T(8,128)S(1)}, f32[152,128]{1,0:T(8,128)S(1)}, u32[]{:S(2)}, u32[]{:S(2)}) collective-permute-start(f32[152,128]{1,0:T(8,128)S(1)} %get-tuple-element.66), channel_id=1, source_target_pairs={{0,4},{4,0},{8,12},{12,8},{16,20},{20,16},{24,28},{28,24},{1,5},{5... | collective-permute-start | bytes 233480 | tf_op jit(solution)/shard_map/ppermute | solution.py:344
  16.9 1.6 %collective-permute-start.10 = (f32[152,128]{1,0:T(8,128)S(1)}, f32[152,128]{1,0:T(8,128)S(1)}, u32[]{:S(2)}, u32[]{:S(2)}) collective-permute-start(f32[152,128]{1,0:T(8,128)S(1)} %get-tuple-element.67), channel_id=1, source_target_pairs={{0,8},{4,12},{8,0},{12,4},{16,24},{20,28},{24,16},{28,20},{1,9},{5... | collective-permute-start | bytes 233480 | tf_op jit(solution)/shard_map/ppermute | solution.py:344
  18.5 0.1 collective-permute-start.11
  18.6 1.7 %collective-permute-start.12 = (bf16[2,192,384]{2,1,0:T(8,128)(2,1)S(1)}, bf16[2,192,384]{2,1,0:T(8,128)(2,1)S(1)}, u32[]{:S(2)}, u32[]{:S(2)}) collective-permute-start(bf16[2,192,384]{2,1,0:T(8,128)(2,1)S(1)} %constant_dynamic-slice_fusion), channel_id=1, source_target_pairs={{0,2},{1,3},{2,0},{3,1},{4,6},{5,7},{6,4},{7,5},{8,10},{9,11},{10,... | collective-permute-start | bytes 884744 | tf_op jit(solution)/shard_map/ppermute | solution.py:344
  20.4 2.6 %collective-permute-start.4 = (f32[152,128]{1,0:T(8,128)S(1)}, f32[152,128]{1,0:T(8,128)S(1)}, u32[]{:S(2)}, u32[]{:S(2)}) collective-permute-start(f32[152,128]{1,0:T(8,128)S(1)} %get-tuple-element.61), channel_id=1, source_target_pairs={{0,16},{4,20},{8,24},{12,28},{16,0},{20,4},{24,8},{28,12},{1,17},{... | collective-permute-start | bytes 233480 | tf_op jit(solution)/shard_map/ppermute | solution.py:344
  23.0 1.4 %collective-permute-start.5 = (f32[152,128]{1,0:T(8,128)S(1)}, f32[152,128]{1,0:T(8,128)S(1)}, u32[]{:S(2)}, u32[]{:S(2)}) collective-permute-start(f32[152,128]{1,0:T(8,128)S(1)} %get-tuple-element.62), channel_id=1, source_target_pairs={{0,20},{4,16},{8,28},{12,24},{16,4},{20,0},{24,12},{28,8},{1,21},{... | collective-permute-start | bytes 233480 | tf_op jit(solution)/shard_map/ppermute | solution.py:344
  24.3 3.7 %collective-permute-start.6 = (f32[152,128]{1,0:T(8,128)S(1)}, f32[152,128]{1,0:T(8,128)S(1)}, u32[]{:S(2)}, u32[]{:S(2)}) collective-permute-start(f32[152,128]{1,0:T(8,128)S(1)} %get-tuple-element.63), channel_id=1, source_target_pairs={{0,24},{4,28},{8,16},{12,20},{16,8},{20,12},{24,0},{28,4},{1,25},{... | collective-permute-start | bytes 233480 | tf_op jit(solution)/shard_map/ppermute | solution.py:344
  28.0 0.2 collective-permute-start.7
  28.3 0.0 copy-start.6
  28.3 0.0 copy-start.7
  28.3 1.1 %collective-permute-start.14 = (f32[616,128]{1,0:T(8,128)S(1)}, f32[616,128]{1,0:T(8,128)S(1)}, u32[]{:S(2)}, u32[]{:S(2)}) collective-permute-start(f32[616,128]{1,0:T(8,128)S(1)} %constant_dynamic-update-slice_fusion.6.mine_ref), channel_id=1, source_target_pairs={{0,2},{1,3},{2,0},{3,1},{4,6},{5,7},{6,4},{7,5},{8,10},{9,11},{10,... | collective-permute-start | bytes 946184 | tf_op jit(solution)/shard_map/ppermute | solution.py:344
  29.4 4.7 %collective-permute-done.5 = f32[152,128]{1,0:T(8,128)S(1)} collective-permute-done((f32[152,128]{1,0:T(8,128)S(1)}, f32[152,128]{1,0:T(8,128)S(1)}, u32[]{:S(2)}, u32[]{:S(2)}) %collective-permute-start.5) | collective-permute-done | bytes 77856 | tf_op jit(solution)/shard_map/ppermute | solution.py:344
  34.1 0.1 collective-permute-start.13
  34.2 1.1 %collective-permute-done.14.chip_ref = f32[616,128]{1,0:T(8,128)S(1)} collective-permute-done((f32[616,128]{1,0:T(8,128)S(1)}, f32[616,128]{1,0:T(8,128)S(1)}, u32[]{:S(2)}, u32[]{:S(2)}) %collective-permute-start.14) | collective-permute-done | bytes 315424 | tf_op jit(solution)/shard_map/ppermute | solution.py:344
  35.3 0.6 collective-permute-start.16
  35.9 0.1 collective-permute-start.17
  36.0 1.0 %collective-permute-start.8 = (f32[608,128]{1,0:T(8,128)S(1)}, f32[608,128]{1,0:T(8,128)S(1)}, u32[]{:S(2)}, u32[]{:S(2)}) collective-permute-start(f32[608,128]{1,0:T(8,128)S(1)} %constant_dynamic-update-slice_fusion.2.far_ref), channel_id=1, source_target_pairs={{0,2},{1,3},{2,0},{3,1},{4,6},{5,7},{6,4},{7,5},{8,10},{9,11},{10,... | collective-permute-start | bytes 933896 | tf_op jit(solution)/shard_map/ppermute | solution.py:344
  37.0 0.8 %collective-permute-done.17.both_ref = bf16[2,192,384]{2,1,0:T(8,128)(2,1)S(1)} collective-permute-done((bf16[2,192,384]{2,1,0:T(8,128)(2,1)S(1)}, bf16[2,192,384]{2,1,0:T(8,128)(2,1)S(1)}, u32[]{:S(2)}, u32[]{:S(2)}) %collective-permute-start.17) | collective-permute-done | bytes 294944 | tf_op jit(solution)/shard_map/ppermute | solution.py:344
  37.8 0.3 shard_map.156
  38.1 4.0 %shard_map.157 = (bf16[384,768]{1,0:T(8,128)(2,1)S(1)}, bf16[384,768]{1,0:T(8,128)(2,1)S(1)}, bf16[384,384]{1,0:T(8,128)(2,1)S(1)}, bf16[384,384]{1,0:T(8,128)(2...) custom-call(f32[616,128]{1,0:T(8,128)S(1)} %constant_dynamic-update-, ...), custom_call_target="tpu_custom_call" | custom-call | flops 2264924160 | bytes 10153472 | tf_op jit(solution)/shard_map/pallas_call | solution.py:332
  42.2 3.5 %collective-permute-done.8.chip_ref = f32[608,128]{1,0:T(8,128)S(1)} collective-permute-done((f32[608,128]{1,0:T(8,128)S(1)}, f32[608,128]{1,0:T(8,128)S(1)}, u32[]{:S(2)}, u32[]{:S(2)}) %collective-permute-start.8) | collective-permute-done | bytes 311328 | tf_op jit(solution)/shard_map/ppermute | solution.py:344
  45.7 1.6 %collective-permute-done.18.both_ref = f32[608,128]{1,0:T(8,128)S(1)} collective-permute-done((f32[608,128]{1,0:T(8,128)S(1)}, f32[608,128]{1,0:T(8,128)S(1)}, u32[]{:S(2)}, u32[]{:S(2)}) %collective-permute-start.18) | collective-permute-done | bytes 311328 | tf_op jit(solution)/shard_map/ppermute | solution.py:344
  47.3 2.5 %shard_map.158 = (bf16[384,384]{1,0:T(8,128)(2,1)S(1)}, bf16[384,384]{1,0:T(8,128)(2,1)S(1)}, f32[144,128]{1,0:T(8,128)S(1)}, f32[144,128]{1,0:T(8,128)S(1)}, f3...) custom-call(f32[608,128]{1,0:T(8,128)S(1)} %collective-permute-done., ...), custom_call_target="tpu_custom_call" | custom-call | flops 1358954496 | bytes 7704576 | tf_op jit(solution)/shard_map/pallas_call | solution.py:332
  49.8 3.1 %collective-permute-start.19 = (f32[144,128]{1,0:T(8,128)S(1)}, f32[144,128]{1,0:T(8,128)S(1)}, u32[]{:S(2)}, u32[]{:S(2)}) collective-permute-start(f32[144,128]{1,0:T(8,128)S(1)} %get-tuple-element.85), channel_id=1, source_target_pairs={{0,16},{4,20},{8,24},{12,28},{16,0},{20,4},{24,8},{28,12},{1,17},{... | collective-permute-start | bytes 221192 | tf_op jit(solution)/shard_map/ppermute | solution.py:344
  52.9 0.6 collective-permute-start.20
  53.5 1.0 %collective-permute-start.21 = (f32[144,128]{1,0:T(8,128)S(1)}, f32[144,128]{1,0:T(8,128)S(1)}, u32[]{:S(2)}, u32[]{:S(2)}) collective-permute-start(f32[144,128]{1,0:T(8,128)S(1)} %get-tuple-element.87), channel_id=1, source_target_pairs={{0,20},{4,16},{8,28},{12,24},{16,4},{20,0},{24,12},{28,8},{1,21},{... | collective-permute-start | bytes 221192 | tf_op jit(solution)/shard_map/ppermute | solution.py:344
  54.5 1.5 %collective-permute-start.22 = (f32[144,128]{1,0:T(8,128)S(1)}, f32[144,128]{1,0:T(8,128)S(1)}, u32[]{:S(2)}, u32[]{:S(2)}) collective-permute-start(f32[144,128]{1,0:T(8,128)S(1)} %get-tuple-element.88), channel_id=1, source_target_pairs={{0,8},{4,12},{8,0},{12,4},{16,24},{20,28},{24,16},{28,20},{1,9},{5... | collective-permute-start | bytes 221192 | tf_op jit(solution)/shard_map/ppermute | solution.py:344
  55.9 2.8 %collective-permute-start.23 = (f32[144,128]{1,0:T(8,128)S(1)}, f32[144,128]{1,0:T(8,128)S(1)}, u32[]{:S(2)}, u32[]{:S(2)}) collective-permute-start(f32[144,128]{1,0:T(8,128)S(1)} %get-tuple-element.89), channel_id=1, source_target_pairs={{0,24},{4,28},{8,16},{12,20},{16,8},{20,12},{24,0},{28,4},{1,25},{... | collective-permute-start | bytes 221192 | tf_op jit(solution)/shard_map/ppermute | solution.py:344
  58.8 1.2 %collective-permute-start.24 = (f32[144,128]{1,0:T(8,128)S(1)}, f32[144,128]{1,0:T(8,128)S(1)}, u32[]{:S(2)}, u32[]{:S(2)}) collective-permute-start(f32[144,128]{1,0:T(8,128)S(1)} %get-tuple-element.90), channel_id=1, source_target_pairs={{0,12},{4,8},{8,4},{12,0},{16,28},{20,24},{24,20},{28,16},{1,13},{... | collective-permute-start | bytes 221192 | tf_op jit(solution)/shard_map/ppermute | solution.py:344
  60.0 2.4 %collective-permute-start.25 = (f32[144,128]{1,0:T(8,128)S(1)}, f32[144,128]{1,0:T(8,128)S(1)}, u32[]{:S(2)}, u32[]{:S(2)}) collective-permute-start(f32[144,128]{1,0:T(8,128)S(1)} %get-tuple-element.91), channel_id=1, source_target_pairs={{0,28},{4,24},{8,20},{12,16},{16,12},{20,8},{24,4},{28,0},{1,29},{... | collective-permute-start | bytes 221192 | tf_op jit(solution)/shard_map/ppermute | solution.py:344
  62.4 4.1 %shard_map.160 = (f32[1,192,768]{2,1,0:T(8,128)}, f32[1,192,768]{2,1,0:T(8,128)}) custom-call(s32[4]{0:T(128)S(1)} %copy-done.2, bf16[384,768]{1,0:T(8,128)(2,1)S(1)} %get-tuple-element.94.ah_ref, bf16[384,768]{1,0:T(8,128)(2,1)S(1)} %get-tuple-element.95.al_ref, bf16[384,384]{1,0:T(8,128)(2,1)S(1)} %get-tuple-element.96.bh_ref, ...), custom_call_target="tpu_custom_call" | custom-call | flops 1358954496 | bytes 4718608 | tf_op jit(solution)/shard_map/pallas_call | solution.py:332
  66.5 0.6 collective-permute-done.25.refs_6_
  67.0 1.7 %shard_map.159 = f32[4,96,192]{2,1,0:T(8,128)} custom-call(s32[4]{0:T(128)S(1)} %copy-done.2, f32[144,128]{1,0:T(8,128)S(1)} %collective-permute-done.19.refs_0_, f32[144,128]{1,0:T(8,128)S(1)} %collective-permute-done.20.refs_1_, f32[144,128]{1,0:T(8,128)S(1)} %collective-permute-done.21.refs_2_, f32[144,128]{1,0:T(8,128)S(1)} %collective-permute-done.22.refs_3_, ...), custom_call_target="tpu_custom_call" | custom-call | bytes 884752 | tf_op jit(solution)/shard_map/pallas_call | solution.py:332
  (45 shorter events, 0.2 us)
Async XLA Ops:
  0.6 1.3 %copy-start = (f32[1,4,96,768]{3,2,1,0:T(8,128)S(1)}, f32[1,4,96,768]{3,2,1,0:T(8,128)}, u32[]{:S(2)}) copy-start(f32[1,4,96,768]{3,2,1,0:T(8,128)} %g_ref.3) | copy-start | bytes 3538948
  1.9 1.0 %copy-start.8 = (bf16[1,192,768]{2,1,0:T(8,128)(2,1)S(1)}, bf16[1,192,768]{2,1,0:T(8,128)(2,1)}, u32[]{:S(2)}) copy-start(bf16[1,192,768]{2,1,0:T(8,128)(2,1)} %param.14) | copy-start | bytes 884740
  1.9 1.0 %copy-start.9 = (bf16[1,192,768]{2,1,0:T(8,128)(2,1)S(1)}, bf16[1,192,768]{2,1,0:T(8,128)(2,1)}, u32[]{:S(2)}) copy-start(bf16[1,192,768]{2,1,0:T(8,128)(2,1)} %param.15) | copy-start | bytes 884740
  1.9 1.6 %copy-start.3 = (f32[1,4,96]{2,1,0:T(4,128)S(1)}, f32[1,4,96]{2,1,0:T(4,128)}, u32[]{:S(2)}) copy-start(f32[1,4,96]{2,1,0:T(4,128)} %refs_0_.1) | copy-start | bytes 4612
  2.1 1.7 %collective-permute-start.1 = (f32[576,128]{1,0:T(8,128)S(1)}, f32[576,128]{1,0:T(8,128)S(1)}, u32[]{:S(2)}, u32[]{:S(2)}) collective-permute-start(f32[576,128]{1,0:T(8,128)S(1)} %get-tuple-element.59), channel_id=1, source_target_pairs={{0,1},{1,0},{2,3},{3,2},{4,5},{5,4},{6,7},{7,6},{8,9},{9,8},{10,11... | collective-permute-start | bytes 884744 | tf_op jit(solution)/shard_map/ppermute | solution.py:344
  3.0 11.1 %copy-start.1 = (f32[4,96,192]{2,1,0:T(8,128)S(1)}, f32[4,96,192]{2,1,0:T(8,128)}, u32[]{:S(2)}) copy-start(f32[4,96,192]{2,1,0:T(8,128)} %v_ref.2) | copy-start | bytes 884740
  3.0 11.1 %copy-start.2 = (s32[4]{0:T(128)S(1)}, s32[4]{0:T(128)}, u32[]{:S(2)}) copy-start(s32[4]{0:T(128)} %owner_ref.5) | copy-start | bytes 52
  3.0 11.1 %collective-permute-start.3 = (bf16[2,192,768]{2,1,0:T(8,128)(2,1)S(1)}, bf16[2,192,768]{2,1,0:T(8,128)(2,1)S(1)}, u32[]{:S(2)}, u32[]{:S(2)}) collective-permute-start(bf16[2,192,768]{2,1,0:T(8,128)(2,1)S(1)} %constant_dynamic-update-slice_fusion.own_ref), channel_id=1, source_target_pairs={{0,1},{1,0},{2,3},{3,2},{4,5},{5,4},{6,7},{7,6},{8,9},{9,8},{10,11... | collective-permute-start | bytes 1769480 | tf_op jit(solution)/shard_map/ppermute | solution.py:344
  3.7 10.4 %collective-permute-start = (f32[584,128]{1,0:T(8,128)S(1)}, f32[584,128]{1,0:T(8,128)S(1)}, u32[]{:S(2)}, u32[]{:S(2)}) collective-permute-start(f32[584,128]{1,0:T(8,128)S(1)} %get-tuple-element.57), channel_id=1, source_target_pairs={{0,1},{1,0},{2,3},{3,2},{4,5},{5,4},{6,7},{7,6},{8,9},{9,8},{10,11... | collective-permute-start | bytes 897032 | tf_op jit(solution)/shard_map/ppermute | solution.py:344
  3.9 10.2 %collective-permute-start.2 = (f32[576,128]{1,0:T(8,128)S(1)}, f32[576,128]{1,0:T(8,128)S(1)}, u32[]{:S(2)}, u32[]{:S(2)}) collective-permute-start(f32[576,128]{1,0:T(8,128)S(1)} %add.7), channel_id=1, source_target_pairs={{0,2},{1,3},{2,0},{3,1},{4,6},{5,7},{6,4},{7,5},{8,10},{9,11},{10,... | collective-permute-start | bytes 884744 | tf_op jit(solution)/shard_map/ppermute | solution.py:344
  15.1 7.9 %collective-permute-start.9 = (f32[152,128]{1,0:T(8,128)S(1)}, f32[152,128]{1,0:T(8,128)S(1)}, u32[]{:S(2)}, u32[]{:S(2)}) collective-permute-start(f32[152,128]{1,0:T(8,128)S(1)} %get-tuple-element.66), channel_id=1, source_target_pairs={{0,4},{4,0},{8,12},{12,8},{16,20},{20,16},{24,28},{28,24},{1,5},{5... | collective-permute-start | bytes 233480 | tf_op jit(solution)/shard_map/ppermute | solution.py:344
  16.9 7.4 %collective-permute-start.10 = (f32[152,128]{1,0:T(8,128)S(1)}, f32[152,128]{1,0:T(8,128)S(1)}, u32[]{:S(2)}, u32[]{:S(2)}) collective-permute-start(f32[152,128]{1,0:T(8,128)S(1)} %get-tuple-element.67), channel_id=1, source_target_pairs={{0,8},{4,12},{8,0},{12,4},{16,24},{20,28},{24,16},{28,20},{1,9},{5... | collective-permute-start | bytes 233480 | tf_op jit(solution)/shard_map/ppermute | solution.py:344
  18.5 9.5 %collective-permute-start.11 = (f32[152,128]{1,0:T(8,128)S(1)}, f32[152,128]{1,0:T(8,128)S(1)}, u32[]{:S(2)}, u32[]{:S(2)}) collective-permute-start(f32[152,128]{1,0:T(8,128)S(1)} %get-tuple-element.68), channel_id=1, source_target_pairs={{0,12},{4,8},{8,4},{12,0},{16,28},{20,24},{24,20},{28,16},{1,13},{... | collective-permute-start | bytes 233480 | tf_op jit(solution)/shard_map/ppermute | solution.py:344
  18.6 9.7 %collective-permute-start.12 = (bf16[2,192,384]{2,1,0:T(8,128)(2,1)S(1)}, bf16[2,192,384]{2,1,0:T(8,128)(2,1)S(1)}, u32[]{:S(2)}, u32[]{:S(2)}) collective-permute-start(bf16[2,192,384]{2,1,0:T(8,128)(2,1)S(1)} %constant_dynamic-slice_fusion), channel_id=1, source_target_pairs={{0,2},{1,3},{2,0},{3,1},{4,6},{5,7},{6,4},{7,5},{8,10},{9,11},{10,... | collective-permute-start | bytes 884744 | tf_op jit(solution)/shard_map/ppermute | solution.py:344
  20.4 9.0 %collective-permute-start.4 = (f32[152,128]{1,0:T(8,128)S(1)}, f32[152,128]{1,0:T(8,128)S(1)}, u32[]{:S(2)}, u32[]{:S(2)}) collective-permute-start(f32[152,128]{1,0:T(8,128)S(1)} %get-tuple-element.61), channel_id=1, source_target_pairs={{0,16},{4,20},{8,24},{12,28},{16,0},{20,4},{24,8},{28,12},{1,17},{... | collective-permute-start | bytes 233480 | tf_op jit(solution)/shard_map/ppermute | solution.py:344
  23.0 11.1 %collective-permute-start.5 = (f32[152,128]{1,0:T(8,128)S(1)}, f32[152,128]{1,0:T(8,128)S(1)}, u32[]{:S(2)}, u32[]{:S(2)}) collective-permute-start(f32[152,128]{1,0:T(8,128)S(1)} %get-tuple-element.62), channel_id=1, source_target_pairs={{0,20},{4,16},{8,28},{12,24},{16,4},{20,0},{24,12},{28,8},{1,21},{... | collective-permute-start | bytes 233480 | tf_op jit(solution)/shard_map/ppermute | solution.py:344
  24.3 9.7 %collective-permute-start.6 = (f32[152,128]{1,0:T(8,128)S(1)}, f32[152,128]{1,0:T(8,128)S(1)}, u32[]{:S(2)}, u32[]{:S(2)}) collective-permute-start(f32[152,128]{1,0:T(8,128)S(1)} %get-tuple-element.63), channel_id=1, source_target_pairs={{0,24},{4,28},{8,16},{12,20},{16,8},{20,12},{24,0},{28,4},{1,25},{... | collective-permute-start | bytes 233480 | tf_op jit(solution)/shard_map/ppermute | solution.py:344
  28.0 7.3 %collective-permute-start.7 = (f32[152,128]{1,0:T(8,128)S(1)}, f32[152,128]{1,0:T(8,128)S(1)}, u32[]{:S(2)}, u32[]{:S(2)}) collective-permute-start(f32[152,128]{1,0:T(8,128)S(1)} %get-tuple-element.64), channel_id=1, source_target_pairs={{0,28},{4,24},{8,20},{12,16},{16,12},{20,8},{24,4},{28,0},{1,29},{... | collective-permute-start | bytes 233480 | tf_op jit(solution)/shard_map/ppermute | solution.py:344
  28.3 9.9 %copy-start.6 = (f32[4,96]{1,0:T(4,128)S(1)}, f32[4,96]{1,0:T(4,128)}, u32[]{:S(2)}) copy-start(f32[4,96]{1,0:T(4,128)} %m_ref.1) | copy-start | bytes 4612
  28.3 9.9 %copy-start.7 = (f32[4,96]{1,0:T(4,128)S(1)}, f32[4,96]{1,0:T(4,128)}, u32[]{:S(2)}) copy-start(f32[4,96]{1,0:T(4,128)} %v_ref.3) | copy-start | bytes 4612
  28.3 7.0 %collective-permute-start.14 = (f32[616,128]{1,0:T(8,128)S(1)}, f32[616,128]{1,0:T(8,128)S(1)}, u32[]{:S(2)}, u32[]{:S(2)}) collective-permute-start(f32[616,128]{1,0:T(8,128)S(1)} %constant_dynamic-update-slice_fusion.6.mine_ref), channel_id=1, source_target_pairs={{0,2},{1,3},{2,0},{3,1},{4,6},{5,7},{6,4},{7,5},{8,10},{9,11},{10,... | collective-permute-start | bytes 946184 | tf_op jit(solution)/shard_map/ppermute | solution.py:344
  34.1 4.0 %collective-permute-start.13 = (f32[616,128]{1,0:T(8,128)S(1)}, f32[616,128]{1,0:T(8,128)S(1)}, u32[]{:S(2)}, u32[]{:S(2)}) collective-permute-start(f32[616,128]{1,0:T(8,128)S(1)} %constant_dynamic-update-slice_fusion.6.mine_ref), channel_id=1, source_target_pairs={{0,1},{1,0},{2,3},{3,2},{4,5},{5,4},{6,7},{7,6},{8,9},{9,8},{10,11... | collective-permute-start | bytes 946184 | tf_op jit(solution)/shard_map/ppermute | solution.py:344
  35.3 2.8 %collective-permute-start.15 = (f32[616,128]{1,0:T(8,128)S(1)}, f32[616,128]{1,0:T(8,128)S(1)}, u32[]{:S(2)}, u32[]{:S(2)}) collective-permute-start(f32[616,128]{1,0:T(8,128)S(1)} %collective-permute-done.14.chip_ref), channel_id=1, source_target_pairs={{0,1},{1,0},{2,3},{3,2},{4,5},{5,4},{6,7},{7,6},{8,9},{9,8},{10,11... | collective-permute-start | bytes 946184 | tf_op jit(solution)/shard_map/ppermute | solution.py:344
  35.3 2.8 %collective-permute-start.16 = (f32[608,128]{1,0:T(8,128)S(1)}, f32[608,128]{1,0:T(8,128)S(1)}, u32[]{:S(2)}, u32[]{:S(2)}) collective-permute-start(f32[608,128]{1,0:T(8,128)S(1)} %constant_dynamic-update-slice_fusion.2.far_ref), channel_id=1, source_target_pairs={{0,1},{1,0},{2,3},{3,2},{4,5},{5,4},{6,7},{7,6},{8,9},{9,8},{10,11... | collective-permute-start | bytes 933896 | tf_op jit(solution)/shard_map/ppermute | solution.py:344
  35.9 1.9 %collective-permute-start.17 = (bf16[2,192,384]{2,1,0:T(8,128)(2,1)S(1)}, bf16[2,192,384]{2,1,0:T(8,128)(2,1)S(1)}, u32[]{:S(2)}, u32[]{:S(2)}) collective-permute-start(bf16[2,192,384]{2,1,0:T(8,128)(2,1)S(1)} %collective-permute-done.12.chip_ref), channel_id=1, source_target_pairs={{0,1},{1,0},{2,3},{3,2},{4,5},{5,4},{6,7},{7,6},{8,9},{9,8},{10,11... | collective-permute-start | bytes 884744 | tf_op jit(solution)/shard_map/ppermute | solution.py:344
  36.0 9.7 %collective-permute-start.8 = (f32[608,128]{1,0:T(8,128)S(1)}, f32[608,128]{1,0:T(8,128)S(1)}, u32[]{:S(2)}, u32[]{:S(2)}) collective-permute-start(f32[608,128]{1,0:T(8,128)S(1)} %constant_dynamic-update-slice_fusion.2.far_ref), channel_id=1, source_target_pairs={{0,2},{1,3},{2,0},{3,1},{4,6},{5,7},{6,4},{7,5},{8,10},{9,11},{10,... | collective-permute-start | bytes 933896 | tf_op jit(solution)/shard_map/ppermute | solution.py:344
  45.7 1.6 %collective-permute-start.18 = (f32[608,128]{1,0:T(8,128)S(1)}, f32[608,128]{1,0:T(8,128)S(1)}, u32[]{:S(2)}, u32[]{:S(2)}) collective-permute-start(f32[608,128]{1,0:T(8,128)S(1)} %collective-permute-done.8.chip_ref), channel_id=1, source_target_pairs={{0,1},{1,0},{2,3},{3,2},{4,5},{5,4},{6,7},{7,6},{8,9},{9,8},{10,11... | collective-permute-start | bytes 933896 | tf_op jit(solution)/shard_map/ppermute | solution.py:344
  47.3 15.1 %copy-start.4 = (f32[1,192,768]{2,1,0:T(8,128)S(1)}, f32[1,192,768]{2,1,0:T(8,128)}, u32[]{:S(2)}) copy-start(f32[1,192,768]{2,1,0:T(8,128)} %left_ref.1) | copy-start | bytes 1769476
  47.3 15.1 %copy-start.5 = (f32[1,192,768]{2,1,0:T(8,128)S(1)}, f32[1,192,768]{2,1,0:T(8,128)}, u32[]{:S(2)}) copy-start(f32[1,192,768]{2,1,0:T(8,128)} %right_ref.1) | copy-start | bytes 1769476
  49.8 8.9 %collective-permute-start.19 = (f32[144,128]{1,0:T(8,128)S(1)}, f32[144,128]{1,0:T(8,128)S(1)}, u32[]{:S(2)}, u32[]{:S(2)}) collective-permute-start(f32[144,128]{1,0:T(8,128)S(1)} %get-tuple-element.85), channel_id=1, source_target_pairs={{0,16},{4,20},{8,24},{12,28},{16,0},{20,4},{24,8},{28,12},{1,17},{... | collective-permute-start | bytes 221192 | tf_op jit(solution)/shard_map/ppermute | solution.py:344
  52.9 7.1 %collective-permute-start.20 = (f32[144,128]{1,0:T(8,128)S(1)}, f32[144,128]{1,0:T(8,128)S(1)}, u32[]{:S(2)}, u32[]{:S(2)}) collective-permute-start(f32[144,128]{1,0:T(8,128)S(1)} %get-tuple-element.86), channel_id=1, source_target_pairs={{0,4},{4,0},{8,12},{12,8},{16,20},{20,16},{24,28},{28,24},{1,5},{5... | collective-permute-start | bytes 221192 | tf_op jit(solution)/shard_map/ppermute | solution.py:344
  53.5 13.0 %collective-permute-start.21 = (f32[144,128]{1,0:T(8,128)S(1)}, f32[144,128]{1,0:T(8,128)S(1)}, u32[]{:S(2)}, u32[]{:S(2)}) collective-permute-start(f32[144,128]{1,0:T(8,128)S(1)} %get-tuple-element.87), channel_id=1, source_target_pairs={{0,20},{4,16},{8,28},{12,24},{16,4},{20,0},{24,12},{28,8},{1,21},{... | collective-permute-start | bytes 221192 | tf_op jit(solution)/shard_map/ppermute | solution.py:344
  54.5 12.0 %collective-permute-start.22 = (f32[144,128]{1,0:T(8,128)S(1)}, f32[144,128]{1,0:T(8,128)S(1)}, u32[]{:S(2)}, u32[]{:S(2)}) collective-permute-start(f32[144,128]{1,0:T(8,128)S(1)} %get-tuple-element.88), channel_id=1, source_target_pairs={{0,8},{4,12},{8,0},{12,4},{16,24},{20,28},{24,16},{28,20},{1,9},{5... | collective-permute-start | bytes 221192 | tf_op jit(solution)/shard_map/ppermute | solution.py:344
  55.9 10.5 %collective-permute-start.23 = (f32[144,128]{1,0:T(8,128)S(1)}, f32[144,128]{1,0:T(8,128)S(1)}, u32[]{:S(2)}, u32[]{:S(2)}) collective-permute-start(f32[144,128]{1,0:T(8,128)S(1)} %get-tuple-element.89), channel_id=1, source_target_pairs={{0,24},{4,28},{8,16},{12,20},{16,8},{20,12},{24,0},{28,4},{1,25},{... | collective-permute-start | bytes 221192 | tf_op jit(solution)/shard_map/ppermute | solution.py:344
  58.8 7.7 %collective-permute-start.24 = (f32[144,128]{1,0:T(8,128)S(1)}, f32[144,128]{1,0:T(8,128)S(1)}, u32[]{:S(2)}, u32[]{:S(2)}) collective-permute-start(f32[144,128]{1,0:T(8,128)S(1)} %get-tuple-element.90), channel_id=1, source_target_pairs={{0,12},{4,8},{8,4},{12,0},{16,28},{20,24},{24,20},{28,16},{1,13},{... | collective-permute-start | bytes 221192 | tf_op jit(solution)/shard_map/ppermute | solution.py:344
  60.0 7.1 %collective-permute-start.25 = (f32[144,128]{1,0:T(8,128)S(1)}, f32[144,128]{1,0:T(8,128)S(1)}, u32[]{:S(2)}, u32[]{:S(2)}) collective-permute-start(f32[144,128]{1,0:T(8,128)S(1)} %get-tuple-element.91), channel_id=1, source_target_pairs={{0,28},{4,24},{8,20},{12,16},{16,12},{20,8},{24,4},{28,0},{1,29},{... | collective-permute-start | bytes 221192 | tf_op jit(solution)/shard_map/ppermute | solution.py:344

commit v5 on v4

--- a/solution.py
+++ b/solution.py
@@ -379,11 +379,12 @@
     near = jnp.concatenate([*arrived[: shards // 2], vec_pair], axis=0)
     far = jnp.concatenate(arrived[shards // 2 :], axis=0)
     near, roots_chip = lax.optimization_barrier((near, roots_chip))
+    near_across = swap(near, "tensor", 2)
+    near_across, roots_both = lax.optimization_barrier((near_across, swap(roots_chip, "tensor", 1)))
     full = shape((size, size), BF16)
     left_full, right_full = kernel_call(
-        roots_kernel, (full, full), (roots, roots_core, roots_chip, swap(roots_chip, "tensor", 1)), mib=24
-    )
-    near_across = swap(near, "tensor", 2)
+        roots_kernel, (full, full), (roots, roots_core, roots_chip, roots_both), mib=24
+    )
     near = near, swap(near, "tensor", 1), near_across, swap(near_across, "tensor", 1)
     far_across = swap(far, "tensor", 2)
     half = size // 2

time: 68.9 us -> 68.5 us (level)
  waiting for transfers between devices: 19.6 us -> 18.8 us
    ppermute x26, waiting for transfers between devices: 19.6 us -> 18.8 us  [swap(): lax.ppermute(a, axis, [(i, i ^ mask) for i in range(lax.axis_size(axis))])]
  transfers between devices with their start and end apart: 26 -> 26, of which waited for: 7 -> 7; matrix products, arithmetic and copies ran while one was open for 0% -> 0% of each run, Pallas kernels for 12% -> 13%
where the time goes in v5:
time: 68.5 us; the launch traced here: 68.3 us
  starting transfers between devices  32.9 us (48%)
  waiting for transfers between devices  18.8 us (27%)
  Pallas kernels  14 us (20%)
  local copies, waits for them, and re-layouts  1.76 us (3%)
  between operations  0.84 us (1%)
    ppermute x26, starting transfers between devices, swap(): lax.ppermute(a, axis, [(i, i ^ mask) for i in range(lax.axis_size(axis))])  32.9 us
    ppermute x26, waiting for transfers between devices, swap(): lax.ppermute(a, axis, [(i, i ^ mask) for i in range(lax.axis_size(axis))])  18.8 us
    pallas_call x8, Pallas kernels, kernel_call(): pl.pallas_call(body, out_shape=outs, in_specs=[pl.BlockSpec(memory_space=...  14 us
    unnamed x28, local copies, waits for them, and re-layouts  1.7 us
  transfers between devices with their start and end apart: 26, of which 7 were waited for; matrix products, arithmetic and copies ran while one was open for 0% of the time, Pallas kernels for 13%

profile of v5, /device:TPU:0, one launch (start us, length us, event | category | flops | bytes accessed | tf_op | source)
XLA Modules:
  0.0 68.3 jit_solution(16173030869065476083)
XLA Ops:
  0.6 1.3 %copy-done = f32[1,4,96,768]{3,2,1,0:T(8,128)S(1)} copy-done((f32[1,4,96,768]{3,2,1,0:T(8,128)S(1)}, f32[1,4,96,768]{3,2,1,0:T(8,128)}, u32[]{:S(2)}) %copy-start) | copy-done | bytes 1179672
  1.9 0.2 shard_map.154
  2.1 0.5 collective-permute-start.1
  2.6 0.3 copy-done.8
  2.9 0.1 copy-done.9
  3.0 0.0 copy-start.1
  3.0 0.0 copy-start.2
  3.0 0.5 collective-permute-start.3
  3.5 0.2 shard_map.153
  3.7 0.1 collective-permute-start
  3.9 3.0 %collective-permute-start.2 = (f32[576,128]{1,0:T(8,128)S(1)}, f32[576,128]{1,0:T(8,128)S(1)}, u32[]{:S(2)}, u32[]{:S(2)}) collective-permute-start(f32[576,128]{1,0:T(8,128)S(1)} %add.7), channel_id=1, source_target_pairs={{0,2},{1,3},{2,0},{3,1},{4,6},{5,7},{6,4},{7,5},{8,10},{9,11},{10,... | collective-permute-start | bytes 884744 | tf_op jit(solution)/shard_map/ppermute | solution.py:344
  6.9 7.2 %collective-permute-done.2.r_ref = f32[576,128]{1,0:T(8,128)S(1)} collective-permute-done((f32[576,128]{1,0:T(8,128)S(1)}, f32[576,128]{1,0:T(8,128)S(1)}, u32[]{:S(2)}, u32[]{:S(2)}) %collective-permute-start.2) | collective-permute-done | bytes 294944 | tf_op jit(solution)/shard_map/ppermute | solution.py:344
  14.1 0.0 collective-permute-done.3.core_ref
  14.1 0.0 collective-permute-done.rn_ref
  14.1 1.0 %shard_map.155 = (f32[152,128]{1,0:T(8,128)S(1)}, f32[152,128]{1,0:T(8,128)S(1)}, f32[152,128]{1,0:T(8,128)S(1)}, f32[152,128]{1,0:T(8,128)S(1)}, f32[152,128]{1...) custom-call(s32[4]{0:T(128)S(1)} %copy-done.2, ...), custom_call_target="tpu_custom_call" | custom-call | bytes 2109456 | tf_op jit(solution)/shard_map/pallas_call | solution.py:332
  15.1 1.8 %collective-permute-start.9 = (f32[152,128]{1,0:T(8,128)S(1)}, f32[152,128]{1,0:T(8,128)S(1)}, u32[]{:S(2)}, u32[]{:S(2)}) collective-permute-start(f32[152,128]{1,0:T(8,128)S(1)} %get-tuple-element.68), channel_id=1, source_target_pairs={{0,4},{4,0},{8,12},{12,8},{16,20},{20,16},{24,28},{28,24},{1,5},{5... | collective-permute-start | bytes 233480 | tf_op jit(solution)/shard_map/ppermute | solution.py:344
  16.9 1.6 %collective-permute-start.10 = (f32[152,128]{1,0:T(8,128)S(1)}, f32[152,128]{1,0:T(8,128)S(1)}, u32[]{:S(2)}, u32[]{:S(2)}) collective-permute-start(f32[152,128]{1,0:T(8,128)S(1)} %get-tuple-element.69), channel_id=1, source_target_pairs={{0,8},{4,12},{8,0},{12,4},{16,24},{20,28},{24,16},{28,20},{1,9},{5... | collective-permute-start | bytes 233480 | tf_op jit(solution)/shard_map/ppermute | solution.py:344
  18.5 0.1 collective-permute-start.11
  18.6 1.7 %collective-permute-start.12 = (bf16[2,192,384]{2,1,0:T(8,128)(2,1)S(1)}, bf16[2,192,384]{2,1,0:T(8,128)(2,1)S(1)}, u32[]{:S(2)}, u32[]{:S(2)}) collective-permute-start(bf16[2,192,384]{2,1,0:T(8,128)(2,1)S(1)} %constant_dynamic-slice_fusion), channel_id=1, source_target_pairs={{0,2},{1,3},{2,0},{3,1},{4,6},{5,7},{6,4},{7,5},{8,10},{9,11},{10,... | collective-permute-start | bytes 884744 | tf_op jit(solution)/shard_map/ppermute | solution.py:344
  20.4 2.6 %collective-permute-start.4 = (f32[152,128]{1,0:T(8,128)S(1)}, f32[152,128]{1,0:T(8,128)S(1)}, u32[]{:S(2)}, u32[]{:S(2)}) collective-permute-start(f32[152,128]{1,0:T(8,128)S(1)} %get-tuple-element.63), channel_id=1, source_target_pairs={{0,16},{4,20},{8,24},{12,28},{16,0},{20,4},{24,8},{28,12},{1,17},{... | collective-permute-start | bytes 233480 | tf_op jit(solution)/shard_map/ppermute | solution.py:344
  23.0 0.0 collective-permute-done.9
  23.0 1.4 %collective-permute-start.5 = (f32[152,128]{1,0:T(8,128)S(1)}, f32[152,128]{1,0:T(8,128)S(1)}, u32[]{:S(2)}, u32[]{:S(2)}) collective-permute-start(f32[152,128]{1,0:T(8,128)S(1)} %get-tuple-element.64), channel_id=1, source_target_pairs={{0,20},{4,16},{8,28},{12,24},{16,4},{20,0},{24,12},{28,8},{1,21},{... | collective-permute-start | bytes 233480 | tf_op jit(solution)/shard_map/ppermute | solution.py:344
  24.3 3.7 %collective-permute-start.6 = (f32[152,128]{1,0:T(8,128)S(1)}, f32[152,128]{1,0:T(8,128)S(1)}, u32[]{:S(2)}, u32[]{:S(2)}) collective-permute-start(f32[152,128]{1,0:T(8,128)S(1)} %get-tuple-element.65), channel_id=1, source_target_pairs={{0,24},{4,28},{8,16},{12,20},{16,8},{20,12},{24,0},{28,4},{1,25},{... | collective-permute-start | bytes 233480 | tf_op jit(solution)/shard_map/ppermute | solution.py:344
  28.0 0.2 collective-permute-start.7
  28.3 0.0 copy-start.6
  28.3 0.0 copy-start.7
  28.3 1.1 %collective-permute-start.14 = (f32[616,128]{1,0:T(8,128)S(1)}, f32[616,128]{1,0:T(8,128)S(1)}, u32[]{:S(2)}, u32[]{:S(2)}) collective-permute-start(f32[616,128]{1,0:T(8,128)S(1)} %constant_dynamic-update-slice_fusion.6.mine_ref), channel_id=1, source_target_pairs={{0,2},{1,3},{2,0},{3,1},{4,6},{5,7},{6,4},{7,5},{8,10},{9,11},{10,... | collective-permute-start | bytes 946184 | tf_op jit(solution)/shard_map/ppermute | solution.py:344
  29.4 4.7 %collective-permute-done.5 = f32[152,128]{1,0:T(8,128)S(1)} collective-permute-done((f32[152,128]{1,0:T(8,128)S(1)}, f32[152,128]{1,0:T(8,128)S(1)}, u32[]{:S(2)}, u32[]{:S(2)}) %collective-permute-start.5) | collective-permute-done | bytes 77856 | tf_op jit(solution)/shard_map/ppermute | solution.py:344
  34.1 0.1 collective-permute-start.13
  34.2 1.1 %collective-permute-done.14.chip_ref = f32[616,128]{1,0:T(8,128)S(1)} collective-permute-done((f32[616,128]{1,0:T(8,128)S(1)}, f32[616,128]{1,0:T(8,128)S(1)}, u32[]{:S(2)}, u32[]{:S(2)}) %collective-permute-start.14) | collective-permute-done | bytes 315424 | tf_op jit(solution)/shard_map/ppermute | solution.py:344
  35.3 0.6 collective-permute-start.17
  35.9 1.0 %collective-permute-start.8 = (f32[608,128]{1,0:T(8,128)S(1)}, f32[608,128]{1,0:T(8,128)S(1)}, u32[]{:S(2)}, u32[]{:S(2)}) collective-permute-start(f32[608,128]{1,0:T(8,128)S(1)} %constant_dynamic-update-slice_fusion.2.far_ref), channel_id=1, source_target_pairs={{0,2},{1,3},{2,0},{3,1},{4,6},{5,7},{6,4},{7,5},{8,10},{9,11},{10,... | collective-permute-start | bytes 933896 | tf_op jit(solution)/shard_map/ppermute | solution.py:344
  36.9 0.3 shard_map.156
  37.2 0.2 collective-permute-done.17.far_peer_ref
  37.4 4.0 %shard_map.157 = (bf16[384,768]{1,0:T(8,128)(2,1)S(1)}, bf16[384,768]{1,0:T(8,128)(2,1)S(1)}, bf16[384,384]{1,0:T(8,128)(2,1)S(1)}, bf16[384,384]{1,0:T(8,128)(2...) custom-call(f32[616,128]{1,0:T(8,128)S(1)} %constant_dynamic-update-, ...), custom_call_target="tpu_custom_call" | custom-call | flops 2264924160 | bytes 10153472 | tf_op jit(solution)/shard_map/pallas_call | solution.py:332
  41.4 3.8 %collective-permute-done.8.chip_ref = f32[608,128]{1,0:T(8,128)S(1)} collective-permute-done((f32[608,128]{1,0:T(8,128)S(1)}, f32[608,128]{1,0:T(8,128)S(1)}, u32[]{:S(2)}, u32[]{:S(2)}) %collective-permute-start.8) | collective-permute-done | bytes 311328 | tf_op jit(solution)/shard_map/ppermute | solution.py:344
  45.2 1.6 %collective-permute-done.18.both_ref = f32[608,128]{1,0:T(8,128)S(1)} collective-permute-done((f32[608,128]{1,0:T(8,128)S(1)}, f32[608,128]{1,0:T(8,128)S(1)}, u32[]{:S(2)}, u32[]{:S(2)}) %collective-permute-start.18) | collective-permute-done | bytes 311328 | tf_op jit(solution)/shard_map/ppermute | solution.py:344
  46.8 2.5 %shard_map.158 = (bf16[384,384]{1,0:T(8,128)(2,1)S(1)}, bf16[384,384]{1,0:T(8,128)(2,1)S(1)}, f32[144,128]{1,0:T(8,128)S(1)}, f32[144,128]{1,0:T(8,128)S(1)}, f3...) custom-call(f32[608,128]{1,0:T(8,128)S(1)} %collective-permute-done., ...), custom_call_target="tpu_custom_call" | custom-call | flops 1358954496 | bytes 7704576 | tf_op jit(solution)/shard_map/pallas_call | solution.py:332
  49.4 3.4 %collective-permute-start.19 = (f32[144,128]{1,0:T(8,128)S(1)}, f32[144,128]{1,0:T(8,128)S(1)}, u32[]{:S(2)}, u32[]{:S(2)}) collective-permute-start(f32[144,128]{1,0:T(8,128)S(1)} %get-tuple-element.89), channel_id=1, source_target_pairs={{0,16},{4,20},{8,24},{12,28},{16,0},{20,4},{24,8},{28,12},{1,17},{... | collective-permute-start | bytes 221192 | tf_op jit(solution)/shard_map/ppermute | solution.py:344
  52.8 0.6 collective-permute-start.20
  53.4 1.0 %collective-permute-start.21 = (f32[144,128]{1,0:T(8,128)S(1)}, f32[144,128]{1,0:T(8,128)S(1)}, u32[]{:S(2)}, u32[]{:S(2)}) collective-permute-start(f32[144,128]{1,0:T(8,128)S(1)} %get-tuple-element.91), channel_id=1, source_target_pairs={{0,20},{4,16},{8,28},{12,24},{16,4},{20,0},{24,12},{28,8},{1,21},{... | collective-permute-start | bytes 221192 | tf_op jit(solution)/shard_map/ppermute | solution.py:344
  54.4 1.5 %collective-permute-start.22 = (f32[144,128]{1,0:T(8,128)S(1)}, f32[144,128]{1,0:T(8,128)S(1)}, u32[]{:S(2)}, u32[]{:S(2)}) collective-permute-start(f32[144,128]{1,0:T(8,128)S(1)} %get-tuple-element.92), channel_id=1, source_target_pairs={{0,8},{4,12},{8,0},{12,4},{16,24},{20,28},{24,16},{28,20},{1,9},{5... | collective-permute-start | bytes 221192 | tf_op jit(solution)/shard_map/ppermute | solution.py:344
  55.9 2.8 %collective-permute-start.23 = (f32[144,128]{1,0:T(8,128)S(1)}, f32[144,128]{1,0:T(8,128)S(1)}, u32[]{:S(2)}, u32[]{:S(2)}) collective-permute-start(f32[144,128]{1,0:T(8,128)S(1)} %get-tuple-element.93), channel_id=1, source_target_pairs={{0,24},{4,28},{8,16},{12,20},{16,8},{20,12},{24,0},{28,4},{1,25},{... | collective-permute-start | bytes 221192 | tf_op jit(solution)/shard_map/ppermute | solution.py:344
  58.7 0.9 %collective-permute-start.24 = (f32[144,128]{1,0:T(8,128)S(1)}, f32[144,128]{1,0:T(8,128)S(1)}, u32[]{:S(2)}, u32[]{:S(2)}) collective-permute-start(f32[144,128]{1,0:T(8,128)S(1)} %get-tuple-element.94), channel_id=1, source_target_pairs={{0,12},{4,8},{8,4},{12,0},{16,28},{20,24},{24,20},{28,16},{1,13},{... | collective-permute-start | bytes 221192 | tf_op jit(solution)/shard_map/ppermute | solution.py:344
  59.5 2.8 %collective-permute-start.25 = (f32[144,128]{1,0:T(8,128)S(1)}, f32[144,128]{1,0:T(8,128)S(1)}, u32[]{:S(2)}, u32[]{:S(2)}) collective-permute-start(f32[144,128]{1,0:T(8,128)S(1)} %get-tuple-element.95), channel_id=1, source_target_pairs={{0,28},{4,24},{8,20},{12,16},{16,12},{20,8},{24,4},{28,0},{1,29},{... | collective-permute-start | bytes 221192 | tf_op jit(solution)/shard_map/ppermute | solution.py:344
  62.3 4.1 %shard_map.160 = (f32[1,192,768]{2,1,0:T(8,128)}, f32[1,192,768]{2,1,0:T(8,128)}) custom-call(s32[4]{0:T(128)S(1)} %copy-done.2, bf16[384,768]{1,0:T(8,128)(2,1)S(1)} %get-tuple-element.98.ah_ref, bf16[384,768]{1,0:T(8,128)(2,1)S(1)} %get-tuple-element.99.al_ref, bf16[384,384]{1,0:T(8,128)(2,1)S(1)} %get-tuple-element.100.bh_ref, ...), custom_call_target="tpu_custom_call" | custom-call | flops 1358954496 | bytes 4718608 | tf_op jit(solution)/shard_map/pallas_call | solution.py:332
  66.5 0.1 collective-permute-done.25.refs_6_
  66.6 1.7 %shard_map.159 = f32[4,96,192]{2,1,0:T(8,128)} custom-call(s32[4]{0:T(128)S(1)} %copy-done.2, f32[144,128]{1,0:T(8,128)S(1)} %collective-permute-done.19.refs_0_, f32[144,128]{1,0:T(8,128)S(1)} %collective-permute-done.20.refs_1_, f32[144,128]{1,0:T(8,128)S(1)} %collective-permute-done.21.refs_2_, f32[144,128]{1,0:T(8,128)S(1)} %collective-permute-done.22.refs_3_, ...), custom_call_target="tpu_custom_call" | custom-call | bytes 884752 | tf_op jit(solution)/shard_map/pallas_call | solution.py:332
  (45 shorter events, 0.2 us)
Async XLA Ops:
  0.6 1.3 %copy-start = (f32[1,4,96,768]{3,2,1,0:T(8,128)S(1)}, f32[1,4,96,768]{3,2,1,0:T(8,128)}, u32[]{:S(2)}) copy-start(f32[1,4,96,768]{3,2,1,0:T(8,128)} %g_ref.3) | copy-start | bytes 3538948
  1.9 1.0 %copy-start.8 = (bf16[1,192,768]{2,1,0:T(8,128)(2,1)S(1)}, bf16[1,192,768]{2,1,0:T(8,128)(2,1)}, u32[]{:S(2)}) copy-start(bf16[1,192,768]{2,1,0:T(8,128)(2,1)} %param.14) | copy-start | bytes 884740
  1.9 1.0 %copy-start.9 = (bf16[1,192,768]{2,1,0:T(8,128)(2,1)S(1)}, bf16[1,192,768]{2,1,0:T(8,128)(2,1)}, u32[]{:S(2)}) copy-start(bf16[1,192,768]{2,1,0:T(8,128)(2,1)} %param.15) | copy-start | bytes 884740
  1.9 1.6 %copy-start.3 = (f32[1,4,96]{2,1,0:T(4,128)S(1)}, f32[1,4,96]{2,1,0:T(4,128)}, u32[]{:S(2)}) copy-start(f32[1,4,96]{2,1,0:T(4,128)} %refs_0_.1) | copy-start | bytes 4612
  2.1 1.7 %collective-permute-start.1 = (f32[576,128]{1,0:T(8,128)S(1)}, f32[576,128]{1,0:T(8,128)S(1)}, u32[]{:S(2)}, u32[]{:S(2)}) collective-permute-start(f32[576,128]{1,0:T(8,128)S(1)} %get-tuple-element.61), channel_id=1, source_target_pairs={{0,1},{1,0},{2,3},{3,2},{4,5},{5,4},{6,7},{7,6},{8,9},{9,8},{10,11... | collective-permute-start | bytes 884744 | tf_op jit(solution)/shard_map/ppermute | solution.py:344
  3.0 11.1 %copy-start.1 = (f32[4,96,192]{2,1,0:T(8,128)S(1)}, f32[4,96,192]{2,1,0:T(8,128)}, u32[]{:S(2)}) copy-start(f32[4,96,192]{2,1,0:T(8,128)} %v_ref.2) | copy-start | bytes 884740
  3.0 11.1 %copy-start.2 = (s32[4]{0:T(128)S(1)}, s32[4]{0:T(128)}, u32[]{:S(2)}) copy-start(s32[4]{0:T(128)} %owner_ref.5) | copy-start | bytes 52
  3.0 11.1 %collective-permute-start.3 = (bf16[2,192,768]{2,1,0:T(8,128)(2,1)S(1)}, bf16[2,192,768]{2,1,0:T(8,128)(2,1)S(1)}, u32[]{:S(2)}, u32[]{:S(2)}) collective-permute-start(bf16[2,192,768]{2,1,0:T(8,128)(2,1)S(1)} %constant_dynamic-update-slice_fusion.own_ref), channel_id=1, source_target_pairs={{0,1},{1,0},{2,3},{3,2},{4,5},{5,4},{6,7},{7,6},{8,9},{9,8},{10,11... | collective-permute-start | bytes 1769480 | tf_op jit(solution)/shard_map/ppermute | solution.py:344
  3.7 10.4 %collective-permute-start = (f32[584,128]{1,0:T(8,128)S(1)}, f32[584,128]{1,0:T(8,128)S(1)}, u32[]{:S(2)}, u32[]{:S(2)}) collective-permute-start(f32[584,128]{1,0:T(8,128)S(1)} %get-tuple-element.59), channel_id=1, source_target_pairs={{0,1},{1,0},{2,3},{3,2},{4,5},{5,4},{6,7},{7,6},{8,9},{9,8},{10,11... | collective-permute-start | bytes 897032 | tf_op jit(solution)/shard_map/ppermute | solution.py:344
  3.9 10.2 %collective-permute-start.2 = (f32[576,128]{1,0:T(8,128)S(1)}, f32[576,128]{1,0:T(8,128)S(1)}, u32[]{:S(2)}, u32[]{:S(2)}) collective-permute-start(f32[576,128]{1,0:T(8,128)S(1)} %add.7), channel_id=1, source_target_pairs={{0,2},{1,3},{2,0},{3,1},{4,6},{5,7},{6,4},{7,5},{8,10},{9,11},{10,... | collective-permute-start | bytes 884744 | tf_op jit(solution)/shard_map/ppermute | solution.py:344
  15.1 7.9 %collective-permute-start.9 = (f32[152,128]{1,0:T(8,128)S(1)}, f32[152,128]{1,0:T(8,128)S(1)}, u32[]{:S(2)}, u32[]{:S(2)}) collective-permute-start(f32[152,128]{1,0:T(8,128)S(1)} %get-tuple-element.68), channel_id=1, source_target_pairs={{0,4},{4,0},{8,12},{12,8},{16,20},{20,16},{24,28},{28,24},{1,5},{5... | collective-permute-start | bytes 233480 | tf_op jit(solution)/shard_map/ppermute | solution.py:344
  16.9 7.4 %collective-permute-start.10 = (f32[152,128]{1,0:T(8,128)S(1)}, f32[152,128]{1,0:T(8,128)S(1)}, u32[]{:S(2)}, u32[]{:S(2)}) collective-permute-start(f32[152,128]{1,0:T(8,128)S(1)} %get-tuple-element.69), channel_id=1, source_target_pairs={{0,8},{4,12},{8,0},{12,4},{16,24},{20,28},{24,16},{28,20},{1,9},{5... | collective-permute-start | bytes 233480 | tf_op jit(solution)/shard_map/ppermute | solution.py:344
  18.5 9.5 %collective-permute-start.11 = (f32[152,128]{1,0:T(8,128)S(1)}, f32[152,128]{1,0:T(8,128)S(1)}, u32[]{:S(2)}, u32[]{:S(2)}) collective-permute-start(f32[152,128]{1,0:T(8,128)S(1)} %get-tuple-element.70), channel_id=1, source_target_pairs={{0,12},{4,8},{8,4},{12,0},{16,28},{20,24},{24,20},{28,16},{1,13},{... | collective-permute-start | bytes 233480 | tf_op jit(solution)/shard_map/ppermute | solution.py:344
  18.6 9.7 %collective-permute-start.12 = (bf16[2,192,384]{2,1,0:T(8,128)(2,1)S(1)}, bf16[2,192,384]{2,1,0:T(8,128)(2,1)S(1)}, u32[]{:S(2)}, u32[]{:S(2)}) collective-permute-start(bf16[2,192,384]{2,1,0:T(8,128)(2,1)S(1)} %constant_dynamic-slice_fusion), channel_id=1, source_target_pairs={{0,2},{1,3},{2,0},{3,1},{4,6},{5,7},{6,4},{7,5},{8,10},{9,11},{10,... | collective-permute-start | bytes 884744 | tf_op jit(solution)/shard_map/ppermute | solution.py:344
  20.4 9.0 %collective-permute-start.4 = (f32[152,128]{1,0:T(8,128)S(1)}, f32[152,128]{1,0:T(8,128)S(1)}, u32[]{:S(2)}, u32[]{:S(2)}) collective-permute-start(f32[152,128]{1,0:T(8,128)S(1)} %get-tuple-element.63), channel_id=1, source_target_pairs={{0,16},{4,20},{8,24},{12,28},{16,0},{20,4},{24,8},{28,12},{1,17},{... | collective-permute-start | bytes 233480 | tf_op jit(solution)/shard_map/ppermute | solution.py:344
  23.0 11.1 %collective-permute-start.5 = (f32[152,128]{1,0:T(8,128)S(1)}, f32[152,128]{1,0:T(8,128)S(1)}, u32[]{:S(2)}, u32[]{:S(2)}) collective-permute-start(f32[152,128]{1,0:T(8,128)S(1)} %get-tuple-element.64), channel_id=1, source_target_pairs={{0,20},{4,16},{8,28},{12,24},{16,4},{20,0},{24,12},{28,8},{1,21},{... | collective-permute-start | bytes 233480 | tf_op jit(solution)/shard_map/ppermute | solution.py:344
  24.3 9.7 %collective-permute-start.6 = (f32[152,128]{1,0:T(8,128)S(1)}, f32[152,128]{1,0:T(8,128)S(1)}, u32[]{:S(2)}, u32[]{:S(2)}) collective-permute-start(f32[152,128]{1,0:T(8,128)S(1)} %get-tuple-element.65), channel_id=1, source_target_pairs={{0,24},{4,28},{8,16},{12,20},{16,8},{20,12},{24,0},{28,4},{1,25},{... | collective-permute-start | bytes 233480 | tf_op jit(solution)/shard_map/ppermute | solution.py:344
  28.0 7.3 %collective-permute-start.7 = (f32[152,128]{1,0:T(8,128)S(1)}, f32[152,128]{1,0:T(8,128)S(1)}, u32[]{:S(2)}, u32[]{:S(2)}) collective-permute-start(f32[152,128]{1,0:T(8,128)S(1)} %get-tuple-element.66), channel_id=1, source_target_pairs={{0,28},{4,24},{8,20},{12,16},{16,12},{20,8},{24,4},{28,0},{1,29},{... | collective-permute-start | bytes 233480 | tf_op jit(solution)/shard_map/ppermute | solution.py:344
  28.3 9.1 %copy-start.6 = (f32[4,96]{1,0:T(4,128)S(1)}, f32[4,96]{1,0:T(4,128)}, u32[]{:S(2)}) copy-start(f32[4,96]{1,0:T(4,128)} %m_ref.1) | copy-start | bytes 4612
  28.3 9.1 %copy-start.7 = (f32[4,96]{1,0:T(4,128)S(1)}, f32[4,96]{1,0:T(4,128)}, u32[]{:S(2)}) copy-start(f32[4,96]{1,0:T(4,128)} %v_ref.3) | copy-start | bytes 4612
  28.3 7.0 %collective-permute-start.14 = (f32[616,128]{1,0:T(8,128)S(1)}, f32[616,128]{1,0:T(8,128)S(1)}, u32[]{:S(2)}, u32[]{:S(2)}) collective-permute-start(f32[616,128]{1,0:T(8,128)S(1)} %constant_dynamic-update-slice_fusion.6.mine_ref), channel_id=1, source_target_pairs={{0,2},{1,3},{2,0},{3,1},{4,6},{5,7},{6,4},{7,5},{8,10},{9,11},{10,... | collective-permute-start | bytes 946184 | tf_op jit(solution)/shard_map/ppermute | solution.py:344
  29.4 4.8 %collective-permute-start.15 = (bf16[2,192,384]{2,1,0:T(8,128)(2,1)S(1)}, bf16[2,192,384]{2,1,0:T(8,128)(2,1)S(1)}, u32[]{:S(2)}, u32[]{:S(2)}) collective-permute-start(bf16[2,192,384]{2,1,0:T(8,128)(2,1)S(1)} %collective-permute-done.12.chip_ref), channel_id=1, source_target_pairs={{0,1},{1,0},{2,3},{3,2},{4,5},{5,4},{6,7},{7,6},{8,9},{9,8},{10,11... | collective-permute-start | bytes 884744 | tf_op jit(solution)/shard_map/ppermute | solution.py:344
  34.1 3.3 %collective-permute-start.13 = (f32[616,128]{1,0:T(8,128)S(1)}, f32[616,128]{1,0:T(8,128)S(1)}, u32[]{:S(2)}, u32[]{:S(2)}) collective-permute-start(f32[616,128]{1,0:T(8,128)S(1)} %constant_dynamic-update-slice_fusion.6.mine_ref), channel_id=1, source_target_pairs={{0,1},{1,0},{2,3},{3,2},{4,5},{5,4},{6,7},{7,6},{8,9},{9,8},{10,11... | collective-permute-start | bytes 946184 | tf_op jit(solution)/shard_map/ppermute | solution.py:344
  35.3 2.1 %collective-permute-start.16 = (f32[616,128]{1,0:T(8,128)S(1)}, f32[616,128]{1,0:T(8,128)S(1)}, u32[]{:S(2)}, u32[]{:S(2)}) collective-permute-start(f32[616,128]{1,0:T(8,128)S(1)} %collective-permute-done.14.chip_ref), channel_id=1, source_target_pairs={{0,1},{1,0},{2,3},{3,2},{4,5},{5,4},{6,7},{7,6},{8,9},{9,8},{10,11... | collective-permute-start | bytes 946184 | tf_op jit(solution)/shard_map/ppermute | solution.py:344
  35.3 2.0 %collective-permute-start.17 = (f32[608,128]{1,0:T(8,128)S(1)}, f32[608,128]{1,0:T(8,128)S(1)}, u32[]{:S(2)}, u32[]{:S(2)}) collective-permute-start(f32[608,128]{1,0:T(8,128)S(1)} %constant_dynamic-update-slice_fusion.2.far_ref), channel_id=1, source_target_pairs={{0,1},{1,0},{2,3},{3,2},{4,5},{5,4},{6,7},{7,6},{8,9},{9,8},{10,11... | collective-permute-start | bytes 933896 | tf_op jit(solution)/shard_map/ppermute | solution.py:344
  35.9 9.3 %collective-permute-start.8 = (f32[608,128]{1,0:T(8,128)S(1)}, f32[608,128]{1,0:T(8,128)S(1)}, u32[]{:S(2)}, u32[]{:S(2)}) collective-permute-start(f32[608,128]{1,0:T(8,128)S(1)} %constant_dynamic-update-slice_fusion.2.far_ref), channel_id=1, source_target_pairs={{0,2},{1,3},{2,0},{3,1},{4,6},{5,7},{6,4},{7,5},{8,10},{9,11},{10,... | collective-permute-start | bytes 933896 | tf_op jit(solution)/shard_map/ppermute | solution.py:344
  45.2 1.6 %collective-permute-start.18 = (f32[608,128]{1,0:T(8,128)S(1)}, f32[608,128]{1,0:T(8,128)S(1)}, u32[]{:S(2)}, u32[]{:S(2)}) collective-permute-start(f32[608,128]{1,0:T(8,128)S(1)} %collective-permute-done.8.chip_ref), channel_id=1, source_target_pairs={{0,1},{1,0},{2,3},{3,2},{4,5},{5,4},{6,7},{7,6},{8,9},{9,8},{10,11... | collective-permute-start | bytes 933896 | tf_op jit(solution)/shard_map/ppermute | solution.py:344
  46.8 15.5 %copy-start.4 = (f32[1,192,768]{2,1,0:T(8,128)S(1)}, f32[1,192,768]{2,1,0:T(8,128)}, u32[]{:S(2)}) copy-start(f32[1,192,768]{2,1,0:T(8,128)} %left_ref.1) | copy-start | bytes 1769476
  46.8 15.5 %copy-start.5 = (f32[1,192,768]{2,1,0:T(8,128)S(1)}, f32[1,192,768]{2,1,0:T(8,128)}, u32[]{:S(2)}) copy-start(f32[1,192,768]{2,1,0:T(8,128)} %right_ref.1) | copy-start | bytes 1769476
  49.4 9.3 %collective-permute-start.19 = (f32[144,128]{1,0:T(8,128)S(1)}, f32[144,128]{1,0:T(8,128)S(1)}, u32[]{:S(2)}, u32[]{:S(2)}) collective-permute-start(f32[144,128]{1,0:T(8,128)S(1)} %get-tuple-element.89), channel_id=1, source_target_pairs={{0,16},{4,20},{8,24},{12,28},{16,0},{20,4},{24,8},{28,12},{1,17},{... | collective-permute-start | bytes 221192 | tf_op jit(solution)/shard_map/ppermute | solution.py:344
  52.8 6.7 %collective-permute-start.20 = (f32[144,128]{1,0:T(8,128)S(1)}, f32[144,128]{1,0:T(8,128)S(1)}, u32[]{:S(2)}, u32[]{:S(2)}) collective-permute-start(f32[144,128]{1,0:T(8,128)S(1)} %get-tuple-element.90), channel_id=1, source_target_pairs={{0,4},{4,0},{8,12},{12,8},{16,20},{20,16},{24,28},{28,24},{1,5},{5... | collective-permute-start | bytes 221192 | tf_op jit(solution)/shard_map/ppermute | solution.py:344
  53.4 13.0 %collective-permute-start.21 = (f32[144,128]{1,0:T(8,128)S(1)}, f32[144,128]{1,0:T(8,128)S(1)}, u32[]{:S(2)}, u32[]{:S(2)}) collective-permute-start(f32[144,128]{1,0:T(8,128)S(1)} %get-tuple-element.91), channel_id=1, source_target_pairs={{0,20},{4,16},{8,28},{12,24},{16,4},{20,0},{24,12},{28,8},{1,21},{... | collective-permute-start | bytes 221192 | tf_op jit(solution)/shard_map/ppermute | solution.py:344
  54.4 12.1 %collective-permute-start.22 = (f32[144,128]{1,0:T(8,128)S(1)}, f32[144,128]{1,0:T(8,128)S(1)}, u32[]{:S(2)}, u32[]{:S(2)}) collective-permute-start(f32[144,128]{1,0:T(8,128)S(1)} %get-tuple-element.92), channel_id=1, source_target_pairs={{0,8},{4,12},{8,0},{12,4},{16,24},{20,28},{24,16},{28,20},{1,9},{5... | collective-permute-start | bytes 221192 | tf_op jit(solution)/shard_map/ppermute | solution.py:344
  55.9 10.6 %collective-permute-start.23 = (f32[144,128]{1,0:T(8,128)S(1)}, f32[144,128]{1,0:T(8,128)S(1)}, u32[]{:S(2)}, u32[]{:S(2)}) collective-permute-start(f32[144,128]{1,0:T(8,128)S(1)} %get-tuple-element.93), channel_id=1, source_target_pairs={{0,24},{4,28},{8,16},{12,20},{16,8},{20,12},{24,0},{28,4},{1,25},{... | collective-permute-start | bytes 221192 | tf_op jit(solution)/shard_map/ppermute | solution.py:344
  58.7 7.8 %collective-permute-start.24 = (f32[144,128]{1,0:T(8,128)S(1)}, f32[144,128]{1,0:T(8,128)S(1)}, u32[]{:S(2)}, u32[]{:S(2)}) collective-permute-start(f32[144,128]{1,0:T(8,128)S(1)} %get-tuple-element.94), channel_id=1, source_target_pairs={{0,12},{4,8},{8,4},{12,0},{16,28},{20,24},{24,20},{28,16},{1,13},{... | collective-permute-start | bytes 221192 | tf_op jit(solution)/shard_map/ppermute | solution.py:344
  59.5 7.1 %collective-permute-start.25 = (f32[144,128]{1,0:T(8,128)S(1)}, f32[144,128]{1,0:T(8,128)S(1)}, u32[]{:S(2)}, u32[]{:S(2)}) collective-permute-start(f32[144,128]{1,0:T(8,128)S(1)} %get-tuple-element.95), channel_id=1, source_target_pairs={{0,28},{4,24},{8,20},{12,16},{16,12},{20,8},{24,4},{28,0},{1,29},{... | collective-permute-start | bytes 221192 | tf_op jit(solution)/shard_map/ppermute | solution.py:344

commit v6 on v5

--- a/solution.py
+++ b/solution.py
@@ -17,7 +17,7 @@
 BIAS_TWO = 1.0 - BETA_TWO**STEP_COUNT
 HIGH = lax.Precision.HIGHEST
 LANES = 128
-BACK = (4, 1, 5, 2, 6, 3, 7, 0)
+BACK = (4, 1, 5, 3, 6, 2, 7, 0)
 EXTRA = 8
 F32 = jnp.float32
 BF16 = jnp.bfloat16

time: 68.5 us -> 68.6 us (level)
  no operation moved by 1% of the time
where the time goes in v6:
time: 68.6 us; the launch traced here: 68.4 us
  starting transfers between devices  32.9 us (48%)
  waiting for transfers between devices  18.9 us (28%)
  Pallas kernels  14 us (20%)
  local copies, waits for them, and re-layouts  1.76 us (3%)
  between operations  0.84 us (1%)
    ppermute x26, starting transfers between devices, swap(): lax.ppermute(a, axis, [(i, i ^ mask) for i in range(lax.axis_size(axis))])  32.9 us
    ppermute x26, waiting for transfers between devices, swap(): lax.ppermute(a, axis, [(i, i ^ mask) for i in range(lax.axis_size(axis))])  18.9 us
    pallas_call x8, Pallas kernels, kernel_call(): pl.pallas_call(body, out_shape=outs, in_specs=[pl.BlockSpec(memory_space=...  14 us
    unnamed x28, local copies, waits for them, and re-layouts  1.7 us
  transfers between devices with their start and end apart: 26, of which 7 were waited for; matrix products, arithmetic and copies ran while one was open for 0% of the time, Pallas kernels for 13%

profile of v6, /device:TPU:0, one launch (start us, length us, event | category | flops | bytes accessed | tf_op | source)
XLA Modules:
  0.0 68.4 jit_solution(3373682544298358310)
XLA Ops:
  0.6 1.3 %copy-done = f32[1,4,96,768]{3,2,1,0:T(8,128)S(1)} copy-done((f32[1,4,96,768]{3,2,1,0:T(8,128)S(1)}, f32[1,4,96,768]{3,2,1,0:T(8,128)}, u32[]{:S(2)}) %copy-start) | copy-done | bytes 1179672
  1.9 0.2 shard_map.154
  2.1 0.5 collective-permute-start.1
  2.6 0.3 copy-done.8
  2.9 0.1 copy-done.9
  3.0 0.0 copy-start.1
  3.0 0.0 copy-start.2
  3.0 0.5 collective-permute-start.3
  3.5 0.2 shard_map.153
  3.7 0.1 collective-permute-start
  3.8 0.0 collective-permute-done.1
  3.9 3.0 %collective-permute-start.2 = (f32[576,128]{1,0:T(8,128)S(1)}, f32[576,128]{1,0:T(8,128)S(1)}, u32[]{:S(2)}, u32[]{:S(2)}) collective-permute-start(f32[576,128]{1,0:T(8,128)S(1)} %add.7), channel_id=1, source_target_pairs={{0,2},{1,3},{2,0},{3,1},{4,6},{5,7},{6,4},{7,5},{8,10},{9,11},{10,... | collective-permute-start | bytes 884744 | tf_op jit(solution)/shard_map/ppermute | solution.py:344
  6.9 7.2 %collective-permute-done.2.r_ref = f32[576,128]{1,0:T(8,128)S(1)} collective-permute-done((f32[576,128]{1,0:T(8,128)S(1)}, f32[576,128]{1,0:T(8,128)S(1)}, u32[]{:S(2)}, u32[]{:S(2)}) %collective-permute-start.2) | collective-permute-done | bytes 294944 | tf_op jit(solution)/shard_map/ppermute | solution.py:344
  14.1 1.0 %shard_map.155 = (f32[152,128]{1,0:T(8,128)S(1)}, f32[152,128]{1,0:T(8,128)S(1)}, f32[152,128]{1,0:T(8,128)S(1)}, f32[152,128]{1,0:T(8,128)S(1)}, f32[152,128]{1...) custom-call(s32[4]{0:T(128)S(1)} %copy-done.2, ...), custom_call_target="tpu_custom_call" | custom-call | bytes 2109456 | tf_op jit(solution)/shard_map/pallas_call | solution.py:332
  15.1 1.8 %collective-permute-start.9 = (f32[152,128]{1,0:T(8,128)S(1)}, f32[152,128]{1,0:T(8,128)S(1)}, u32[]{:S(2)}, u32[]{:S(2)}) collective-permute-start(f32[152,128]{1,0:T(8,128)S(1)} %get-tuple-element.68), channel_id=1, source_target_pairs={{0,4},{4,0},{8,12},{12,8},{16,20},{20,16},{24,28},{28,24},{1,5},{5... | collective-permute-start | bytes 233480 | tf_op jit(solution)/shard_map/ppermute | solution.py:344
  16.9 1.6 %collective-permute-start.10 = (f32[152,128]{1,0:T(8,128)S(1)}, f32[152,128]{1,0:T(8,128)S(1)}, u32[]{:S(2)}, u32[]{:S(2)}) collective-permute-start(f32[152,128]{1,0:T(8,128)S(1)} %get-tuple-element.69), channel_id=1, source_target_pairs={{0,8},{4,12},{8,0},{12,4},{16,24},{20,28},{24,16},{28,20},{1,9},{5... | collective-permute-start | bytes 233480 | tf_op jit(solution)/shard_map/ppermute | solution.py:344
  18.5 0.1 collective-permute-start.11
  18.6 1.7 %collective-permute-start.12 = (bf16[2,192,384]{2,1,0:T(8,128)(2,1)S(1)}, bf16[2,192,384]{2,1,0:T(8,128)(2,1)S(1)}, u32[]{:S(2)}, u32[]{:S(2)}) collective-permute-start(bf16[2,192,384]{2,1,0:T(8,128)(2,1)S(1)} %constant_dynamic-slice_fusion), channel_id=1, source_target_pairs={{0,2},{1,3},{2,0},{3,1},{4,6},{5,7},{6,4},{7,5},{8,10},{9,11},{10,... | collective-permute-start | bytes 884744 | tf_op jit(solution)/shard_map/ppermute | solution.py:344
  20.4 2.6 %collective-permute-start.4 = (f32[152,128]{1,0:T(8,128)S(1)}, f32[152,128]{1,0:T(8,128)S(1)}, u32[]{:S(2)}, u32[]{:S(2)}) collective-permute-start(f32[152,128]{1,0:T(8,128)S(1)} %get-tuple-element.63), channel_id=1, source_target_pairs={{0,16},{4,20},{8,24},{12,28},{16,0},{20,4},{24,8},{28,12},{1,17},{... | collective-permute-start | bytes 233480 | tf_op jit(solution)/shard_map/ppermute | solution.py:344
  23.0 1.4 %collective-permute-start.5 = (f32[152,128]{1,0:T(8,128)S(1)}, f32[152,128]{1,0:T(8,128)S(1)}, u32[]{:S(2)}, u32[]{:S(2)}) collective-permute-start(f32[152,128]{1,0:T(8,128)S(1)} %get-tuple-element.64), channel_id=1, source_target_pairs={{0,20},{4,16},{8,28},{12,24},{16,4},{20,0},{24,12},{28,8},{1,21},{... | collective-permute-start | bytes 233480 | tf_op jit(solution)/shard_map/ppermute | solution.py:344
  24.3 3.7 %collective-permute-start.6 = (f32[152,128]{1,0:T(8,128)S(1)}, f32[152,128]{1,0:T(8,128)S(1)}, u32[]{:S(2)}, u32[]{:S(2)}) collective-permute-start(f32[152,128]{1,0:T(8,128)S(1)} %get-tuple-element.65), channel_id=1, source_target_pairs={{0,24},{4,28},{8,16},{12,20},{16,8},{20,12},{24,0},{28,4},{1,25},{... | collective-permute-start | bytes 233480 | tf_op jit(solution)/shard_map/ppermute | solution.py:344
  28.0 0.2 collective-permute-start.7
  28.3 0.0 copy-start.6
  28.3 0.0 copy-start.7
  28.3 0.0 collective-permute-done.12.chip_ref
  28.3 1.1 %collective-permute-start.14 = (f32[616,128]{1,0:T(8,128)S(1)}, f32[616,128]{1,0:T(8,128)S(1)}, u32[]{:S(2)}, u32[]{:S(2)}) collective-permute-start(f32[616,128]{1,0:T(8,128)S(1)} %constant_dynamic-update-slice_fusion.6.mine_ref), channel_id=1, source_target_pairs={{0,2},{1,3},{2,0},{3,1},{4,6},{5,7},{6,4},{7,5},{8,10},{9,11},{10,... | collective-permute-start | bytes 946184 | tf_op jit(solution)/shard_map/ppermute | solution.py:344
  29.4 4.7 %collective-permute-done.5 = f32[152,128]{1,0:T(8,128)S(1)} collective-permute-done((f32[152,128]{1,0:T(8,128)S(1)}, f32[152,128]{1,0:T(8,128)S(1)}, u32[]{:S(2)}, u32[]{:S(2)}) %collective-permute-start.5) | collective-permute-done | bytes 77856 | tf_op jit(solution)/shard_map/ppermute | solution.py:344
  34.1 0.1 collective-permute-start.13
  34.2 0.0 collective-permute-done.15.both_ref
  34.2 1.1 %collective-permute-done.14.chip_ref = f32[616,128]{1,0:T(8,128)S(1)} collective-permute-done((f32[616,128]{1,0:T(8,128)S(1)}, f32[616,128]{1,0:T(8,128)S(1)}, u32[]{:S(2)}, u32[]{:S(2)}) %collective-permute-start.14) | collective-permute-done | bytes 315424 | tf_op jit(solution)/shard_map/ppermute | solution.py:344
  35.3 0.6 collective-permute-start.17
  35.9 1.0 %collective-permute-start.8 = (f32[608,128]{1,0:T(8,128)S(1)}, f32[608,128]{1,0:T(8,128)S(1)}, u32[]{:S(2)}, u32[]{:S(2)}) collective-permute-start(f32[608,128]{1,0:T(8,128)S(1)} %constant_dynamic-update-slice_fusion.2.far_ref), channel_id=1, source_target_pairs={{0,2},{1,3},{2,0},{3,1},{4,6},{5,7},{6,4},{7,5},{8,10},{9,11},{10,... | collective-permute-start | bytes 933896 | tf_op jit(solution)/shard_map/ppermute | solution.py:344
  36.9 0.3 shard_map.156
  37.2 0.2 collective-permute-done.17.far_peer_ref
  37.4 4.0 %shard_map.157 = (bf16[384,768]{1,0:T(8,128)(2,1)S(1)}, bf16[384,768]{1,0:T(8,128)(2,1)S(1)}, bf16[384,384]{1,0:T(8,128)(2,1)S(1)}, bf16[384,384]{1,0:T(8,128)(2...) custom-call(f32[616,128]{1,0:T(8,128)S(1)} %constant_dynamic-update-, ...), custom_call_target="tpu_custom_call" | custom-call | flops 2264924160 | bytes 10153472 | tf_op jit(solution)/shard_map/pallas_call | solution.py:332
  41.4 3.8 %collective-permute-done.8.chip_ref = f32[608,128]{1,0:T(8,128)S(1)} collective-permute-done((f32[608,128]{1,0:T(8,128)S(1)}, f32[608,128]{1,0:T(8,128)S(1)}, u32[]{:S(2)}, u32[]{:S(2)}) %collective-permute-start.8) | collective-permute-done | bytes 311328 | tf_op jit(solution)/shard_map/ppermute | solution.py:344
  45.2 1.6 %collective-permute-done.18.both_ref = f32[608,128]{1,0:T(8,128)S(1)} collective-permute-done((f32[608,128]{1,0:T(8,128)S(1)}, f32[608,128]{1,0:T(8,128)S(1)}, u32[]{:S(2)}, u32[]{:S(2)}) %collective-permute-start.18) | collective-permute-done | bytes 311328 | tf_op jit(solution)/shard_map/ppermute | solution.py:344
  46.8 2.5 %shard_map.158 = (bf16[384,384]{1,0:T(8,128)(2,1)S(1)}, bf16[384,384]{1,0:T(8,128)(2,1)S(1)}, f32[144,128]{1,0:T(8,128)S(1)}, f32[144,128]{1,0:T(8,128)S(1)}, f3...) custom-call(f32[608,128]{1,0:T(8,128)S(1)} %collective-permute-done., ...), custom_call_target="tpu_custom_call" | custom-call | flops 1358954496 | bytes 7704576 | tf_op jit(solution)/shard_map/pallas_call | solution.py:332
  49.4 3.4 %collective-permute-start.19 = (f32[144,128]{1,0:T(8,128)S(1)}, f32[144,128]{1,0:T(8,128)S(1)}, u32[]{:S(2)}, u32[]{:S(2)}) collective-permute-start(f32[144,128]{1,0:T(8,128)S(1)} %get-tuple-element.89), channel_id=1, source_target_pairs={{0,16},{4,20},{8,24},{12,28},{16,0},{20,4},{24,8},{28,12},{1,17},{... | collective-permute-start | bytes 221192 | tf_op jit(solution)/shard_map/ppermute | solution.py:344
  52.8 0.6 collective-permute-start.20
  53.4 0.9 %collective-permute-start.21 = (f32[144,128]{1,0:T(8,128)S(1)}, f32[144,128]{1,0:T(8,128)S(1)}, u32[]{:S(2)}, u32[]{:S(2)}) collective-permute-start(f32[144,128]{1,0:T(8,128)S(1)} %get-tuple-element.91), channel_id=1, source_target_pairs={{0,20},{4,16},{8,28},{12,24},{16,4},{20,0},{24,12},{28,8},{1,21},{... | collective-permute-start | bytes 221192 | tf_op jit(solution)/shard_map/ppermute | solution.py:344
  54.4 2.0 %collective-permute-start.22 = (f32[144,128]{1,0:T(8,128)S(1)}, f32[144,128]{1,0:T(8,128)S(1)}, u32[]{:S(2)}, u32[]{:S(2)}) collective-permute-start(f32[144,128]{1,0:T(8,128)S(1)} %get-tuple-element.92), channel_id=1, source_target_pairs={{0,12},{4,8},{8,4},{12,0},{16,28},{20,24},{24,20},{28,16},{1,13},{... | collective-permute-start | bytes 221192 | tf_op jit(solution)/shard_map/ppermute | solution.py:344
  56.4 2.4 %collective-permute-start.23 = (f32[144,128]{1,0:T(8,128)S(1)}, f32[144,128]{1,0:T(8,128)S(1)}, u32[]{:S(2)}, u32[]{:S(2)}) collective-permute-start(f32[144,128]{1,0:T(8,128)S(1)} %get-tuple-element.93), channel_id=1, source_target_pairs={{0,24},{4,28},{8,16},{12,20},{16,8},{20,12},{24,0},{28,4},{1,25},{... | collective-permute-start | bytes 221192 | tf_op jit(solution)/shard_map/ppermute | solution.py:344
  58.7 0.8 %collective-permute-start.24 = (f32[144,128]{1,0:T(8,128)S(1)}, f32[144,128]{1,0:T(8,128)S(1)}, u32[]{:S(2)}, u32[]{:S(2)}) collective-permute-start(f32[144,128]{1,0:T(8,128)S(1)} %get-tuple-element.94), channel_id=1, source_target_pairs={{0,8},{4,12},{8,0},{12,4},{16,24},{20,28},{24,16},{28,20},{1,9},{5... | collective-permute-start | bytes 221192 | tf_op jit(solution)/shard_map/ppermute | solution.py:344
  59.5 2.8 %collective-permute-start.25 = (f32[144,128]{1,0:T(8,128)S(1)}, f32[144,128]{1,0:T(8,128)S(1)}, u32[]{:S(2)}, u32[]{:S(2)}) collective-permute-start(f32[144,128]{1,0:T(8,128)S(1)} %get-tuple-element.95), channel_id=1, source_target_pairs={{0,28},{4,24},{8,20},{12,16},{16,12},{20,8},{24,4},{28,0},{1,29},{... | collective-permute-start | bytes 221192 | tf_op jit(solution)/shard_map/ppermute | solution.py:344
  62.3 4.1 %shard_map.160 = (f32[1,192,768]{2,1,0:T(8,128)}, f32[1,192,768]{2,1,0:T(8,128)}) custom-call(s32[4]{0:T(128)S(1)} %copy-done.2, bf16[384,768]{1,0:T(8,128)(2,1)S(1)} %get-tuple-element.98.ah_ref, bf16[384,768]{1,0:T(8,128)(2,1)S(1)} %get-tuple-element.99.al_ref, bf16[384,384]{1,0:T(8,128)(2,1)S(1)} %get-tuple-element.100.bh_ref, ...), custom_call_target="tpu_custom_call" | custom-call | flops 1358954496 | bytes 4718608 | tf_op jit(solution)/shard_map/pallas_call | solution.py:332
  66.5 0.2 collective-permute-done.25.refs_6_
  66.7 1.7 %shard_map.159 = f32[4,96,192]{2,1,0:T(8,128)} custom-call(s32[4]{0:T(128)S(1)} %copy-done.2, f32[144,128]{1,0:T(8,128)S(1)} %collective-permute-done.19.refs_0_, f32[144,128]{1,0:T(8,128)S(1)} %collective-permute-done.20.refs_1_, f32[144,128]{1,0:T(8,128)S(1)} %collective-permute-done.21.refs_2_, f32[144,128]{1,0:T(8,128)S(1)} %collective-permute-done.22.refs_3_, ...), custom_call_target="tpu_custom_call" | custom-call | bytes 884752 | tf_op jit(solution)/shard_map/pallas_call | solution.py:332
  (45 shorter events, 0.2 us)
Async XLA Ops:
  0.6 1.3 %copy-start = (f32[1,4,96,768]{3,2,1,0:T(8,128)S(1)}, f32[1,4,96,768]{3,2,1,0:T(8,128)}, u32[]{:S(2)}) copy-start(f32[1,4,96,768]{3,2,1,0:T(8,128)} %g_ref.3) | copy-start | bytes 3538948
  1.9 1.0 %copy-start.8 = (bf16[1,192,768]{2,1,0:T(8,128)(2,1)S(1)}, bf16[1,192,768]{2,1,0:T(8,128)(2,1)}, u32[]{:S(2)}) copy-start(bf16[1,192,768]{2,1,0:T(8,128)(2,1)} %param.14) | copy-start | bytes 884740
  1.9 1.0 %copy-start.9 = (bf16[1,192,768]{2,1,0:T(8,128)(2,1)S(1)}, bf16[1,192,768]{2,1,0:T(8,128)(2,1)}, u32[]{:S(2)}) copy-start(bf16[1,192,768]{2,1,0:T(8,128)(2,1)} %param.15) | copy-start | bytes 884740
  1.9 1.6 %copy-start.3 = (f32[1,4,96]{2,1,0:T(4,128)S(1)}, f32[1,4,96]{2,1,0:T(4,128)}, u32[]{:S(2)}) copy-start(f32[1,4,96]{2,1,0:T(4,128)} %refs_0_.1) | copy-start | bytes 4612
  2.1 1.7 %collective-permute-start.1 = (f32[576,128]{1,0:T(8,128)S(1)}, f32[576,128]{1,0:T(8,128)S(1)}, u32[]{:S(2)}, u32[]{:S(2)}) collective-permute-start(f32[576,128]{1,0:T(8,128)S(1)} %get-tuple-element.61), channel_id=1, source_target_pairs={{0,1},{1,0},{2,3},{3,2},{4,5},{5,4},{6,7},{7,6},{8,9},{9,8},{10,11... | collective-permute-start | bytes 884744 | tf_op jit(solution)/shard_map/ppermute | solution.py:344
  3.0 11.1 %copy-start.1 = (f32[4,96,192]{2,1,0:T(8,128)S(1)}, f32[4,96,192]{2,1,0:T(8,128)}, u32[]{:S(2)}) copy-start(f32[4,96,192]{2,1,0:T(8,128)} %v_ref.2) | copy-start | bytes 884740
  3.0 11.1 %copy-start.2 = (s32[4]{0:T(128)S(1)}, s32[4]{0:T(128)}, u32[]{:S(2)}) copy-start(s32[4]{0:T(128)} %owner_ref.5) | copy-start | bytes 52
  3.0 11.1 %collective-permute-start.3 = (bf16[2,192,768]{2,1,0:T(8,128)(2,1)S(1)}, bf16[2,192,768]{2,1,0:T(8,128)(2,1)S(1)}, u32[]{:S(2)}, u32[]{:S(2)}) collective-permute-start(bf16[2,192,768]{2,1,0:T(8,128)(2,1)S(1)} %constant_dynamic-update-slice_fusion.own_ref), channel_id=1, source_target_pairs={{0,1},{1,0},{2,3},{3,2},{4,5},{5,4},{6,7},{7,6},{8,9},{9,8},{10,11... | collective-permute-start | bytes 1769480 | tf_op jit(solution)/shard_map/ppermute | solution.py:344
  3.7 10.4 %collective-permute-start = (f32[584,128]{1,0:T(8,128)S(1)}, f32[584,128]{1,0:T(8,128)S(1)}, u32[]{:S(2)}, u32[]{:S(2)}) collective-permute-start(f32[584,128]{1,0:T(8,128)S(1)} %get-tuple-element.59), channel_id=1, source_target_pairs={{0,1},{1,0},{2,3},{3,2},{4,5},{5,4},{6,7},{7,6},{8,9},{9,8},{10,11... | collective-permute-start | bytes 897032 | tf_op jit(solution)/shard_map/ppermute | solution.py:344
  3.9 10.2 %collective-permute-start.2 = (f32[576,128]{1,0:T(8,128)S(1)}, f32[576,128]{1,0:T(8,128)S(1)}, u32[]{:S(2)}, u32[]{:S(2)}) collective-permute-start(f32[576,128]{1,0:T(8,128)S(1)} %add.7), channel_id=1, source_target_pairs={{0,2},{1,3},{2,0},{3,1},{4,6},{5,7},{6,4},{7,5},{8,10},{9,11},{10,... | collective-permute-start | bytes 884744 | tf_op jit(solution)/shard_map/ppermute | solution.py:344
  15.1 7.9 %collective-permute-start.9 = (f32[152,128]{1,0:T(8,128)S(1)}, f32[152,128]{1,0:T(8,128)S(1)}, u32[]{:S(2)}, u32[]{:S(2)}) collective-permute-start(f32[152,128]{1,0:T(8,128)S(1)} %get-tuple-element.68), channel_id=1, source_target_pairs={{0,4},{4,0},{8,12},{12,8},{16,20},{20,16},{24,28},{28,24},{1,5},{5... | collective-permute-start | bytes 233480 | tf_op jit(solution)/shard_map/ppermute | solution.py:344
  16.9 7.4 %collective-permute-start.10 = (f32[152,128]{1,0:T(8,128)S(1)}, f32[152,128]{1,0:T(8,128)S(1)}, u32[]{:S(2)}, u32[]{:S(2)}) collective-permute-start(f32[152,128]{1,0:T(8,128)S(1)} %get-tuple-element.69), channel_id=1, source_target_pairs={{0,8},{4,12},{8,0},{12,4},{16,24},{20,28},{24,16},{28,20},{1,9},{5... | collective-permute-start | bytes 233480 | tf_op jit(solution)/shard_map/ppermute | solution.py:344
  18.5 9.5 %collective-permute-start.11 = (f32[152,128]{1,0:T(8,128)S(1)}, f32[152,128]{1,0:T(8,128)S(1)}, u32[]{:S(2)}, u32[]{:S(2)}) collective-permute-start(f32[152,128]{1,0:T(8,128)S(1)} %get-tuple-element.70), channel_id=1, source_target_pairs={{0,12},{4,8},{8,4},{12,0},{16,28},{20,24},{24,20},{28,16},{1,13},{... | collective-permute-start | bytes 233480 | tf_op jit(solution)/shard_map/ppermute | solution.py:344
  18.6 9.7 %collective-permute-start.12 = (bf16[2,192,384]{2,1,0:T(8,128)(2,1)S(1)}, bf16[2,192,384]{2,1,0:T(8,128)(2,1)S(1)}, u32[]{:S(2)}, u32[]{:S(2)}) collective-permute-start(bf16[2,192,384]{2,1,0:T(8,128)(2,1)S(1)} %constant_dynamic-slice_fusion), channel_id=1, source_target_pairs={{0,2},{1,3},{2,0},{3,1},{4,6},{5,7},{6,4},{7,5},{8,10},{9,11},{10,... | collective-permute-start | bytes 884744 | tf_op jit(solution)/shard_map/ppermute | solution.py:344
  20.4 9.0 %collective-permute-start.4 = (f32[152,128]{1,0:T(8,128)S(1)}, f32[152,128]{1,0:T(8,128)S(1)}, u32[]{:S(2)}, u32[]{:S(2)}) collective-permute-start(f32[152,128]{1,0:T(8,128)S(1)} %get-tuple-element.63), channel_id=1, source_target_pairs={{0,16},{4,20},{8,24},{12,28},{16,0},{20,4},{24,8},{28,12},{1,17},{... | collective-permute-start | bytes 233480 | tf_op jit(solution)/shard_map/ppermute | solution.py:344
  23.0 11.1 %collective-permute-start.5 = (f32[152,128]{1,0:T(8,128)S(1)}, f32[152,128]{1,0:T(8,128)S(1)}, u32[]{:S(2)}, u32[]{:S(2)}) collective-permute-start(f32[152,128]{1,0:T(8,128)S(1)} %get-tuple-element.64), channel_id=1, source_target_pairs={{0,20},{4,16},{8,28},{12,24},{16,4},{20,0},{24,12},{28,8},{1,21},{... | collective-permute-start | bytes 233480 | tf_op jit(solution)/shard_map/ppermute | solution.py:344
  24.3 9.7 %collective-permute-start.6 = (f32[152,128]{1,0:T(8,128)S(1)}, f32[152,128]{1,0:T(8,128)S(1)}, u32[]{:S(2)}, u32[]{:S(2)}) collective-permute-start(f32[152,128]{1,0:T(8,128)S(1)} %get-tuple-element.65), channel_id=1, source_target_pairs={{0,24},{4,28},{8,16},{12,20},{16,8},{20,12},{24,0},{28,4},{1,25},{... | collective-permute-start | bytes 233480 | tf_op jit(solution)/shard_map/ppermute | solution.py:344
  28.0 7.3 %collective-permute-start.7 = (f32[152,128]{1,0:T(8,128)S(1)}, f32[152,128]{1,0:T(8,128)S(1)}, u32[]{:S(2)}, u32[]{:S(2)}) collective-permute-start(f32[152,128]{1,0:T(8,128)S(1)} %get-tuple-element.66), channel_id=1, source_target_pairs={{0,28},{4,24},{8,20},{12,16},{16,12},{20,8},{24,4},{28,0},{1,29},{... | collective-permute-start | bytes 233480 | tf_op jit(solution)/shard_map/ppermute | solution.py:344
  28.3 9.1 %copy-start.6 = (f32[4,96]{1,0:T(4,128)S(1)}, f32[4,96]{1,0:T(4,128)}, u32[]{:S(2)}) copy-start(f32[4,96]{1,0:T(4,128)} %m_ref.1) | copy-start | bytes 4612
  28.3 9.1 %copy-start.7 = (f32[4,96]{1,0:T(4,128)S(1)}, f32[4,96]{1,0:T(4,128)}, u32[]{:S(2)}) copy-start(f32[4,96]{1,0:T(4,128)} %v_ref.3) | copy-start | bytes 4612
  28.3 7.0 %collective-permute-start.14 = (f32[616,128]{1,0:T(8,128)S(1)}, f32[616,128]{1,0:T(8,128)S(1)}, u32[]{:S(2)}, u32[]{:S(2)}) collective-permute-start(f32[616,128]{1,0:T(8,128)S(1)} %constant_dynamic-update-slice_fusion.6.mine_ref), channel_id=1, source_target_pairs={{0,2},{1,3},{2,0},{3,1},{4,6},{5,7},{6,4},{7,5},{8,10},{9,11},{10,... | collective-permute-start | bytes 946184 | tf_op jit(solution)/shard_map/ppermute | solution.py:344
  29.4 4.8 %collective-permute-start.15 = (bf16[2,192,384]{2,1,0:T(8,128)(2,1)S(1)}, bf16[2,192,384]{2,1,0:T(8,128)(2,1)S(1)}, u32[]{:S(2)}, u32[]{:S(2)}) collective-permute-start(bf16[2,192,384]{2,1,0:T(8,128)(2,1)S(1)} %collective-permute-done.12.chip_ref), channel_id=1, source_target_pairs={{0,1},{1,0},{2,3},{3,2},{4,5},{5,4},{6,7},{7,6},{8,9},{9,8},{10,11... | collective-permute-start | bytes 884744 | tf_op jit(solution)/shard_map/ppermute | solution.py:344
  34.1 3.3 %collective-permute-start.13 = (f32[616,128]{1,0:T(8,128)S(1)}, f32[616,128]{1,0:T(8,128)S(1)}, u32[]{:S(2)}, u32[]{:S(2)}) collective-permute-start(f32[616,128]{1,0:T(8,128)S(1)} %constant_dynamic-update-slice_fusion.6.mine_ref), channel_id=1, source_target_pairs={{0,1},{1,0},{2,3},{3,2},{4,5},{5,4},{6,7},{7,6},{8,9},{9,8},{10,11... | collective-permute-start | bytes 946184 | tf_op jit(solution)/shard_map/ppermute | solution.py:344
  35.3 2.1 %collective-permute-start.16 = (f32[616,128]{1,0:T(8,128)S(1)}, f32[616,128]{1,0:T(8,128)S(1)}, u32[]{:S(2)}, u32[]{:S(2)}) collective-permute-start(f32[616,128]{1,0:T(8,128)S(1)} %collective-permute-done.14.chip_ref), channel_id=1, source_target_pairs={{0,1},{1,0},{2,3},{3,2},{4,5},{5,4},{6,7},{7,6},{8,9},{9,8},{10,11... | collective-permute-start | bytes 946184 | tf_op jit(solution)/shard_map/ppermute | solution.py:344
  35.3 2.0 %collective-permute-start.17 = (f32[608,128]{1,0:T(8,128)S(1)}, f32[608,128]{1,0:T(8,128)S(1)}, u32[]{:S(2)}, u32[]{:S(2)}) collective-permute-start(f32[608,128]{1,0:T(8,128)S(1)} %constant_dynamic-update-slice_fusion.2.far_ref), channel_id=1, source_target_pairs={{0,1},{1,0},{2,3},{3,2},{4,5},{5,4},{6,7},{7,6},{8,9},{9,8},{10,11... | collective-permute-start | bytes 933896 | tf_op jit(solution)/shard_map/ppermute | solution.py:344
  35.9 9.3 %collective-permute-start.8 = (f32[608,128]{1,0:T(8,128)S(1)}, f32[608,128]{1,0:T(8,128)S(1)}, u32[]{:S(2)}, u32[]{:S(2)}) collective-permute-start(f32[608,128]{1,0:T(8,128)S(1)} %constant_dynamic-update-slice_fusion.2.far_ref), channel_id=1, source_target_pairs={{0,2},{1,3},{2,0},{3,1},{4,6},{5,7},{6,4},{7,5},{8,10},{9,11},{10,... | collective-permute-start | bytes 933896 | tf_op jit(solution)/shard_map/ppermute | solution.py:344
  45.2 1.6 %collective-permute-start.18 = (f32[608,128]{1,0:T(8,128)S(1)}, f32[608,128]{1,0:T(8,128)S(1)}, u32[]{:S(2)}, u32[]{:S(2)}) collective-permute-start(f32[608,128]{1,0:T(8,128)S(1)} %collective-permute-done.8.chip_ref), channel_id=1, source_target_pairs={{0,1},{1,0},{2,3},{3,2},{4,5},{5,4},{6,7},{7,6},{8,9},{9,8},{10,11... | collective-permute-start | bytes 933896 | tf_op jit(solution)/shard_map/ppermute | solution.py:344
  46.8 15.5 %copy-start.4 = (f32[1,192,768]{2,1,0:T(8,128)S(1)}, f32[1,192,768]{2,1,0:T(8,128)}, u32[]{:S(2)}) copy-start(f32[1,192,768]{2,1,0:T(8,128)} %left_ref.1) | copy-start | bytes 1769476
  46.8 15.5 %copy-start.5 = (f32[1,192,768]{2,1,0:T(8,128)S(1)}, f32[1,192,768]{2,1,0:T(8,128)}, u32[]{:S(2)}) copy-start(f32[1,192,768]{2,1,0:T(8,128)} %right_ref.1) | copy-start | bytes 1769476
  49.4 9.3 %collective-permute-start.19 = (f32[144,128]{1,0:T(8,128)S(1)}, f32[144,128]{1,0:T(8,128)S(1)}, u32[]{:S(2)}, u32[]{:S(2)}) collective-permute-start(f32[144,128]{1,0:T(8,128)S(1)} %get-tuple-element.89), channel_id=1, source_target_pairs={{0,16},{4,20},{8,24},{12,28},{16,0},{20,4},{24,8},{28,12},{1,17},{... | collective-permute-start | bytes 221192 | tf_op jit(solution)/shard_map/ppermute | solution.py:344
  52.8 6.7 %collective-permute-start.20 = (f32[144,128]{1,0:T(8,128)S(1)}, f32[144,128]{1,0:T(8,128)S(1)}, u32[]{:S(2)}, u32[]{:S(2)}) collective-permute-start(f32[144,128]{1,0:T(8,128)S(1)} %get-tuple-element.90), channel_id=1, source_target_pairs={{0,4},{4,0},{8,12},{12,8},{16,20},{20,16},{24,28},{28,24},{1,5},{5... | collective-permute-start | bytes 221192 | tf_op jit(solution)/shard_map/ppermute | solution.py:344
  53.4 13.0 %collective-permute-start.21 = (f32[144,128]{1,0:T(8,128)S(1)}, f32[144,128]{1,0:T(8,128)S(1)}, u32[]{:S(2)}, u32[]{:S(2)}) collective-permute-start(f32[144,128]{1,0:T(8,128)S(1)} %get-tuple-element.91), channel_id=1, source_target_pairs={{0,20},{4,16},{8,28},{12,24},{16,4},{20,0},{24,12},{28,8},{1,21},{... | collective-permute-start | bytes 221192 | tf_op jit(solution)/shard_map/ppermute | solution.py:344
  54.4 12.1 %collective-permute-start.22 = (f32[144,128]{1,0:T(8,128)S(1)}, f32[144,128]{1,0:T(8,128)S(1)}, u32[]{:S(2)}, u32[]{:S(2)}) collective-permute-start(f32[144,128]{1,0:T(8,128)S(1)} %get-tuple-element.92), channel_id=1, source_target_pairs={{0,12},{4,8},{8,4},{12,0},{16,28},{20,24},{24,20},{28,16},{1,13},{... | collective-permute-start | bytes 221192 | tf_op jit(solution)/shard_map/ppermute | solution.py:344
  56.4 10.1 %collective-permute-start.23 = (f32[144,128]{1,0:T(8,128)S(1)}, f32[144,128]{1,0:T(8,128)S(1)}, u32[]{:S(2)}, u32[]{:S(2)}) collective-permute-start(f32[144,128]{1,0:T(8,128)S(1)} %get-tuple-element.93), channel_id=1, source_target_pairs={{0,24},{4,28},{8,16},{12,20},{16,8},{20,12},{24,0},{28,4},{1,25},{... | collective-permute-start | bytes 221192 | tf_op jit(solution)/shard_map/ppermute | solution.py:344
  58.7 7.7 %collective-permute-start.24 = (f32[144,128]{1,0:T(8,128)S(1)}, f32[144,128]{1,0:T(8,128)S(1)}, u32[]{:S(2)}, u32[]{:S(2)}) collective-permute-start(f32[144,128]{1,0:T(8,128)S(1)} %get-tuple-element.94), channel_id=1, source_target_pairs={{0,8},{4,12},{8,0},{12,4},{16,24},{20,28},{24,16},{28,20},{1,9},{5... | collective-permute-start | bytes 221192 | tf_op jit(solution)/shard_map/ppermute | solution.py:344
  59.5 7.1 %collective-permute-start.25 = (f32[144,128]{1,0:T(8,128)S(1)}, f32[144,128]{1,0:T(8,128)S(1)}, u32[]{:S(2)}, u32[]{:S(2)}) collective-permute-start(f32[144,128]{1,0:T(8,128)S(1)} %get-tuple-element.95), channel_id=1, source_target_pairs={{0,28},{4,24},{8,20},{12,16},{16,12},{20,8},{24,4},{28,0},{1,29},{... | collective-permute-start | bytes 221192 | tf_op jit(solution)/shard_map/ppermute | solution.py:344
